TPU v7x, 32 devices: a whole 2x2x4 slice. The times are simulated.
32 devices in a mesh: dp: 8 (over z, y), tensor: 4 (over x, core).
Axes of the slice: x: 2, y: 2, z: 4, core: 2. Of those that a mesh axis runs over, the one named last changes fastest.
Arguments:
- inputs: bfloat16 [4096, 2048], P('dp'), may hold values from -6 to 6
- targets: int32 [4096], P('dp'), may hold values from 0 to 25599
- doc_lengths: int32 [8, 4], P('dp'), may hold values from 1 to 384, 512 in all within a row
- desirable: int32 [8, 4], P('dp'), may hold values 0 or 1
- head_weight: bfloat16 [2048, 25600], P(None, 'tensor'), may hold values from -0.21213203 to 0.21213203, as said below
- qkv_master: float32 [2048, 6144], P('dp', 'tensor'), may hold values from -0.125 to 0.125
- out_master: float32 [2048, 2048], P('tensor', 'dp'), may hold values from -0.5 to 0.5
- up_master: float32 [2048, 8192], P('dp', 'tensor'), may hold values from -0.125 to 0.125
- down_master: float32 [8192, 2048], P('tensor', 'dp'), may hold values from -0.0625 to 0.0625
- vectors: float32 [6, 2048], replicated, may hold values from -0.525 to 2.125, as said below
- hidden_bias: float32 [14336], P('tensor'), may hold values from -1.5 to 1.5
- qkv_mean: float32 [2048, 6144], P('dp', 'tensor'), may hold values from -2.3841858e-06 to 2.3841858e-06
- out_mean: float32 [2048, 2048], P('tensor', 'dp'), may hold values from -2.3841858e-06 to 2.3841858e-06
- up_mean: float32 [2048, 8192], P('dp', 'tensor'), may hold values from -2.3841858e-06 to 2.3841858e-06
- down_mean: float32 [8192, 2048], P('tensor', 'dp'), may hold values from -2.3841858e-06 to 2.3841858e-06
- vectors_mean: float32 [6, 2048], replicated, may hold values from -9.536743e-06 to 9.536743e-06
- hidden_mean: float32 [14336], P('tensor'), may hold values from -9.536743e-06 to 9.536743e-06
- qkv_square: float32 [2048, 6144], P('dp', 'tensor'), may hold values from 9.928856e-16 to 1.5886169e-14
- out_square: float32 [2048, 2048], P('tensor', 'dp'), may hold values from 9.928856e-16 to 1.5886169e-14
- up_square: float32 [2048, 8192], P('dp', 'tensor'), may hold values from 9.928856e-16 to 1.5886169e-14
- down_square: float32 [8192, 2048], P('tensor', 'dp'), may hold values from 9.928856e-16 to 1.5886169e-14
- vectors_square: float32 [6, 2048], replicated, may hold values from 1.5886169e-14 to 2.541787e-13
- hidden_square: float32 [14336], P('tensor'), may hold values from 1.5886169e-14 to 2.541787e-13
- qkv_frozen: bfloat16 [2048, 6144], P('dp', 'tensor'), may hold values from -0.125 to 0.125
- out_frozen: bfloat16 [2048, 2048], P('tensor', 'dp'), may hold values from -0.5 to 0.5
- up_frozen: bfloat16 [2048, 8192], P('dp', 'tensor'), may hold values from -0.125 to 0.125
- down_frozen: bfloat16 [8192, 2048], P('tensor', 'dp'), may hold values from -0.0625 to 0.0625
- vectors_frozen: float32 [6, 2048], replicated, may hold values from -0.525 to 2.125
- hidden_frozen: float32 [14336], P('tensor'), may hold values from -1.5 to 1.5
Outputs:
- block_out: bfloat16 [4096, 2048], P('dp')
- input_grad: float32 [4096, 2048], P('dp')
- grad_norm: float32 [], replicated
- qkv_mean_new: float32 [2048, 6144], P('dp', 'tensor')
- qkv_square_new: float32 [2048, 6144], P('dp', 'tensor')
- qkv_master_new: float32 [2048, 6144], P('dp', 'tensor')
- out_mean_new: float32 [2048, 2048], P('tensor', 'dp')
- out_square_new: float32 [2048, 2048], P('tensor', 'dp')
- out_master_new: float32 [2048, 2048], P('tensor', 'dp')
- up_mean_new: float32 [2048, 8192], P('dp', 'tensor')
- up_square_new: float32 [2048, 8192], P('dp', 'tensor')
- up_master_new: float32 [2048, 8192], P('dp', 'tensor')
- down_mean_new: float32 [8192, 2048], P('tensor', 'dp')
- down_square_new: float32 [8192, 2048], P('tensor', 'dp')
- down_master_new: float32 [8192, 2048], P('tensor', 'dp')
- vectors_mean_new: float32 [6, 2048], replicated
- vectors_square_new: float32 [6, 2048], replicated
- vectors_new: float32 [6, 2048], replicated
- hidden_mean_new: float32 [14336], P('tensor')
- hidden_square_new: float32 [14336], P('tensor')
- hidden_bias_new: float32 [14336], P('tensor')
Inputs may be any that keep to these rules, and one draw needn't show every extreme that they name: `doc_lengths`: each row sums to 512. `vectors`: rows 0 and 2 are gains, the other rows shifts and biases. `head_weight`: frozen head weights of order one over the root of 2048.
All inputs are finite; a program needn't handle non-finite values. No bound on the sum of `desirable` on one device may be relied on, other than what follows from the above.
Results may differ from a plain program's by a relative error of at most 0.015.
Values may be sent and summed in bfloat16 or wider, within the bound.
A program may use at most 256 MiB of HBM per device.

v0:
```python
import jax
import jax.numpy as jnp
from jax import lax
from jax.sharding import PartitionSpec as P

HD = 128
ROT = 32
SEGS = 4
STEP = 3


EPS_NORM = 1e-05
BETA_KTO = 0.1
CLIP_NORM = 0.01
LEARN_RATE = 0.02
VECTOR_RATE = 0.2
BETA_FIRST = 0.9
BETA_SECOND = 0.999
ADAM_EPS = 1e-08
WEIGHT_DECAY = 0.01
MASKED = -1e30


def combined_all(value, axis, join):
    pieces = jax.tree.map(lambda part: lax.all_gather(part, axis), value)
    head = jax.tree.map(lambda part: part[0], pieces)
    tail = jax.tree.map(lambda part: part[1:], pieces)
    total, _ = lax.scan(lambda total, section: (join(total, section), None), head, tail)
    return total


def layer_norm(values, gain_row, shift_row):
    centre = values - jnp.mean(values, axis=-1, keepdims=True)
    spread = jnp.mean(centre * centre, axis=-1, keepdims=True)
    return centre * lax.rsqrt(spread + EPS_NORM) * gain_row + shift_row


def rotate(values, positions, direction):
    half_rot = ROT // 2
    frequency = 10000.0 ** (-2.0 * jnp.arange(half_rot, dtype=jnp.float32) / ROT)
    angles = positions.astype(jnp.float32)[:, None] * frequency[None, :]
    cosine = jnp.cos(angles)[:, None, :]
    sine_part = direction * jnp.sin(angles)[:, None, :]
    first_half = values[..., :half_rot]
    second_half = values[..., half_rot:ROT]
    return jnp.concatenate(
        [
            first_half * cosine - second_half * sine_part,
            second_half * cosine + first_half * sine_part,
            values[..., ROT:],
        ],
        axis=-1,
    )


def doc_layout(lengths_row, row_count):
    doc_ends = jnp.cumsum(lengths_row)
    starts = doc_ends - lengths_row
    index_rows = jnp.arange(row_count, dtype=jnp.int32)
    member = (index_rows[:, None] >= starts[None, :]) & (index_rows[:, None] < doc_ends[None, :])
    doc_ids = jnp.arange(lengths_row.shape[0], dtype=jnp.int32)
    doc_of = jnp.sum(jnp.where(member, doc_ids[None, :], 0), axis=1)
    positions = index_rows - jnp.sum(jnp.where(member, starts[None, :], 0), axis=1)
    allowed = (doc_of[:, None] == doc_of[None, :]) & (index_rows[:, None] >= index_rows[None, :])
    return (member, positions, allowed)


def contract_rows(left_rows, right_rows):
    return lax.dot_general(
        left_rows, right_rows, (((0,), (0,)), ((), ())), preferred_element_type=jnp.float32
    )


def contract_cols(left_rows, right_rows):
    return lax.dot_general(
        left_rows, right_rows, (((1,), (1,)), ((), ())), preferred_element_type=jnp.float32
    )


def attention_mlp(normed_one, normed_two, bias_local, weight_set, positions, allowed):
    qkv_full, out_full, up_full, down_full = weight_set
    row_count = normed_one.shape[0]
    split_at = qkv_full.shape[1]
    heads_local = split_at // (3 * HD)
    one_low = normed_one.astype(jnp.bfloat16)
    two_low = normed_two.astype(jnp.bfloat16)
    mixed_proj = (
        jnp.dot(one_low, qkv_full, preferred_element_type=jnp.float32) + bias_local[:split_at]
    )
    mixed_proj = mixed_proj.reshape(row_count, heads_local, 3, HD)
    query_low = rotate(mixed_proj[:, :, 0], positions, 1.0).astype(jnp.bfloat16)
    key_low = rotate(mixed_proj[:, :, 1], positions, 1.0).astype(jnp.bfloat16)
    value_low = mixed_proj[:, :, 2].astype(jnp.bfloat16)
    scores = jnp.einsum(
        "qhd,khd->hqk", query_low, key_low, preferred_element_type=jnp.float32
    ) * HD ** (-0.5)
    scores = jnp.where(allowed[None], scores, MASKED)
    highest = jnp.max(scores, axis=2, keepdims=True)
    log_total = highest + jnp.log(jnp.sum(jnp.exp(scores - highest), axis=2, keepdims=True))
    probs_low = jnp.exp(scores - log_total).astype(jnp.bfloat16)
    attended = jnp.einsum("hqk,khd->qhd", probs_low, value_low, preferred_element_type=jnp.float32)
    attended = attended.reshape(row_count, heads_local * HD).astype(jnp.bfloat16)
    hidden = jnp.dot(two_low, up_full, preferred_element_type=jnp.float32) + bias_local[split_at:]
    active = jax.nn.gelu(hidden, approximate=False).astype(jnp.bfloat16)
    branch_part = jnp.dot(attended, out_full, preferred_element_type=jnp.float32) + jnp.dot(
        active, down_full, preferred_element_type=jnp.float32
    )
    kept_values = (
        one_low,
        two_low,
        query_low,
        key_low,
        value_low,
        log_total,
        attended,
        hidden,
        active,
    )
    return (branch_part, kept_values)


def layer_backward(branch_low, kept_values, weight_set, positions, allowed):
    qkv_full, out_full, up_full, down_full = weight_set
    one_low, two_low, query_low, key_low, value_low, log_total, attended, hidden, active = (
        kept_values
    )
    row_count = query_low.shape[0]
    heads_local = query_low.shape[1]
    active_grad = contract_cols(branch_low, down_full)
    cumulative = 0.5 * (1.0 + lax.erf(hidden * 0.7071067811865476))
    density = jnp.exp(-0.5 * hidden * hidden) * 0.3989422804014327
    hidden_low = (active_grad * (cumulative + hidden * density)).astype(jnp.bfloat16)
    attended_grad = (
        contract_cols(branch_low, out_full).reshape(row_count, heads_local, HD).astype(jnp.bfloat16)
    )
    score_scale = HD ** (-0.5)
    scores = (
        jnp.einsum("qhd,khd->hqk", query_low, key_low, preferred_element_type=jnp.float32)
        * score_scale
    )
    scores = jnp.where(allowed[None], scores, MASKED)
    probs = jnp.exp(scores - log_total)
    prob_grad = jnp.einsum(
        "qhd,khd->hqk", attended_grad, value_low, preferred_element_type=jnp.float32
    )
    value_grad = jnp.einsum(
        "hqk,qhd->khd",
        probs.astype(jnp.bfloat16),
        attended_grad,
        preferred_element_type=jnp.float32,
    )
    score_grad = (probs * (prob_grad - jnp.sum(probs * prob_grad, axis=2, keepdims=True))).astype(
        jnp.bfloat16
    )
    query_grad = (
        jnp.einsum("hqk,khd->qhd", score_grad, key_low, preferred_element_type=jnp.float32)
        * score_scale
    )
    key_grad = (
        jnp.einsum("hqk,qhd->khd", score_grad, query_low, preferred_element_type=jnp.float32)
        * score_scale
    )
    mixed_grad = jnp.stack(
        [rotate(query_grad, positions, -1.0), rotate(key_grad, positions, -1.0), value_grad], axis=2
    )
    mixed_grad = mixed_grad.reshape(row_count, heads_local * 3 * HD).astype(jnp.bfloat16)
    one_part = contract_cols(mixed_grad, qkv_full)
    two_part = contract_cols(hidden_low, up_full)
    bias_grad = jnp.concatenate(
        [
            jnp.sum(mixed_grad, axis=0, dtype=jnp.float32),
            jnp.sum(hidden_low, axis=0, dtype=jnp.float32),
        ]
    )
    return (one_part, two_part, bias_grad, mixed_grad, hidden_low)


def vocab_stats(final_low, head_weight, targets, vocab_start):
    logits = jnp.dot(final_low, head_weight, preferred_element_type=jnp.float32)
    highest = jnp.max(logits, axis=1)
    log_total = highest + jnp.log(jnp.sum(jnp.exp(logits - highest[:, None]), axis=1))
    column = vocab_start + lax.broadcasted_iota(jnp.int32, logits.shape, 1)
    chosen = column == targets[:, None]
    picked = jnp.sum(jnp.where(chosen, logits, 0.0), axis=1)
    return (logits, log_total, picked, chosen)


def combine_totals(first_set, second_set):
    return (
        jnp.logaddexp(first_set[0], second_set[0]),
        first_set[1] + second_set[1],
        jnp.logaddexp(first_set[2], second_set[2]),
        first_set[3] + second_set[3],
    )


def adam_step(master, mean_old, square_old, gradient, factor, rate, decay_rate):
    clipped = gradient * factor
    mean_new = BETA_FIRST * mean_old + (1.0 - BETA_FIRST) * clipped
    square_new = BETA_SECOND * square_old + (1.0 - BETA_SECOND) * clipped * clipped
    mean_hat = mean_new / (1.0 - BETA_FIRST**STEP)
    square_hat = square_new / (1.0 - BETA_SECOND**STEP)
    master_new = master - rate * (
        mean_hat / (jnp.sqrt(square_hat) + ADAM_EPS) + decay_rate * master
    )
    return (mean_new, square_new, master_new)


def on_device(
    inputs,
    targets,
    doc_lengths,
    desirable,
    head_weight,
    qkv_master,
    out_master,
    up_master,
    down_master,
    vectors,
    hidden_bias,
    qkv_mean,
    out_mean,
    up_mean,
    down_mean,
    vectors_mean,
    hidden_mean,
    qkv_square,
    out_square,
    up_square,
    down_square,
    vectors_square,
    hidden_square,
    qkv_frozen,
    out_frozen,
    up_frozen,
    down_frozen,
    vectors_frozen,
    hidden_frozen,
):
    dp_size = lax.axis_size("dp")
    tensor_size = lax.axis_size("tensor")
    gathered = (
        lax.all_gather(qkv_master.astype(jnp.bfloat16), "dp", axis=0, tiled=True),
        lax.all_gather(out_master.astype(jnp.bfloat16), "dp", axis=1, tiled=True),
        lax.all_gather(up_master.astype(jnp.bfloat16), "dp", axis=0, tiled=True),
        lax.all_gather(down_master.astype(jnp.bfloat16), "dp", axis=1, tiled=True),
        lax.all_gather(qkv_frozen, "dp", axis=0, tiled=True),
        lax.all_gather(out_frozen, "dp", axis=1, tiled=True),
        lax.all_gather(up_frozen, "dp", axis=0, tiled=True),
        lax.all_gather(down_frozen, "dp", axis=1, tiled=True),
    )
    policy_set = gathered[:4]
    frozen_set = gathered[4:]
    member, positions, allowed = doc_layout(doc_lengths[0], inputs.shape[0])
    inputs_f32 = inputs.astype(jnp.float32)
    normed_one, back_one = jax.vjp(layer_norm, inputs_f32, vectors[0], vectors[1])
    normed_two, back_two = jax.vjp(layer_norm, inputs_f32, vectors[2], vectors[3])
    policy_part, kept_values = attention_mlp(
        normed_one, normed_two, hidden_bias, policy_set, positions, allowed
    )
    frozen_one = layer_norm(inputs_f32, vectors_frozen[0], vectors_frozen[1])
    frozen_two = layer_norm(inputs_f32, vectors_frozen[2], vectors_frozen[3])
    frozen_part, unused = attention_mlp(
        frozen_one, frozen_two, hidden_frozen, frozen_set, positions, allowed
    )
    policy_sum, frozen_sum = lax.psum((policy_part, frozen_part), "tensor")
    policy_final = inputs_f32 + (policy_sum + vectors[4] + vectors[5])
    frozen_final = inputs_f32 + (frozen_sum + vectors_frozen[4] + vectors_frozen[5])
    vocab_start = lax.axis_index("tensor") * head_weight.shape[1]
    policy_logits, policy_total, policy_pick, chosen = vocab_stats(
        policy_final.astype(jnp.bfloat16), head_weight, targets, vocab_start
    )
    unused_logits, frozen_total, frozen_pick, unused_chosen = vocab_stats(
        frozen_final.astype(jnp.bfloat16), head_weight, targets, vocab_start
    )
    policy_total, policy_pick, frozen_total, frozen_pick = combined_all(
        (policy_total, policy_pick, frozen_total, frozen_pick), "tensor", combine_totals
    )
    doc_weights = member.astype(jnp.float32)
    policy_docs = jnp.sum(doc_weights * (policy_pick - policy_total)[:, None], axis=0)
    frozen_docs = jnp.sum(doc_weights * (frozen_pick - frozen_total)[:, None], axis=0)
    reward = policy_docs - frozen_docs
    seq_count = dp_size * SEGS
    reward_shift = lax.psum(jnp.sum(reward), "dp") / seq_count
    sigmoid_value = jax.nn.sigmoid(BETA_KTO * (reward - reward_shift))
    labels = desirable[0].astype(jnp.float32)
    doc_grad = BETA_KTO * sigmoid_value * (1.0 - sigmoid_value) * (1.0 - 2.0 * labels) / seq_count
    token_grad = jnp.sum(doc_weights * doc_grad[None, :], axis=1)
    logit_grad = (
        token_grad[:, None]
        * (chosen.astype(jnp.float32) - jnp.exp(policy_logits - policy_total[:, None]))
    ).astype(jnp.bfloat16)
    final_grad = lax.psum(contract_cols(logit_grad, head_weight), "tensor")
    branch_low = final_grad.astype(jnp.bfloat16)
    one_low = kept_values[0]
    two_low = kept_values[1]
    attended = kept_values[6]
    active = kept_values[8]
    one_part, two_part, bias_grad, mixed_grad, hidden_low = layer_backward(
        branch_low, kept_values, policy_set, positions, allowed
    )
    qkv_grad, out_grad, up_grad, down_grad = (
        lax.psum_scatter(contract_rows(one_low, mixed_grad), "dp", scatter_dimension=0, tiled=True),
        lax.psum_scatter(
            contract_rows(attended, branch_low), "dp", scatter_dimension=1, tiled=True
        ),
        lax.psum_scatter(contract_rows(two_low, hidden_low), "dp", scatter_dimension=0, tiled=True),
        lax.psum_scatter(contract_rows(active, branch_low), "dp", scatter_dimension=1, tiled=True),
    )
    one_grad, two_grad = lax.psum((one_part, two_part), "tensor")
    input_one, gain_one, shift_one = back_one(one_grad)
    input_two, gain_two, shift_two = back_two(two_grad)
    input_grad = final_grad + (input_one + input_two)
    norm_grads = jnp.stack([gain_one, shift_one, gain_two, shift_two])
    branch_bias = jnp.sum(branch_low, axis=0, dtype=jnp.float32)
    vector_grad = jnp.concatenate([norm_grads, jnp.stack([branch_bias, branch_bias])], axis=0)
    vector_grad, hidden_grad = (
        lax.psum(vector_grad.astype(jnp.bfloat16), "dp").astype(jnp.float32),
        lax.psum(bias_grad.astype(jnp.bfloat16), "dp").astype(jnp.float32),
    )
    local_square = (
        jnp.sum(qkv_grad * qkv_grad)
        + jnp.sum(out_grad * out_grad)
        + jnp.sum(up_grad * up_grad)
        + jnp.sum(down_grad * down_grad)
    )
    local_square = (
        local_square
        + jnp.sum(vector_grad * vector_grad) / (dp_size * tensor_size)
        + jnp.sum(hidden_grad * hidden_grad) / dp_size
    )
    grad_norm = jnp.sqrt(lax.psum(local_square, ("dp", "tensor")))
    factor = jnp.minimum(1.0, CLIP_NORM / (grad_norm + 1e-06))
    qkv_state = adam_step(
        qkv_master, qkv_mean, qkv_square, qkv_grad, factor, LEARN_RATE, WEIGHT_DECAY
    )
    out_state = adam_step(
        out_master, out_mean, out_square, out_grad, factor, LEARN_RATE, WEIGHT_DECAY
    )
    up_state = adam_step(up_master, up_mean, up_square, up_grad, factor, LEARN_RATE, WEIGHT_DECAY)
    down_state = adam_step(
        down_master, down_mean, down_square, down_grad, factor, LEARN_RATE, WEIGHT_DECAY
    )
    vector_state = adam_step(
        vectors, vectors_mean, vectors_square, vector_grad, factor, VECTOR_RATE, 0.0
    )
    hidden_state = adam_step(
        hidden_bias, hidden_mean, hidden_square, hidden_grad, factor, VECTOR_RATE, 0.0
    )
    return (
        policy_final.astype(jnp.bfloat16),
        input_grad,
        grad_norm,
        qkv_state[0],
        qkv_state[1],
        qkv_state[2],
        out_state[0],
        out_state[1],
        out_state[2],
        up_state[0],
        up_state[1],
        up_state[2],
        down_state[0],
        down_state[1],
        down_state[2],
        vector_state[0],
        vector_state[1],
        vector_state[2],
        hidden_state[0],
        hidden_state[1],
        hidden_state[2],
    )


def solution(mesh):
    placed = (
        P("dp", None),
        P("dp"),
        P("dp", None),
        P("dp", None),
        P(None, "tensor"),
        P("dp", "tensor"),
        P("tensor", "dp"),
        P("dp", "tensor"),
        P("tensor", "dp"),
        P(),
        P("tensor"),
        P("dp", "tensor"),
        P("tensor", "dp"),
        P("dp", "tensor"),
        P("tensor", "dp"),
        P(),
        P("tensor"),
        P("dp", "tensor"),
        P("tensor", "dp"),
        P("dp", "tensor"),
        P("tensor", "dp"),
        P(),
        P("tensor"),
        P("dp", "tensor"),
        P("tensor", "dp"),
        P("dp", "tensor"),
        P("tensor", "dp"),
        P(),
        P("tensor"),
    )
    return jax.shard_map(
        on_device,
        mesh=mesh,
        in_specs=placed,
        out_specs=(
            P("dp", None),
            P("dp", None),
            P(),
            P("dp", "tensor"),
            P("dp", "tensor"),
            P("dp", "tensor"),
            P("tensor", "dp"),
            P("tensor", "dp"),
            P("tensor", "dp"),
            P("dp", "tensor"),
            P("dp", "tensor"),
            P("dp", "tensor"),
            P("tensor", "dp"),
            P("tensor", "dp"),
            P("tensor", "dp"),
            P(),
            P(),
            P(),
            P("tensor"),
            P("tensor"),
            P("tensor"),
        ),
        check_vma=False,
    )
```

profile of v0, /device:TPU:0, one launch (start us, length us, event | category | flops | bytes accessed | tf_op | source)
XLA Modules:
  0.0 2342.0 jit_solution(1622588191557680006)
XLA Ops:
  24.3 87.8 %all-gather.25.cloned.1.call-done = bf16[2048,1536]{1,0:T(8,128)(2,1)} async-done(((bf16[256,1536]{1,0:T(8,128)(2,1)}), bf16[2048,1536]{1,0:T(8,128)(2,1)}) %all-gather.25.cloned.1.call-update) | async-done | bytes 6291472 | tf_op jit(solution)/shard_map/all_gather | solution.py:247
  134.1 77.9 %all-gather.17.cloned.1.call-done = bf16[2048,1536]{1,0:T(8,128)(2,1)} async-done(((bf16[256,1536]{1,0:T(8,128)(2,1)}), bf16[2048,1536]{1,0:T(8,128)(2,1)}) %all-gather.17.cloned.1.call-update) | async-done | bytes 6291472 | tf_op jit(solution)/shard_map/all_gather | solution.py:243
  252.1 85.2 %all-gather.29.cloned.1.call-done = bf16[2048,2048]{1,0:T(8,128)(2,1)} async-done(((bf16[256,2048]{1,0:T(8,128)(2,1)}), bf16[2048,2048]{1,0:T(8,128)(2,1)}) %all-gather.29.cloned.1.call-update) | async-done | bytes 8388624 | tf_op jit(solution)/shard_map/all_gather | solution.py:249
  337.3 125.5 %all-gather.31.cloned.1.call-done = bf16[2048,2048]{1,0:T(8,128)(2,1)} async-done(((bf16[2048,256]{1,0:T(8,128)(2,1)}), bf16[2048,2048]{1,0:T(8,128)(2,1)}) %all-gather.31.cloned.1.call-update) | async-done | bytes 8388624 | tf_op jit(solution)/shard_map/all_gather | solution.py:250
  462.8 23.8 %fusion.66 = f32[512,2048]{1,0:T(8,128)} fusion(bf16[2048,2048]{1,0:T(8,128)(2,1)} %all-gather.31.cloned.1.call-done, bf16[2048,2048]{1,0:T(8,128)(2,1)} %all-gather.29.cloned.1.call-done, bf16[512,2048]{1,0:T(8,128)(2,1)S(1)} %copy-done.2, f32[2048]{0:T(1024)S(1)} %slice.183, f32[2048]{0:T(1024)S(1)} %bitcast.180, f32[2048]{0:T(1024)S(1)} %bitcast.181, ...), kind=kOutput, calls=%fused_computation.117 | convolution fusion | flops 8665432064 | bytes 23097344 | tf_op jit(solution)/shard_map/dot_general | solution.py:105
  486.6 27.3 %all-gather.27.cloned.1.call-done = bf16[512,2048]{1,0:T(8,128)(2,1)} async-done(((bf16[512,256]{1,0:T(8,128)(2,1)}), bf16[512,2048]{1,0:T(8,128)(2,1)}) %all-gather.27.cloned.1.call-update) | async-done | bytes 2097168 | tf_op jit(solution)/shard_map/all_gather | solution.py:248
  520.0 119.7 %all-gather.21.cloned.1.call-done = bf16[2048,2048]{1,0:T(8,128)(2,1)} async-done(((bf16[256,2048]{1,0:T(8,128)(2,1)}), bf16[2048,2048]{1,0:T(8,128)(2,1)}) %all-gather.21.cloned.1.call-update) | async-done | bytes 8388624 | tf_op jit(solution)/shard_map/all_gather | solution.py:245
  639.7 17.2 fusion.25
  656.9 109.0 %all-gather.23.cloned.1.call-done = bf16[2048,2048]{1,0:T(8,128)(2,1)} async-done(((bf16[2048,256]{1,0:T(8,128)(2,1)}), bf16[2048,2048]{1,0:T(8,128)(2,1)}) %all-gather.23.cloned.1.call-update) | async-done | bytes 8388624 | tf_op jit(solution)/shard_map/all_gather | solution.py:246
  776.4 41.4 %all-gather.19.cloned.1.call-done = bf16[512,2048]{1,0:T(8,128)(2,1)} async-done(((bf16[512,256]{1,0:T(8,128)(2,1)}), bf16[512,2048]{1,0:T(8,128)(2,1)}) %all-gather.19.cloned.1.call-update) | async-done | bytes 2097168 | tf_op jit(solution)/shard_map/all_gather | solution.py:244
  824.0 151.5 %all-reduce.11.cloned.1.call-done = (f32[512,2048]{1,0:T(8,128)}, f32[512,2048]{1,0:T(8,128)}) async-done(((f32[512,2048]{1,0:T(8,128)}, f32[512,2048]{1,0:T(8,128)}), (f32[512,2048]{1,0:T(8,128)}, f32[512,2048]{1,0:T(8,128)})) %all-reduce.11.cloned.1.call-update) | async-done | bytes 8388624 | tf_op jit(solution)/shard_map/psum | solution.py:266
  978.4 22.7 fusion.223
  1001.2 23.7 %fusion.224 = (f32[512]{0:T(512)S(1)}, f32[512,6400]{1,0:T(8,128)}) fusion(bf16[2048,6400]{1,0:T(8,128)(2,1)} %param.35, bf16[512,2048]{1,0:T(8,128)(2,1)S(1)} %copy-done.2, f32[512,2048]{1,0:T(8,128)} %get-tuple-element.120, f32[2048]{0:T(1024)S(1)} %bitcast.179, f32[2048]{0:T(1024)S(1)} %bitcast.178), kind=kOutput, calls=%fused_computation.331 | convolution fusion | flops 13430292480 | bytes 45631488 | tf_op jit(solution)/shard_map/dot_general | solution.py:179
  1058.7 22.0 psum.65
  1081.4 22.4 fusion.17
  1104.7 81.2 %all-reduce.7.cloned.1.call-done = f32[512,2048]{1,0:T(8,128)} async-done(((f32[512,2048]{1,0:T(8,128)}), f32[512,2048]{1,0:T(8,128)}) %all-reduce.7.cloned.1.call-update) | async-done | bytes 4194320 | tf_op jit(solution)/shard_map/psum | solution.py:293
  1258.5 13.0 fusion.230
  1271.5 115.7 %all-reduce.9.cloned.1.call-done = (f32[512,2048]{1,0:T(8,128)}, f32[512,2048]{1,0:T(8,128)}) async-done(((f32[512,2048]{1,0:T(8,128)}, f32[512,2048]{1,0:T(8,128)}), (f32[512,2048]{1,0:T(8,128)}, f32[512,2048]{1,0:T(8,128)})) %all-reduce.9.cloned.1.call-update) | async-done | bytes 8388624 | tf_op jit(solution)/shard_map/psum | solution.py:310
  1396.9 40.2 %all-reduce.2 = (bf16[6,2048]{1,0:T(8,128)(2,1)S(1)}, bf16[3584]{0:T(1024)(128)(2,1)S(1)}) all-reduce(bf16[6,2048]{1,0:T(8,128)(2,1)S(1)} %concatenate.36, bf16[3584]{0:T(1024)(128)(2,1)S(1)} %pad_maximum_fusion.2), channel_id=1, replica_groups=mesh['dp'=8,'tensor'=4] {'dp'}, use_global_device_ids=true, to_apply=%region_45.46 | all-reduce | flops 15872 | bytes 63488 | tf_op jit(solution)/shard_map/psum | solution.py:318
  1439.6 41.5 %reduce-scatter.7.cloned.1.call-done = f32[512,256]{1,0:T(8,128)} async-done(((f32[512,2048]{1,0:T(8,128)}), f32[512,256]{1,0:T(8,128)}) %reduce-scatter.7.cloned.1.call-update) | async-done | bytes 524304 | tf_op jit(solution)/shard_map/reduce_scatter | solution.py:304
  1482.9 209.0 %reduce-scatter.5.cloned.1.call-done = f32[256,1536]{1,0:T(8,128)} async-done(((f32[2048,1536]{1,0:T(8,128)}), f32[256,1536]{1,0:T(8,128)}) %reduce-scatter.5.cloned.1.call-update) | async-done | bytes 1572880 | tf_op jit(solution)/shard_map/reduce_scatter | solution.py:303
  1695.6 281.7 %reduce-scatter.9.cloned.1.call-done = f32[256,2048]{1,0:T(8,128)} async-done(((f32[2048,2048]{1,0:T(8,128)}), f32[256,2048]{1,0:T(8,128)}) %reduce-scatter.9.cloned.1.call-update) | async-done | bytes 2097168 | tf_op jit(solution)/shard_map/reduce_scatter | solution.py:307
  1980.7 282.4 %reduce-scatter.11.cloned.1.call-done = f32[2048,256]{1,0:T(8,128)} async-done(((f32[2048,2048]{1,0:T(8,128)}), f32[2048,256]{1,0:T(8,128)}) %reduce-scatter.11.cloned.1.call-update) | async-done | bytes 2097168 | tf_op jit(solution)/shard_map/reduce_scatter | solution.py:308
  2274.1 38.9 %psum.71 = f32[]{:T(128)} all-reduce(f32[]{:T(128)S(6)} %add.445), channel_id=1, replica_groups=mesh['dp'=8,'tensor'=4] {'dp','tensor'}, use_global_device_ids=true, to_apply=%region_51.52 | all-reduce | flops 1 | bytes 8 | tf_op jit(solution)/shard_map/psum | solution.py:332
  (321 shorter events, 260.0 us)
Async XLA Ops:
  7.2 104.8 %all-gather.25.cloned.1.call-start = ((), (), s32[]{:S(2)}) async-start(), calls=%async_computation.8 | async-start | bytes 7077888 | tf_op jit(solution)/shard_map/all_gather | solution.py:247
  7.9 204.1 %all-gather.17.cloned.1.call-start = ((), (), s32[]{:S(2)}) async-start(), calls=%async_computation.4 | async-start | bytes 7077888 | tf_op jit(solution)/shard_map/all_gather | solution.py:243
  10.4 326.9 %all-gather.29.cloned.1.call-start = ((), (), s32[]{:S(2)}) async-start(), calls=%async_computation.10 | async-start | bytes 9437184 | tf_op jit(solution)/shard_map/all_gather | solution.py:249
  11.1 451.7 %all-gather.31.cloned.1.call-start = ((), (), s32[]{:S(2)}) async-start(), calls=%async_computation.11 | async-start | bytes 9437184 | tf_op jit(solution)/shard_map/all_gather | solution.py:250
  11.7 502.3 %all-gather.27.cloned.1.call-start = ((), (), s32[]{:S(2)}) async-start(), calls=%async_computation.9 | async-start | bytes 2359296 | tf_op jit(solution)/shard_map/all_gather | solution.py:248
  12.3 627.3 %all-gather.21.cloned.1.call-start = ((), (), s32[]{:S(2)}) async-start(), calls=%async_computation.6 | async-start | bytes 9437184 | tf_op jit(solution)/shard_map/all_gather | solution.py:245
  15.3 750.6 %all-gather.23.cloned.1.call-start = ((), (), s32[]{:S(2)}) async-start(), calls=%async_computation.7 | async-start | bytes 9437184 | tf_op jit(solution)/shard_map/all_gather | solution.py:246
  18.0 94.0 %slice-start.1 = ((f32[3584]{0:T(1024)}), f32[1536]{0:T(1024)S(1)}, s32[]{:S(2)}) async-start(f32[3584]{0:T(1024)} %param.59), calls=%async_computation.20 | async-start | bytes 16384 | tf_op jit(solution)/shard_map/slice | solution.py:88
  18.0 799.8 %all-gather.19.cloned.1.call-start = ((), (), s32[]{:S(2)}) async-start(), calls=%async_computation.5 | async-start | bytes 2359296 | tf_op jit(solution)/shard_map/all_gather | solution.py:244
  18.8 956.6 %all-reduce.11.cloned.1.call-start = ((), (), s32[]{:S(2)}) async-start(), calls=%async_computation.18 | async-start | bytes 16777216 | tf_op jit(solution)/shard_map/psum | solution.py:266
  19.5 620.2 %copy-start.50 = (f32[512]{0:T(512)}, f32[512]{0:T(512)S(1)}, u32[]{:S(2)}) copy-start(f32[512]{0:T(512)S(1)} %broadcast_multiply_fusion.1) | copy-start | bytes 6148
  20.2 619.4 %copy-start.53 = (f32[512]{0:T(512)}, f32[512]{0:T(512)S(1)}, u32[]{:S(2)}) copy-start(f32[512]{0:T(512)S(1)} %fusion.157) | copy-start | bytes 6148
  21.5 190.6 %copy-start.41 = (f32[1,2048]{1,0:T(1,128)}, f32[1,2048]{1,0:T(1,128)S(1)}, u32[]{:S(2)}) copy-start(f32[1,2048]{1,0:T(1,128)S(1)} %get-tuple-element.187) | copy-start | bytes 24580
  21.5 190.5 %copy-start.62 = (f32[1,2048]{1,0:T(1,128)}, f32[1,2048]{1,0:T(1,128)S(1)}, u32[]{:S(2)}) copy-start(f32[1,2048]{1,0:T(1,128)S(1)} %get-tuple-element.186) | copy-start | bytes 24580
  21.5 618.2 %copy-start.39 = (f32[1,2048]{1,0:T(1,128)}, f32[1,2048]{1,0:T(1,128)S(1)}, u32[]{:S(2)}) copy-start(f32[1,2048]{1,0:T(1,128)S(1)} %get-tuple-element.185) | copy-start | bytes 24580
  21.5 618.2 %copy-start.60 = (f32[1,2048]{1,0:T(1,128)}, f32[1,2048]{1,0:T(1,128)S(1)}, u32[]{:S(2)}) copy-start(f32[1,2048]{1,0:T(1,128)S(1)} %get-tuple-element.184) | copy-start | bytes 24580
  21.7 227.2 %copy-start.10 = (pred[512,512]{0,1:T(8,128)(4,1)}, pred[512,512]{0,1:T(8,128)(4,1)S(1)}, u32[]{:S(2)}) copy-start(pred[512,512]{0,1:T(8,128)(4,1)S(1)} %fusion.129) | copy-start | bytes 786436
  126.8 85.2 %slice-start = ((f32[3584]{0:T(1024)}), f32[1536]{0:T(1024)S(1)}, s32[]{:S(2)}) async-start(f32[3584]{0:T(1024)} %param.41), calls=%async_computation.19 | async-start | bytes 16384 | tf_op jit(solution)/shard_map/slice | solution.py:88
  823.9 362.0 %all-reduce.7.cloned.1.call-start = ((), (), s32[]{:S(2)}) async-start(), calls=%async_computation.12 | async-start | bytes 8388608 | tf_op jit(solution)/shard_map/psum | solution.py:293
  1103.9 283.3 %all-reduce.9.cloned.1.call-start = ((), (), s32[]{:S(2)}) async-start(), calls=%async_computation.17 | async-start | bytes 16777216 | tf_op jit(solution)/shard_map/psum | solution.py:310
  1233.7 247.4 %reduce-scatter.7.cloned.1.call-start = ((), (), s32[]{:S(2)}) async-start(), calls=%async_computation.14 | async-start | bytes 4718592 | tf_op jit(solution)/shard_map/reduce_scatter | solution.py:304
  1238.6 453.2 %reduce-scatter.5.cloned.1.call-start = ((), (), s32[]{:S(2)}) async-start(), calls=%async_computation.13 | async-start | bytes 14155776 | tf_op jit(solution)/shard_map/reduce_scatter | solution.py:303
  1247.3 730.0 %reduce-scatter.9.cloned.1.call-start = ((), (), s32[]{:S(2)}) async-start(), calls=%async_computation.15 | async-start | bytes 18874368 | tf_op jit(solution)/shard_map/reduce_scatter | solution.py:307
  1258.5 1004.6 %reduce-scatter.11.cloned.1.call-start = ((), (), s32[]{:S(2)}) async-start(), calls=%async_computation.16 | async-start | bytes 18874368 | tf_op jit(solution)/shard_map/reduce_scatter | solution.py:308
  (67 other events, 797.3 us)
Sparse Core Ops, SparseCore 0:
  10.2 101.7 all-gather.24
  114.8 97.1 all-gather.16
  214.2 123.1 all-gather.28
  339.2 123.5 all-gather.30
  464.7 49.2 all-gather.26
  516.5 123.1 all-gather.20
  642.3 123.5 all-gather.22
  768.5 49.2 all-gather.18
  824.0 151.3 all-reduce.10
  1104.0 81.8 all-reduce.6
  1233.8 153.3 all-reduce.8
  1391.1 89.9 reduce-scatter.6
  1484.7 207.1 reduce-scatter.4
  1695.5 281.7 reduce-scatter.8
  1981.4 281.6 reduce-scatter.10
where the time goes:
time: 2350 us; the launch traced here: 2340 us
  waiting for transfers between devices  1840 us (78%)
  matrix products  228 us (10%)
  blocking collectives  122 us (5%)
  other arithmetic  85.4 us (4%)
  local copies, waits for them, and re-layouts  44.6 us (2%)
    reduce_scatter x1, waiting for transfers between devices, on_device(): lax.psum_scatter(contract_rows(active, branch_low), 'dp', scatter_dimensi...  282 us
    reduce_scatter x1, waiting for transfers between devices, on_device(): lax.psum_scatter(contract_rows(two_low, hidden_low), 'dp', scatter_dimens...  282 us
    reduce_scatter x1, waiting for transfers between devices, on_device(): lax.psum_scatter(contract_rows(one_low, mixed_grad), 'dp', scatter_dimens...  209 us
    psum x1, waiting for transfers between devices, on_device(): policy_sum, frozen_sum = lax.psum((policy_part, frozen_part), 'tensor')  151 us
    all_gather x1, waiting for transfers between devices, on_device(): lax.all_gather(down_frozen, 'dp', axis=1, tiled=True)  126 us
    all_gather x1, waiting for transfers between devices, on_device(): lax.all_gather(up_master.astype(jnp.bfloat16), 'dp', axis=0, tiled=True)  120 us
    psum x1, waiting for transfers between devices, on_device(): one_grad, two_grad = lax.psum((one_part, two_part), 'tensor')  116 us
    all_gather x1, waiting for transfers between devices, on_device(): lax.all_gather(down_master.astype(jnp.bfloat16), 'dp', axis=1, tiled=True)  109 us
  transfers between devices with their start and end apart: 15, of which 15 were waited for; matrix products, arithmetic and copies ran while one was open for 8% of the time, Pallas kernels for 0%

commit v1 on v0

v1 whole, which is shorter than its diff:
```python
import functools

import jax
import jax.numpy as jnp
from jax import lax
from jax.experimental import pallas as pl
from jax.experimental.pallas import tpu as pltpu
from jax.sharding import PartitionSpec as P

HD = 128
ROT = 32
SEGS = 4
STEP = 3
SPLIT = 4
QUARTERS = 4


EPS_NORM = 1e-05
BETA_KTO = 0.1
CLIP_NORM = 0.01
LEARN_RATE = 0.02
VECTOR_RATE = 0.2
BETA_FIRST = 0.9
BETA_SECOND = 0.999
ADAM_EPS = 1e-08
WEIGHT_DECAY = 0.01
MASKED = -1e30

MESH = pl.DeviceIdType.MESH
BF16 = jnp.bfloat16
F32 = jnp.float32
ANY_SPEC = pl.BlockSpec(memory_space=pltpu.HBM)
VMEM_SPEC = pl.BlockSpec(memory_space=pltpu.VMEM)


class Place:
    def __init__(self, inner):
        self.inner = inner
        self.dp = lax.axis_index("dp")
        self.t = lax.axis_index("tensor")
        self.o = self.dp // inner
        self.i = self.dp % inner
        self.near = self.t + 1 - 2 * (self.t % 2)
        self.far = (self.t + 2) % QUARTERS

    def outer_peer(self, shift):
        return (((self.o + shift) % SPLIT) * self.inner + self.i, self.t)

    def inner_peer(self, shift):
        return (self.o * self.inner + (self.i + shift) % self.inner, self.t)

    def near_peer(self):
        return (self.dp, self.near)

    def far_peer(self):
        return (self.dp, self.far)


def aligned(shard):
    return shard % 128 == 0


def greet(peers):
    barrier = pltpu.get_barrier_semaphore()
    for peer in peers:
        pl.semaphore_signal(barrier, inc=1, device_id=peer, device_id_type=MESH)
    pl.semaphore_wait(barrier, len(peers))


def remote(src, dst, send_sem, recv_sem, peer):
    copy = pltpu.make_async_remote_copy(
        src_ref=src,
        dst_ref=dst,
        send_sem=send_sem,
        recv_sem=recv_sem,
        device_id=peer,
        device_id_type=MESH,
    )
    copy.start()
    return copy


def spread_weights_kernel(inner, with_tokens, *refs):
    here = Place(inner)
    if with_tokens:
        (qkv, out, up, down, tokens, lengths, qkv_all, up_all, low_all, tokens_all, lengths_all,
         send_o, recv_o, send_i, recv_i, local, send_t, recv_t, send_l, recv_l) = refs
    else:
        qkv, out, up, down, qkv_all, up_all, low_all, send_o, recv_o, send_i, recv_i, local = refs
    shard = qkv.shape[0]
    width_qkv, width_up = qkv.shape[1] // SPLIT, up.shape[1] // SPLIT
    width_out, width_down = out.shape[0] // SPLIT, down.shape[0] // SPLIT

    def src(m, part):
        if m == 0:
            return qkv.at[:, pl.ds(part * width_qkv, width_qkv)]
        if m == 1:
            return up.at[:, pl.ds(part * width_up, width_up)]
        if m == 2:
            return out.at[pl.ds(part * width_out, width_out), :]
        return down.at[pl.ds(part * width_down, width_down), :]

    def dst(m, index):
        where = pl.ds(index * shard, shard)
        if m == 0:
            return qkv_all.at[where, :]
        if m == 1:
            return up_all.at[where, :]
        rows = pl.ds(0, width_out) if m == 2 else pl.ds(width_out, width_down)
        return low_all.at[rows, where] if aligned(shard) else low_all.at[index, rows, :]

    peers = [here.outer_peer(s) for s in range(1, SPLIT)]
    peers += [here.inner_peer(r) for r in range(1, inner)]
    if with_tokens:
        peers += [here.far_peer(), here.near_peer()]
    greet(peers)

    waits = []
    token_copies = []
    if with_tokens:
        rows = tokens.shape[0] // QUARTERS

        def piece(part, quarter):
            return tokens_all.at[pl.ds((part * QUARTERS + quarter) * rows, rows), :]

        for s in range(1, SPLIT):
            token_copies.append(
                remote(
                    tokens.at[pl.ds(here.t * rows, rows), :],
                    piece(here.o, here.t),
                    send_t.at[0, s - 1],
                    recv_t.at[0, s - 1],
                    here.outer_peer(s),
                )
            )
        for s in range(1, SPLIT):
            waits.append(
                remote(
                    lengths,
                    lengths_all.at[here.o],
                    send_l.at[s - 1],
                    recv_l.at[s - 1],
                    here.outer_peer(s),
                )
            )
    first = {}
    for m in range(4):
        for s in range(1, SPLIT):
            first[m, s] = remote(
                src(m, (here.o + s) % SPLIT),
                dst(m, here.dp),
                send_o.at[m, s - 1],
                recv_o.at[m, s - 1],
                here.outer_peer(s),
            )
    own = []
    for m in range(4):
        own.append(pltpu.make_async_copy(src(m, here.o), dst(m, here.dp), local.at[m]))
    if with_tokens:
        block = tokens.shape[0]
        own.append(
            pltpu.make_async_copy(
                tokens, tokens_all.at[pl.ds(here.o * block, block), :], local.at[4]
            )
        )
        own.append(pltpu.make_async_copy(lengths, lengths_all.at[here.o], local.at[5]))
    for copy in own:
        copy.start()
    for m in range(4):
        for r in range(1, inner):
            waits.append(
                remote(
                    src(m, here.o),
                    dst(m, here.dp),
                    send_i.at[m, 0, r - 1],
                    recv_i.at[m, 0, r - 1],
                    here.inner_peer(r),
                )
            )
    across = {}
    if with_tokens:
        for s in range(1, SPLIT):
            token_copies[s - 1].wait_recv()
            part = (here.o + SPLIT - s) % SPLIT
            across[s] = remote(
                piece(part, here.t),
                piece(part, here.t),
                send_t.at[1, s - 1],
                recv_t.at[1, s - 1],
                here.far_peer(),
            )
            waits.append(
                remote(
                    piece(part, here.t),
                    piece(part, here.t),
                    send_t.at[2, s - 1],
                    recv_t.at[2, s - 1],
                    here.near_peer(),
                )
            )
    for m in range(4):
        for s in range(1, SPLIT):
            first[m, s].wait_recv()
            index = ((here.o + SPLIT - s) % SPLIT) * inner + here.i
            for r in range(1, inner):
                waits.append(
                    remote(
                        dst(m, index),
                        dst(m, index),
                        send_i.at[m, s, r - 1],
                        recv_i.at[m, s, r - 1],
                        here.inner_peer(r),
                    )
                )
    if with_tokens:
        for s in range(1, SPLIT):
            across[s].wait_recv()
            part = (here.o + SPLIT - s) % SPLIT
            waits.append(
                remote(
                    piece(part, here.far),
                    piece(part, here.far),
                    send_t.at[3, s - 1],
                    recv_t.at[3, s - 1],
                    here.near_peer(),
                )
            )
        for copy in token_copies:
            copy.wait_send()
        for copy in across.values():
            copy.wait_send()
    for copy in first.values():
        copy.wait_send()
    for copy in own:
        copy.wait()
    for copy in waits:
        copy.wait()


def spread_weights(shards, inner, tokens, lengths, number):
    qkv, out, up, down = shards
    d_model = out.shape[1] * SPLIT * inner
    width = out.shape[0] // SPLIT + down.shape[0] // SPLIT
    shapes = [
        jax.ShapeDtypeStruct((d_model, qkv.shape[1] // SPLIT), BF16),
        jax.ShapeDtypeStruct((d_model, up.shape[1] // SPLIT), BF16),
        jax.ShapeDtypeStruct(
            (width, d_model) if aligned(out.shape[1]) else (SPLIT * inner, width, out.shape[1]),
            BF16,
        ),
    ]
    dma = pltpu.SemaphoreType.DMA
    scratch = [
        dma((4, SPLIT - 1)),
        dma((4, SPLIT - 1)),
        dma((4, SPLIT, max(inner - 1, 1))),
        dma((4, SPLIT, max(inner - 1, 1))),
        dma((6,)),
    ]
    operands = [qkv, out, up, down]
    if tokens is not None:
        operands += [tokens, lengths]
        shapes += [
            jax.ShapeDtypeStruct((tokens.shape[0] * SPLIT, tokens.shape[1]), BF16),
            jax.ShapeDtypeStruct((SPLIT, *lengths.shape), lengths.dtype),
        ]
        scratch += [
            dma((4, SPLIT - 1)),
            dma((4, SPLIT - 1)),
            dma((SPLIT - 1,)),
            dma((SPLIT - 1,)),
        ]
    qkv_all, up_all, low_all, *gathered = pl.pallas_call(
        functools.partial(spread_weights_kernel, inner, tokens is not None),
        out_shape=shapes,
        in_specs=[ANY_SPEC] * len(operands),
        out_specs=[ANY_SPEC] * len(shapes),
        scratch_shapes=scratch,
        compiler_params=pltpu.CompilerParams(collective_id=number, has_side_effects=True),
    )(*operands)
    if low_all.ndim == 3:
        low_all = jnp.swapaxes(low_all, 0, 1).reshape(width, d_model)
    return (qkv_all, up_all, low_all, *gathered)


def f32(value):
    return value.astype(F32)


def reduce_rows(here, part_ref, near_in, far_in, far_out, outer_in, outer_out, sems, last):
    rows = far_out.shape[1]
    near_send, near_recv, far_send, far_recv, outer_send, outer_recv = sems

    def rows_of(step, quarter):
        block = (here.o + 1 + step) % SPLIT
        return pl.ds((block * QUARTERS + quarter) * rows, rows)

    near = {}
    for step in range(SPLIT):
        for side, quarter in enumerate(((here.near + 2) % QUARTERS, here.near)):
            near[step, side] = remote(
                part_ref.at[rows_of(step, quarter), :],
                near_in.at[step, side],
                near_send.at[step, side],
                near_recv.at[step, side],
                here.near_peer(),
            )
    far = []
    for step in range(SPLIT):
        near[step, 0].wait_recv()
        far_out[step] = (f32(part_ref[rows_of(step, here.far), :]) + f32(near_in[step, 0])).astype(
            BF16
        )
        far.append(
            remote(
                far_out.at[step],
                far_in.at[step],
                far_send.at[step],
                far_recv.at[step],
                here.far_peer(),
            )
        )
    outer = []
    for step in range(SPLIT):
        near[step, 1].wait_recv()
        far[step].wait_recv()
        total = (
            f32(part_ref[rows_of(step, here.t), :]) + f32(near_in[step, 1]) + f32(far_in[step])
        )
        if step < SPLIT - 1:
            outer_out[step] = total.astype(BF16)
            outer.append(
                remote(
                    outer_out.at[step],
                    outer_in.at[step],
                    outer_send.at[step],
                    outer_recv.at[step],
                    here.outer_peer(step + 1),
                )
            )
        else:
            last(total)
    for copy in outer:
        copy.wait_recv()
    for copy in list(near.values()) + far + outer:
        copy.wait_send()


def gather_quarters(here, ref, rows, send, recv):
    def piece(quarter):
        return ref.at[pl.ds(quarter * rows, rows), :]

    far = remote(piece(here.t), piece(here.t), send.at[0], recv.at[0], here.far_peer())
    near = remote(piece(here.t), piece(here.t), send.at[1], recv.at[1], here.near_peer())
    far.wait_recv()
    passed = remote(piece(here.far), piece(here.far), send.at[2], recv.at[2], here.near_peer())
    near.wait_recv()
    passed.wait_recv()
    for copy in (far, near, passed):
        copy.wait_send()


def reduce_peers(here):
    return [here.outer_peer(s) for s in range(1, SPLIT)] + [here.far_peer(), here.near_peer()]


def branch_kernel(inner, part_ref, tokens_ref, rows_ref, final_ref, total, *scratch):
    here = Place(inner)
    buffers, sems, (send, recv) = scratch[:5], scratch[5:11], scratch[11:]
    rows = total.shape[0]
    greet(reduce_peers(here))
    mine = pl.ds(here.t * rows, rows)

    def last(value):
        total[...] = value

    reduce_rows(here, part_ref, *buffers, sems, last)
    outer_in = buffers[3]
    branch = total[...]
    for step in range(SPLIT - 1):
        branch = branch + f32(outer_in[step])
    branch = branch + rows_ref[0:1, :] + rows_ref[1:2, :]
    final_ref[mine, :] = (f32(tokens_ref[mine, :]) + branch).astype(BF16)
    gather_quarters(here, final_ref, rows, send, recv)


def input_kernel(inner, part_ref, tokens_ref, final_grad_ref, grad_ref, total, *scratch):
    here = Place(inner)
    buffers, sems, (send, recv) = scratch[:5], scratch[5:11], scratch[11:]
    rows = total.shape[0]
    greet(reduce_peers(here))
    mine = pl.ds(here.t * rows, rows)

    def last(value):
        total[...] = value

    reduce_rows(here, part_ref, *buffers, sems, last)
    outer_in = buffers[3]
    scaled = total[...]
    for step in range(SPLIT - 1):
        scaled = scaled + f32(outer_in[step])
    values = f32(tokens_ref[mine, :])
    centre = values - jnp.mean(values, axis=1, keepdims=True)
    spread = jnp.mean(centre * centre, axis=1, keepdims=True)
    scale = lax.rsqrt(spread + EPS_NORM)
    normed = centre * scale
    along = jnp.mean(scaled * normed, axis=1, keepdims=True)
    change = scale * (scaled - jnp.mean(scaled, axis=1, keepdims=True) - normed * along)
    grad_ref[mine, :] = (final_grad_ref[...] + change).astype(BF16)
    gather_quarters(here, grad_ref, rows, send, recv)


def reduce_scratch(rows, width):
    dma = pltpu.SemaphoreType.DMA
    return [
        pltpu.VMEM((rows, width), F32),
        pltpu.VMEM((SPLIT, 2, rows, width), BF16),
        pltpu.VMEM((SPLIT, rows, width), BF16),
        pltpu.VMEM((SPLIT, rows, width), BF16),
        pltpu.VMEM((SPLIT - 1, rows, width), BF16),
        pltpu.VMEM((SPLIT - 1, rows, width), BF16),
        dma((SPLIT, 2)),
        dma((SPLIT, 2)),
        dma((SPLIT,)),
        dma((SPLIT,)),
        dma((SPLIT - 1,)),
        dma((SPLIT - 1,)),
        dma((3,)),
        dma((3,)),
    ]


def reduce_call(body, inner, part, tokens, extra, number):
    block, width = tokens.shape
    return pl.pallas_call(
        functools.partial(body, inner),
        out_shape=jax.ShapeDtypeStruct((block, width), BF16),
        in_specs=[VMEM_SPEC] * 3,
        out_specs=VMEM_SPEC,
        scratch_shapes=reduce_scratch(block // QUARTERS, width),
        compiler_params=pltpu.CompilerParams(
            collective_id=number, has_side_effects=True, vmem_limit_bytes=56 * 1024 * 1024
        ),
    )(part, tokens, extra)


def final_grad_kernel(
    inner, part_ref, quarter_ref, branch_all, near_in, far_in, far_out, low, near_out,
    near_send, near_recv, far_send, far_recv, send, recv, local,
):
    here = Place(inner)
    rows = quarter_ref.shape[0]
    greet(reduce_peers(here))

    def rows_of(quarter):
        return pl.ds(quarter * rows, rows)

    near = []
    for side, quarter in enumerate(((here.near + 2) % QUARTERS, here.near)):
        near_out[side] = part_ref[rows_of(quarter), :].astype(BF16)
        near.append(
            remote(
                near_out.at[side],
                near_in.at[side],
                near_send.at[side],
                near_recv.at[side],
                here.near_peer(),
            )
        )
    near[0].wait_recv()
    far_out[...] = (part_ref[rows_of(here.far), :] + f32(near_in[0])).astype(BF16)
    far = remote(far_out, far_in, far_send, far_recv, here.far_peer())
    near[1].wait_recv()
    far.wait_recv()
    quarter_ref[...] = part_ref[rows_of(here.t), :] + f32(near_in[1]) + f32(far_in[...])
    low[...] = quarter_ref[...].astype(BF16)
    for copy in near + [far]:
        copy.wait_send()

    def piece(part, quarter):
        return branch_all.at[pl.ds((part * QUARTERS + quarter) * rows, rows), :]

    outer = [
        remote(
            low, piece(here.o, here.t), send.at[0, s], recv.at[0, s], here.outer_peer(s)
        )
        for s in range(1, SPLIT)
    ]
    own = pltpu.make_async_copy(low, piece(here.o, here.t), local)
    own.start()
    across, beside = [], []
    for s in range(SPLIT):
        part = (here.o + SPLIT - s) % SPLIT
        if s:
            outer[s - 1].wait_recv()
        source = piece(part, here.t) if s else low
        across.append(
            remote(source, piece(part, here.t), send.at[1, s], recv.at[1, s], here.far_peer())
        )
        beside.append(
            remote(source, piece(part, here.t), send.at[2, s], recv.at[2, s], here.near_peer())
        )
    for s in range(SPLIT):
        part = (here.o + SPLIT - s) % SPLIT
        across[s].wait_recv()
        beside.append(
            remote(
                piece(part, here.far),
                piece(part, here.far),
                send.at[3, s],
                recv.at[3, s],
                here.near_peer(),
            )
        )
    for copy in beside:
        copy.wait_recv()
    for copy in outer + across + beside:
        copy.wait_send()
    own.wait()


def final_grad_call(part, inner, number):
    block, width = part.shape
    rows = block // QUARTERS
    dma = pltpu.SemaphoreType.DMA
    return pl.pallas_call(
        functools.partial(final_grad_kernel, inner),
        out_shape=[
            jax.ShapeDtypeStruct((rows, width), F32),
            jax.ShapeDtypeStruct((SPLIT * block, width), BF16),
        ],
        in_specs=[VMEM_SPEC],
        out_specs=[VMEM_SPEC, ANY_SPEC],
        scratch_shapes=[
            pltpu.VMEM((2, rows, width), BF16),
            pltpu.VMEM((rows, width), BF16),
            pltpu.VMEM((rows, width), BF16),
            pltpu.VMEM((rows, width), BF16),
            pltpu.VMEM((2, rows, width), BF16),
            dma((2,)),
            dma((2,)),
            dma,
            dma,
            dma((4, SPLIT)),
            dma((4, SPLIT)),
            dma,
        ],
        compiler_params=pltpu.CompilerParams(
            collective_id=number, has_side_effects=True, vmem_limit_bytes=48 * 1024 * 1024
        ),
    )(part)


def weight_grads_kernel(inner, qkv, up, low, *refs):
    here = Place(inner)
    outs, inputs, sends = refs[:4], refs[4:8], refs[8:12]
    send_i, recv_i, send_o, recv_o, local = refs[12:]
    shard = outs[0].shape[0]
    width_out = outs[2].shape[0] // SPLIT
    width_down = outs[3].shape[0] // SPLIT

    def src(m, index):
        where = pl.ds(index * shard, shard)
        if m == 0:
            return qkv.at[where, :]
        if m == 1:
            return up.at[where, :]
        rows = pl.ds(0, width_out) if m == 2 else pl.ds(width_out, width_down)
        return low.at[rows, where] if aligned(shard) else low.at[index, rows, :]

    def dst(m):
        if m < 2:
            width = outs[m].shape[1] // SPLIT
            return outs[m].at[:, pl.ds(here.o * width, width)]
        width = outs[m].shape[0] // SPLIT
        return outs[m].at[pl.ds(here.o * width, width), :]

    peers = [here.outer_peer(s) for s in range(1, SPLIT)]
    peers += [here.inner_peer(r) for r in range(1, inner)]
    greet(peers)
    order = (2, 3, 1, 0)
    first = {}
    for m in order:
        for s in range(SPLIT):
            part = (here.o + s) % SPLIT
            for r in range(1, inner):
                first[m, s, r] = remote(
                    src(m, part * inner + (here.i + r) % inner),
                    inputs[m].at[s, r - 1],
                    send_i.at[m, s, r - 1],
                    recv_i.at[m, s, r - 1],
                    here.inner_peer(r),
                )
    last, own = [], []
    for m in order:
        for s in range(SPLIT):
            part = (here.o + s) % SPLIT
            total = f32(src(m, part * inner + here.i)[...])
            for r in range(1, inner):
                first[m, s, r].wait_recv()
                total = total + f32(inputs[m][s, r - 1])
            sends[m][s] = total.astype(BF16)
            if s:
                last.append(
                    remote(
                        sends[m].at[s],
                        dst(m),
                        send_o.at[m, s - 1],
                        recv_o.at[m, s - 1],
                        here.outer_peer(s),
                    )
                )
            else:
                copy = pltpu.make_async_copy(sends[m].at[0], dst(m), local.at[m])
                copy.start()
                own.append(copy)
    for copy in last:
        copy.wait()
    for copy in own:
        copy.wait()
    for copy in first.values():
        copy.wait_send()


def weight_grads_call(grads, shards, inner, number):
    dma = pltpu.SemaphoreType.DMA
    qkv, out, up, down = shards
    ordered = (qkv, up, out, down)
    if not aligned(out[1]):
        low = grads[2].reshape(grads[2].shape[0], SPLIT * inner, out[1])
        grads = (*grads[:2], jnp.swapaxes(low, 0, 1))
    pieces = [
        (qkv[0], qkv[1] // SPLIT),
        (up[0], up[1] // SPLIT),
        (out[0] // SPLIT, out[1]),
        (down[0] // SPLIT, down[1]),
    ]
    peers = max(inner - 1, 1)
    return pl.pallas_call(
        functools.partial(weight_grads_kernel, inner),
        out_shape=[jax.ShapeDtypeStruct(shape, BF16) for shape in ordered],
        in_specs=[VMEM_SPEC] * 3,
        out_specs=[ANY_SPEC] * 4,
        scratch_shapes=[pltpu.VMEM((SPLIT, peers, *piece), BF16) for piece in pieces]
        + [pltpu.VMEM((SPLIT, *piece), BF16) for piece in pieces]
        + [
            dma((4, SPLIT, peers)),
            dma((4, SPLIT, peers)),
            dma((4, SPLIT - 1)),
            dma((4, SPLIT - 1)),
            dma((4,)),
        ],
        compiler_params=pltpu.CompilerParams(
            collective_id=number, has_side_effects=True, vmem_limit_bytes=48 * 1024 * 1024
        ),
    )(*grads)


def combined_all(value, axis, join):
    pieces = jax.tree.map(lambda part: lax.all_gather(part, axis), value)
    head = jax.tree.map(lambda part: part[0], pieces)
    tail = jax.tree.map(lambda part: part[1:], pieces)
    total, _ = lax.scan(lambda total, section: (join(total, section), None), head, tail)
    return total


def rotate(values, positions, direction):
    half_rot = ROT // 2
    frequency = 10000.0 ** (-2.0 * jnp.arange(half_rot, dtype=F32) / ROT)
    angles = positions.astype(F32)[..., None] * frequency
    cosine = jnp.cos(angles)[..., None, :]
    sine_part = direction * jnp.sin(angles)[..., None, :]
    first_half = values[..., :half_rot]
    second_half = values[..., half_rot:ROT]
    return jnp.concatenate(
        [
            first_half * cosine - second_half * sine_part,
            second_half * cosine + first_half * sine_part,
            values[..., ROT:],
        ],
        axis=-1,
    )


def doc_layout(lengths_row, row_count):
    ends, run = [], 0
    for segment in range(lengths_row.shape[0]):
        run = run + lengths_row[segment]
        ends.append(run)
    doc_ends = jnp.stack(ends)
    starts = doc_ends - lengths_row
    index_rows = jnp.arange(row_count, dtype=jnp.int32)
    member = (index_rows[:, None] >= starts[None, :]) & (index_rows[:, None] < doc_ends[None, :])
    doc_ids = jnp.arange(lengths_row.shape[0], dtype=jnp.int32)
    doc_of = jnp.sum(jnp.where(member, doc_ids[None, :], 0), axis=1)
    positions = index_rows - jnp.sum(jnp.where(member, starts[None, :], 0), axis=1)
    return (member, positions, doc_of)


def allowed_keys(doc_of):
    index_rows = jnp.arange(doc_of.shape[-1], dtype=jnp.int32)
    return (doc_of[..., :, None] == doc_of[..., None, :]) & (
        index_rows[:, None] >= index_rows[None, :]
    )


def contract_rows(left_rows, right_rows):
    return lax.dot_general(
        left_rows, right_rows, (((0,), (0,)), ((), ())), preferred_element_type=F32
    )


def contract_cols(left_rows, right_rows):
    return lax.dot_general(
        left_rows, right_rows, (((1,), (1,)), ((), ())), preferred_element_type=F32
    )


def normed_rows(normed, gain_row, shift_row):
    return (normed * gain_row + shift_row).astype(BF16)


def attention_mlp(one_low, two_low, qkv_bias, up_bias, weight_set, positions, allowed):
    qkv_all, up_all, low_all = weight_set
    blocks, block = positions.shape
    heads_local = qkv_bias.shape[0] // (3 * HD)
    mixed_proj = jnp.dot(one_low, qkv_all, preferred_element_type=F32) + qkv_bias
    mixed_proj = mixed_proj.reshape(blocks, block, heads_local, 3, HD)
    query_low = rotate(mixed_proj[:, :, :, 0], positions, 1.0).astype(BF16)
    key_low = rotate(mixed_proj[:, :, :, 1], positions, 1.0).astype(BF16)
    value_low = mixed_proj[:, :, :, 2].astype(BF16)
    scores = jnp.einsum(
        "bqhd,bkhd->bhqk", query_low, key_low, preferred_element_type=F32
    ) * HD ** (-0.5)
    scores = jnp.where(allowed[:, None], scores, MASKED)
    highest = jnp.max(scores, axis=3, keepdims=True)
    log_total = highest + jnp.log(jnp.sum(jnp.exp(scores - highest), axis=3, keepdims=True))
    probs_low = jnp.exp(scores - log_total).astype(BF16)
    attended = jnp.einsum("bhqk,bkhd->bqhd", probs_low, value_low, preferred_element_type=F32)
    attended = attended.reshape(blocks * block, heads_local * HD).astype(BF16)
    hidden = jnp.dot(two_low, up_all, preferred_element_type=F32) + up_bias
    active = jax.nn.gelu(hidden, approximate=False).astype(BF16)
    joined = jnp.concatenate([attended, active], axis=1)
    branch_part = jnp.dot(joined, low_all, preferred_element_type=F32).astype(BF16)
    kept_values = (query_low, key_low, value_low, log_total, hidden, joined)
    return (branch_part, kept_values)


def layer_backward(branch_low, kept_values, weight_set, positions, allowed):
    qkv_all, up_all, low_all = weight_set
    query_low, key_low, value_low, log_total, hidden, joined = kept_values
    blocks, block, heads_local, _ = query_low.shape
    cut = heads_local * HD
    joined_grad = contract_cols(branch_low, low_all)
    active_grad = joined_grad[:, cut:]
    cumulative = 0.5 * (1.0 + lax.erf(hidden * 0.7071067811865476))
    density = jnp.exp(-0.5 * hidden * hidden) * 0.3989422804014327
    hidden_low = (active_grad * (cumulative + hidden * density)).astype(BF16)
    attended_grad = joined_grad[:, :cut].reshape(blocks, block, heads_local, HD).astype(BF16)
    score_scale = HD ** (-0.5)
    scores = (
        jnp.einsum("bqhd,bkhd->bhqk", query_low, key_low, preferred_element_type=F32) * score_scale
    )
    scores = jnp.where(allowed[:, None], scores, MASKED)
    probs = jnp.exp(scores - log_total)
    prob_grad = jnp.einsum("bqhd,bkhd->bhqk", attended_grad, value_low, preferred_element_type=F32)
    value_grad = jnp.einsum(
        "bhqk,bqhd->bkhd", probs.astype(BF16), attended_grad, preferred_element_type=F32
    )
    score_grad = (probs * (prob_grad - jnp.sum(probs * prob_grad, axis=3, keepdims=True))).astype(
        BF16
    )
    query_grad = (
        jnp.einsum("bhqk,bkhd->bqhd", score_grad, key_low, preferred_element_type=F32) * score_scale
    )
    key_grad = (
        jnp.einsum("bhqk,bqhd->bkhd", score_grad, query_low, preferred_element_type=F32)
        * score_scale
    )
    mixed_grad = jnp.stack(
        [rotate(query_grad, positions, -1.0), rotate(key_grad, positions, -1.0), value_grad], axis=3
    )
    mixed_grad = mixed_grad.reshape(blocks * block, heads_local * 3 * HD).astype(BF16)
    one_part = contract_cols(mixed_grad, qkv_all)
    two_part = contract_cols(hidden_low, up_all)
    return (one_part, two_part, mixed_grad, hidden_low)


def vocab_stats(final_low, head_weight, targets, vocab_start):
    logits = jnp.dot(final_low, head_weight, preferred_element_type=F32)
    highest = jnp.max(logits, axis=1)
    log_total = highest + jnp.log(jnp.sum(jnp.exp(logits - highest[:, None]), axis=1))
    column = vocab_start + lax.broadcasted_iota(jnp.int32, logits.shape, 1)
    chosen = column == targets[:, None]
    picked = jnp.sum(jnp.where(chosen, logits, 0.0), axis=1)
    return (logits, log_total, picked, chosen)


def combine_totals(first_set, second_set):
    return (
        jnp.logaddexp(first_set[0], second_set[0]),
        first_set[1] + second_set[1],
        jnp.logaddexp(first_set[2], second_set[2]),
        first_set[3] + second_set[3],
    )


def adam_step(master, mean_old, square_old, gradient, factor, rate, decay_rate):
    clipped = f32(gradient) * factor
    mean_new = BETA_FIRST * mean_old + (1.0 - BETA_FIRST) * clipped
    square_new = BETA_SECOND * square_old + (1.0 - BETA_SECOND) * clipped * clipped
    mean_hat = mean_new / (1.0 - BETA_FIRST**STEP)
    square_hat = square_new / (1.0 - BETA_SECOND**STEP)
    master_new = master - rate * (
        mean_hat / (jnp.sqrt(square_hat) + ADAM_EPS) + decay_rate * master
    )
    return (mean_new, square_new, master_new)


def on_device(
    inputs,
    targets,
    doc_lengths,
    desirable,
    head_weight,
    qkv_master,
    out_master,
    up_master,
    down_master,
    vectors,
    hidden_bias,
    qkv_mean,
    out_mean,
    up_mean,
    down_mean,
    vectors_mean,
    hidden_mean,
    qkv_square,
    out_square,
    up_square,
    down_square,
    vectors_square,
    hidden_square,
    qkv_frozen,
    out_frozen,
    up_frozen,
    down_frozen,
    vectors_frozen,
    hidden_frozen,
):
    dp_size = lax.axis_size("dp")
    tensor_size = lax.axis_size("tensor")
    inner = dp_size // SPLIT
    outer_index = lax.axis_index("dp") // inner
    block = inputs.shape[0]
    lengths_tile = jnp.zeros((8, 128), jnp.int32).at[0, :SEGS].set(doc_lengths[0])
    masters = tuple(w.astype(BF16) for w in (qkv_master, out_master, up_master, down_master))
    *policy_set, tokens_all, lengths_all = spread_weights(masters, inner, inputs, lengths_tile, 0)
    frozen_set = spread_weights(
        (qkv_frozen, out_frozen, up_frozen, down_frozen), inner, None, None, 1
    )
    member, _, _ = doc_layout(doc_lengths[0], block)
    _, positions, doc_of = jax.vmap(lambda row: doc_layout(row, block))(lengths_all[:, 0, :SEGS])
    allowed = allowed_keys(doc_of)

    cut = qkv_master.shape[1]
    width_qkv, width_up = cut // SPLIT, up_master.shape[1] // SPLIT

    def own_bias(bias):
        return (
            lax.dynamic_slice(bias, (outer_index * width_qkv,), (width_qkv,)),
            lax.dynamic_slice(bias, (cut + outer_index * width_up,), (width_up,)),
        )

    values = f32(tokens_all)
    centre = values - jnp.mean(values, axis=1, keepdims=True)
    scale = lax.rsqrt(jnp.mean(centre * centre, axis=1, keepdims=True) + EPS_NORM)
    normed = centre * scale
    one_low = normed_rows(normed, vectors[0], vectors[1])
    two_low = normed_rows(normed, vectors[2], vectors[3])
    policy_part, kept_values = attention_mlp(
        one_low, two_low, *own_bias(hidden_bias), policy_set, positions, allowed
    )
    final_low = reduce_call(branch_kernel, inner, policy_part, inputs, vectors[4:6], 2)
    frozen_part, _ = attention_mlp(
        normed_rows(normed, vectors_frozen[0], vectors_frozen[1]),
        normed_rows(normed, vectors_frozen[2], vectors_frozen[3]),
        *own_bias(hidden_frozen),
        frozen_set,
        positions,
        allowed,
    )
    frozen_low = reduce_call(branch_kernel, inner, frozen_part, inputs, vectors_frozen[4:6], 3)
    vocab_start = lax.axis_index("tensor") * head_weight.shape[1]
    policy_logits, policy_total, policy_pick, chosen = vocab_stats(
        final_low, head_weight, targets, vocab_start
    )
    _, frozen_total, frozen_pick, _ = vocab_stats(frozen_low, head_weight, targets, vocab_start)
    policy_total, policy_pick, frozen_total, frozen_pick = combined_all(
        (policy_total, policy_pick, frozen_total, frozen_pick), "tensor", combine_totals
    )
    doc_weights = member.astype(F32)
    policy_docs = jnp.sum(doc_weights * (policy_pick - policy_total)[:, None], axis=0)
    frozen_docs = jnp.sum(doc_weights * (frozen_pick - frozen_total)[:, None], axis=0)
    reward = policy_docs - frozen_docs
    seq_count = dp_size * SEGS
    reward_shift = lax.psum(jnp.sum(reward), "dp") / seq_count
    sigmoid_value = jax.nn.sigmoid(BETA_KTO * (reward - reward_shift))
    labels = desirable[0].astype(F32)
    doc_grad = BETA_KTO * sigmoid_value * (1.0 - sigmoid_value) * (1.0 - 2.0 * labels) / seq_count
    token_grad = jnp.sum(doc_weights * doc_grad[None, :], axis=1)
    logit_grad = (
        token_grad[:, None]
        * (chosen.astype(F32) - jnp.exp(policy_logits - policy_total[:, None]))
    ).astype(BF16)
    final_part = contract_cols(logit_grad, head_weight)
    final_quarter, branch_low = final_grad_call(final_part, inner, 4)
    joined = kept_values[5]
    one_part, two_part, mixed_grad, hidden_low = layer_backward(
        branch_low, kept_values, policy_set, positions, allowed
    )
    scaled_part = (one_part * vectors[0] + two_part * vectors[2]).astype(BF16)
    input_grad = f32(reduce_call(input_kernel, inner, scaled_part, inputs, final_quarter, 5))
    shards = tuple(w.shape for w in masters)
    grads = (
        contract_rows(one_low, mixed_grad).astype(BF16),
        contract_rows(two_low, hidden_low).astype(BF16),
        contract_rows(joined, branch_low).astype(BF16),
    )
    qkv_grad, up_grad, out_grad, down_grad = weight_grads_call(grads, shards, inner, 6)
    branch_bias = jnp.sum(f32(final_quarter.astype(BF16)), axis=0)
    vector_grad = jnp.stack(
        [
            jnp.sum(one_part * normed, axis=0),
            jnp.sum(one_part, axis=0),
            jnp.sum(two_part * normed, axis=0),
            jnp.sum(two_part, axis=0),
            branch_bias,
            branch_bias,
        ]
    )
    bias_grad = jnp.concatenate(
        [
            lax.dynamic_update_slice(
                jnp.zeros((cut,), F32),
                jnp.sum(mixed_grad, axis=0, dtype=F32),
                (outer_index * width_qkv,),
            ),
            lax.dynamic_update_slice(
                jnp.zeros((up_master.shape[1],), F32),
                jnp.sum(hidden_low, axis=0, dtype=F32),
                (outer_index * width_up,),
            ),
        ]
    )
    vector_grad, hidden_grad = (
        f32(lax.psum(vector_grad.astype(BF16), ("dp", "tensor"))),
        f32(lax.psum(bias_grad.astype(BF16), "dp")),
    )
    local_square = sum(jnp.sum(f32(g) * f32(g)) for g in (qkv_grad, out_grad, up_grad, down_grad))
    local_square = (
        local_square
        + jnp.sum(vector_grad * vector_grad) / (dp_size * tensor_size)
        + jnp.sum(hidden_grad * hidden_grad) / dp_size
    )
    grad_norm = jnp.sqrt(lax.psum(local_square, ("dp", "tensor")))
    factor = jnp.minimum(1.0, CLIP_NORM / (grad_norm + 1e-06))
    qkv_state = adam_step(
        qkv_master, qkv_mean, qkv_square, qkv_grad, factor, LEARN_RATE, WEIGHT_DECAY
    )
    out_state = adam_step(
        out_master, out_mean, out_square, out_grad, factor, LEARN_RATE, WEIGHT_DECAY
    )
    up_state = adam_step(up_master, up_mean, up_square, up_grad, factor, LEARN_RATE, WEIGHT_DECAY)
    down_state = adam_step(
        down_master, down_mean, down_square, down_grad, factor, LEARN_RATE, WEIGHT_DECAY
    )
    vector_state = adam_step(
        vectors, vectors_mean, vectors_square, vector_grad, factor, VECTOR_RATE, 0.0
    )
    hidden_state = adam_step(
        hidden_bias, hidden_mean, hidden_square, hidden_grad, factor, VECTOR_RATE, 0.0
    )
    return (
        final_low,
        input_grad,
        grad_norm,
        *qkv_state,
        *out_state,
        *up_state,
        *down_state,
        *vector_state,
        *hidden_state,
    )


def solution(mesh):
    rows, cols = P("dp", "tensor"), P("tensor", "dp")
    matrices = (rows, cols, rows, cols)
    placed = (
        P("dp", None),
        P("dp"),
        P("dp", None),
        P("dp", None),
        P(None, "tensor"),
        *matrices,
        P(),
        P("tensor"),
        *matrices,
        P(),
        P("tensor"),
        *matrices,
        P(),
        P("tensor"),
        *matrices,
        P(),
        P("tensor"),
    )
    return jax.shard_map(
        on_device,
        mesh=mesh,
        in_specs=placed,
        out_specs=(
            P("dp", None),
            P("dp", None),
            P(),
            *(spec for spec in matrices for _ in range(3)),
            P(),
            P(),
            P(),
            P("tensor"),
            P("tensor"),
            P("tensor"),
        ),
        check_vma=False,
    )
```

time: 2350 us -> 1140 us (0.49)
  waiting for transfers between devices: 1840 us -> 0 us
  Pallas kernels: 0 us -> 639 us
  blocking collectives: 122 us -> 150 us
    reduce_scatter x4 -> x0, waiting for transfers between devices: 815 us -> none  [the longest x1 282 us: on_device(): lax.psum_scatter(contract_rows(active, branch_low), 'dp', scatter_dimensi...]
    all_gather x8 -> x0, waiting for transfers between devices: 674 us -> none  [the longest x1 126 us: on_device(): lax.all_gather(down_frozen, 'dp', axis=1, tiled=True)]
    pallas_call x0 -> x7, Pallas kernels: none -> 639 us  [the longest x3 251 us: reduce_call(): pl.pallas_call(functools.partial(body, inner), out_shape=jax.ShapeDtypeSt...]
    psum x3 -> x0, waiting for transfers between devices: 348 us -> none  [the longest x1 151 us: on_device(): policy_sum, frozen_sum = lax.psum((policy_part, frozen_part), 'tensor')]
    psum x1 -> x2, blocking collectives: 40.2 us -> 65.5 us  [the longest x1 37.5 us: on_device(): lax.psum(vector_grad.astype(BF16), ('dp', 'tensor'))]
    dot_general x17 -> x16, matrix products: 140 us -> 127 us  [the longest x2 45.9 us: vocab_stats(): logits = jnp.dot(final_low, head_weight, preferred_element_type=F32)]
    dot_general x5 -> x4, matrix products: 51.3 us -> 56.5 us  [contract_cols(): lax.dot_general(left_rows, right_rows, (((1,), (1,)), ((), ())), preferre...]
  transfers between devices with their start and end apart: 15 -> 0, of which waited for: 15 -> 0; matrix products, arithmetic and copies ran while one was open for 8% -> 0% of each run, Pallas kernels for 0% -> 0%
where the time goes in v1:
time: 1140 us
  Pallas kernels  639 us (56%)
  matrix products  208 us (18%)
  blocking collectives  150 us (13%)
  other arithmetic  73.8 us (6%)
  local copies, waits for them, and re-layouts  53.6 us (5%)
    pallas_call x3, Pallas kernels, reduce_call(): pl.pallas_call(functools.partial(body, inner), out_shape=jax.ShapeDtypeSt...  251 us
    pallas_call x2, Pallas kernels, spread_weights(): pl.pallas_call(functools.partial(spread_weights_kernel, inner, tokens is...  224 us
    pallas_call x1, Pallas kernels, weight_grads_call(): pl.pallas_call(functools.partial(weight_grads_kernel, inner), out_shape=[...  85.5 us
    pallas_call x1, Pallas kernels, final_grad_call(): pl.pallas_call(functools.partial(final_grad_kernel, inner), out_shape=[ja...  78.6 us
    dot_general x4, matrix products, contract_cols(): lax.dot_general(left_rows, right_rows, (((1,), (1,)), ((), ())), preferre...  56.5 us
    dot_general x2, matrix products, vocab_stats(): logits = jnp.dot(final_low, head_weight, preferred_element_type=F32)  45.9 us
    psum x1, blocking collectives, on_device(): grad_norm = jnp.sqrt(lax.psum(local_square, ('dp', 'tensor')))  42.5 us
    psum x1, blocking collectives, on_device(): lax.psum(vector_grad.astype(BF16), ('dp', 'tensor'))  37.5 us

profile of v1, /device:TPU:0, one launch (start us, length us, event | category | flops | bytes accessed | tf_op | source)
XLA Modules:
  0.0 1135.6 jit_solution(1047889182865981107)
XLA Ops:
  7.9 138.6 %shard_map.436 = (bf16[2048,384]{1,0:T(8,128)(2,1)}, bf16[2048,512]{1,0:T(8,128)(2,1)}, bf16[640,2048]{1,0:T(8,128)(2,1)}, bf16[2048,2048]{1,0:T(8,128)(2,1)}, s32[4,8,128]{2,1,0:T(8,128)}) custom-call(bf16[256,1536]{1,0:T(8,128)(2,1)} %convert_element_type.218.refs_0_, bf16[512,256]{1,0:T(8,128)(2,1)} %convert_element_type.219.refs_1_, ...), custom_call_target="tpu_custom_call" | custom-call | tf_op jit(solution)/shard_map/pallas_call | solution.py:273
  154.7 85.8 %shard_map.438 = (bf16[2048,384]{1,0:T(8,128)(2,1)}, bf16[2048,512]{1,0:T(8,128)(2,1)}, bf16[640,2048]{1,0:T(8,128)(2,1)}) custom-call(bf16[256,1536]{1,0:T(8,128)(2,1)} %refs_0_.1, bf16[512,256]{1,0:T(8,128)(2,1)} %refs_1_.1, bf16[256,2048]{1,0:T(8,128)(2,1)} %refs_2_.1, bf16[2048,256]{1,0:T(8,128)(2,1)} %refs_3_.1), custom_call_target="tpu_custom_call" | custom-call | tf_op jit(solution)/shard_map/pallas_call | solution.py:273
  260.3 9.8 fusion.9
  308.2 16.8 %fusion.43 = bf16[2048,512]{1,0:T(8,128)(2,1)S(1)} fusion(bf16[2048,512]{1,0:T(8,128)(2,1)} %get-tuple-element.103, bf16[2048,2048]{1,0:T(8,128)(2,1)} %get-tuple-element.97, f32[2048]{0:T(1024)S(1)} %bitcast.242, f32[2048]{0:T(1024)S(1)} %bitcast.241, f32[2048]{0:T(1024)S(1)} %add_rsqrt_fusion, f32[2048]{0:T(1024)S(1)} %broadcast_multiply_fusion, ...), kind=kOutput, calls=%fused_computation.59 | convolution fusion | flops 4389339136 | bytes 12617728 | tf_op jit(solution)/shard_map/dot_general | solution.py:741
  324.9 8.9 convolution_convert_fusion.part_ref
  335.3 82.0 %shard_map.439 = bf16[512,2048]{1,0:T(8,128)(2,1)} custom-call(bf16[2048,2048]{1,0:T(8,128)(2,1)} %convolution_convert_fusion.part_ref, bf16[512,2048]{1,0:T(8,128)(2,1)} %tokens_ref.5, f32[2,2048]{1,0:T(2,128)} %slice.229.rows_ref), custom_call_target="tpu_custom_call" | custom-call | tf_op jit(solution)/shard_map/pallas_call | solution.py:435
  417.3 22.8 %fusion.222 = (f32[512]{0:T(512)S(1)}, f32[512,6400]{1,0:T(8,128)}) fusion(bf16[512,2048]{1,0:T(8,128)(2,1)} %shard_map.439, bf16[2048,6400]{1,0:T(8,128)(2,1)} %param.37), kind=kOutput, calls=%fused_computation.325 | convolution fusion | flops 13425049600 | bytes 41420800 | tf_op jit(solution)/shard_map/dot_general | solution.py:790
  452.5 17.3 %fusion.40 = (bf16[2048,512]{1,0:T(8,128)(2,1)S(1)}, f32[2048,512]{1,0:T(8,128)}) fusion(f32[512]{0:T(512)S(1)} %dynamic_slice.26, bf16[2048,2048]{1,0:T(8,128)(2,1)} %get-tuple-element.184, bf16[2048,512]{1,0:T(8,128)(2,1)} %get-tuple-element.100), kind=kOutput, calls=%fused_computation.56 | convolution fusion | flops 4364173312 | bytes 16779264 | tf_op jit(solution)/shard_map/dot_general | solution.py:741
  469.8 8.9 convolution_convert_fusion.1.part_ref
  480.1 86.7 %shard_map.437 = bf16[512,2048]{1,0:T(8,128)(2,1)} custom-call(bf16[2048,2048]{1,0:T(8,128)(2,1)} %convolution_convert_fusion.1.part_ref, bf16[512,2048]{1,0:T(8,128)(2,1)} %tokens_ref.5, f32[2,2048]{1,0:T(2,128)} %slice.208.rows_ref), custom_call_target="tpu_custom_call" | custom-call | tf_op jit(solution)/shard_map/pallas_call | solution.py:435
  566.9 23.2 %fusion.221 = (f32[512]{0:T(512)S(1)}, f32[512,6400]{1,0:T(8,128)}) fusion(bf16[512,2048]{1,0:T(8,128)(2,1)} %shard_map.437, bf16[2048,6400]{1,0:T(8,128)(2,1)} %param.37), kind=kOutput, calls=%fused_computation.324 | convolution fusion | flops 13425049600 | bytes 41420800 | tf_op jit(solution)/shard_map/dot_general | solution.py:790
  590.1 11.5 %fusion.20 = (f32[512]{0:T(512)S(1)}, f32[512]{0:T(512)S(1)}, f32[512]{0:T(512)S(1)}, f32[512]{0:T(512)S(1)}) fusion(f32[512,6400]{1,0:T(8,128)} %get-tuple-element.228, s32[6400]{0:T(1024)S(1)} %iota_add_fusion, s32[512]{0:T(512)S(1)} %copy-done.64, f32[512]{0:T(512)S(1)} %get-tuple-element.227, f32[512,6400]{1,0:T(8,128)} %get-tuple-element.224, ...), kind=kLoop, calls=%fused_computation.32 | loop fusion | flops 29489152 | bytes 26254336 | tf_op jit(solution)/shard_map/reduce_sum | solution.py:795
  628.2 21.2 %psum.28 = f32[]{:T(128)} all-reduce(f32[]{:T(128)} %get-tuple-element.169), channel_id=1, replica_groups=mesh['dp'=8,'tensor'=4] {'dp'}, use_global_device_ids=true, to_apply=%region_19.20 | all-reduce | flops 1 | bytes 8 | tf_op jit(solution)/shard_map/psum | solution.py:907
  650.1 20.7 %fusion.32.part_ref = f32[512,2048]{1,0:T(8,128)S(1)} fusion(bf16[2048,6400]{1,0:T(8,128)(2,1)} %param.37, f32[512,6400]{1,0:T(8,128)} %get-tuple-element.224, f32[512]{0:T(512)S(1)} %get-tuple-element.106, f32[512]{0:T(512)S(1)} %select_reduce_fusion.2, s32[6400]{0:T(1024)} %copy-done.45, s32[512]{0:T(512)} %param.34), kind=kOutput, calls=%fused_computation.46 | convolution fusion | flops 13441433600 | bytes 43547648 | tf_op jit(solution)/shard_map/dot_general | solution.py:714
  670.8 78.6 %shard_map.440 = (f32[128,2048]{1,0:T(8,128)S(1)}, bf16[2048,2048]{1,0:T(8,128)(2,1)}) custom-call(f32[512,2048]{1,0:T(8,128)S(1)} %fusion.32.part_ref), custom_call_target="tpu_custom_call" | custom-call | tf_op jit(solution)/shard_map/pallas_call | solution.py:526
  749.4 10.3 fusion.223
  773.8 27.9 %psum.30 = bf16[3584]{0:T(1024)(128)(2,1)S(1)} all-reduce(bf16[3584]{0:T(1024)(128)(2,1)S(1)} %pad_maximum_fusion.9), channel_id=1, replica_groups=mesh['dp'=8,'tensor'=4] {'dp'}, use_global_device_ids=true, to_apply=%region_35.36 | all-reduce | flops 3584 | bytes 14336 | tf_op jit(solution)/shard_map/psum | solution.py:958
  813.3 17.0 %fusion.198 = (bf16[2048]{0:T(1024)(128)(2,1)S(1)}, bf16[2048]{0:T(1024)(128)(2,1)S(1)}, bf16[2048,2048]{1,0:T(8,128)(2,1)}, bf16[2048]{0:T(1024)(128)(2,1)S(1)}, bf16[2048]{0:T(1024)(128)(2,1)S(1)}) fusion(f32[2048]{0:T(1024)S(1)} %copy-done.52, f32[2048]{0:T(1024)S(1)} %copy-done.47, bf16[2048,2048]{1,0:T(8,128)(2,1)} %get-tuple-element.97, ...), kind=kOutput, calls=%fused_computation.314 | convolution fusion | flops 4349485056 | bytes 37797888 | tf_op jit(solution)/shard_map/dot_general | solution.py:714
  830.5 37.5 %psum.29 = bf16[6,2048]{1,0:T(8,128)(2,1)S(1)} all-reduce(bf16[6,2048]{1,0:T(8,128)(2,1)S(1)} %stack.71), channel_id=1, replica_groups=mesh['dp'=8,'tensor'=4] {'dp','tensor'}, use_global_device_ids=true, to_apply=%region_31.32 | all-reduce | flops 12288 | bytes 49152 | tf_op jit(solution)/shard_map/psum | solution.py:957
  869.4 9.9 convolution_convert_fusion.2.low
  879.3 9.6 convolution_convert_fusion.3.up
  893.5 85.5 %shard_map.442 = (bf16[256,1536]{1,0:T(8,128)(2,1)S(1)}, bf16[256,2048]{1,0:T(8,128)(2,1)S(1)}, bf16[512,256]{1,0:T(8,128)(2,1)S(1)}, bf16[2048,256]{1,0:T(8,128)(2,1)S(1)}) custom-call(bf16[2048,384]{1,0:T(8,128)(2,1)S(1)} %convolution_convert_fusion.4.qkv, bf16[2048,512]{1,0:T(8,128)(2,1)} %convolution_convert_fusion.3.up, ...), custom_call_target="tpu_custom_call" | custom-call | tf_op jit(solution)/shard_map/pallas_call | solution.py:639
  985.7 42.5 %psum.31 = f32[]{:T(128)} all-reduce(f32[]{:T(128)S(6)} %add.442), channel_id=1, replica_groups=mesh['dp'=8,'tensor'=4] {'dp','tensor'}, use_global_device_ids=true, to_apply=%region_37.38 | all-reduce | flops 1 | bytes 8 | tf_op jit(solution)/shard_map/psum | solution.py:966
  1046.5 82.1 %shard_map.441 = bf16[512,2048]{1,0:T(8,128)(2,1)} custom-call(bf16[2048,2048]{1,0:T(8,128)(2,1)} %get-tuple-element.180.part_ref, bf16[512,2048]{1,0:T(8,128)(2,1)} %tokens_ref.5, f32[128,2048]{1,0:T(8,128)} %copy-done), custom_call_target="tpu_custom_call" | custom-call | tf_op jit(solution)/shard_map/pallas_call | solution.py:435
  (287 shorter events, 169.6 us)
Async XLA Ops:
  152.3 155.9 %copy-start.46 = (f32[2048]{0:T(1024)}, f32[2048]{0:T(1024)S(1)}, u32[]{:S(2)}) copy-start(f32[2048]{0:T(1024)S(1)} %broadcast_multiply_fusion) | copy-start | bytes 24580
  154.6 153.5 %copy-start.51 = (f32[2048]{0:T(1024)}, f32[2048]{0:T(1024)S(1)}, u32[]{:S(2)}) copy-start(f32[2048]{0:T(1024)S(1)} %add_rsqrt_fusion) | copy-start | bytes 24580
  260.3 13.1 %copy-start.23 = (bf16[2048,384]{1,0:T(8,128)(2,1)S(1)}, bf16[2048,384]{1,0:T(8,128)(2,1)}, u32[]{:S(2)}) copy-start(bf16[2048,384]{1,0:T(8,128)(2,1)} %get-tuple-element.98) | copy-start | bytes 4718596
  308.2 16.8 %copy-start.67 = (bf16[640,2048]{1,0:T(8,128)(2,1)S(1)}, bf16[640,2048]{1,0:T(8,128)(2,1)}, u32[]{:S(2)}) copy-start(bf16[640,2048]{1,0:T(8,128)(2,1)} %get-tuple-element.104) | copy-start | bytes 7864324
  417.3 23.0 %copy-start.28 = (pred[512,512]{0,1:T(8,128)(4,1)S(1)}, pred[512,512]{0,1:T(8,128)(4,1)}, u32[]{:S(2)}) copy-start(pred[512,512]{0,1:T(8,128)(4,1)} %copy-done.27) | copy-start | bytes 786436
  417.3 23.0 %copy-start.33 = (bf16[4,512,16]{1,2,0:T(8,128)(2,1)S(1)}, bf16[4,512,16]{1,2,0:T(8,128)(2,1)}, u32[]{:S(2)}) copy-start(bf16[4,512,16]{1,2,0:T(8,128)(2,1)} %get-tuple-element.209) | copy-start | bytes 196612
  417.3 23.0 %copy-start.35 = (bf16[4,512,16]{1,2,0:T(8,128)(2,1)S(1)}, bf16[4,512,16]{1,2,0:T(8,128)(2,1)}, u32[]{:S(2)}) copy-start(bf16[4,512,16]{1,2,0:T(8,128)(2,1)} %get-tuple-element.210) | copy-start | bytes 196612
  417.3 23.0 %copy-start.37 = (bf16[4,512,16]{1,2,0:T(8,128)(2,1)S(1)}, bf16[4,512,16]{1,2,0:T(8,128)(2,1)}, u32[]{:S(2)}) copy-start(bf16[4,512,16]{1,2,0:T(8,128)(2,1)} %get-tuple-element.213) | copy-start | bytes 196612
  417.3 23.0 %copy-start.39 = (bf16[4,512,16]{1,2,0:T(8,128)(2,1)S(1)}, bf16[4,512,16]{1,2,0:T(8,128)(2,1)}, u32[]{:S(2)}) copy-start(bf16[4,512,16]{1,2,0:T(8,128)(2,1)} %get-tuple-element.214) | copy-start | bytes 196612
  451.7 18.1 %copy-start.29 = (bf16[4,512,1,128]{3,1,0,2:T(8,128)(2,1)}, bf16[4,512,1,128]{3,1,0,2:T(8,128)(2,1)S(1)}, u32[]{:S(2)}) copy-start(bf16[4,512,1,128]{3,1,0,2:T(8,128)(2,1)S(1)} %copy.172) | copy-start | bytes 1572868
  452.5 17.3 %copy-start.66 = (bf16[640,2048]{1,0:T(8,128)(2,1)S(1)}, bf16[640,2048]{1,0:T(8,128)(2,1)}, u32[]{:S(2)}) copy-start(bf16[640,2048]{1,0:T(8,128)(2,1)} %get-tuple-element.101) | copy-start | bytes 7864324
  566.9 23.2 %copy-start.64 = (s32[512]{0:T(512)S(1)}, s32[512]{0:T(512)}, u32[]{:S(2)}) copy-start(s32[512]{0:T(512)} %param.34) | copy-start | bytes 6148
  590.1 32.6 %copy-start.59 = (s32[1,4]{1,0:T(1,128)S(1)}, s32[1,4]{1,0:T(1,128)}, u32[]{:S(2)}) copy-start(s32[1,4]{1,0:T(1,128)} %param.35) | copy-start | bytes 52
  590.1 59.9 %copy-start.65 = (s32[1,4]{1,0:T(1,128)S(1)}, s32[1,4]{1,0:T(1,128)}, u32[]{:S(2)}) copy-start(s32[1,4]{1,0:T(1,128)} %param.36) | copy-start | bytes 52
  773.4 31.3 %copy-start.24 = (bf16[2048,384]{1,0:T(8,128)(2,1)S(1)}, bf16[2048,384]{1,0:T(8,128)(2,1)}, u32[]{:S(2)}) copy-start(bf16[2048,384]{1,0:T(8,128)(2,1)} %get-tuple-element.98) | copy-start | bytes 4718596
  813.2 17.1 %copy-start.1 = (f32[128,2048]{1,0:T(8,128)S(1)}, f32[128,2048]{1,0:T(8,128)}, u32[]{:S(2)}) copy-start(f32[128,2048]{1,0:T(8,128)} %copy-done) | copy-start | bytes 3145732
  813.2 56.1 %copy-start.30 = (bf16[4,512,1,128]{3,1,0,2:T(8,128)(2,1)S(1)}, bf16[4,512,1,128]{3,1,0,2:T(8,128)(2,1)}, u32[]{:S(2)}) copy-start(bf16[4,512,1,128]{3,1,0,2:T(8,128)(2,1)} %copy-done.29) | copy-start | bytes 1572868
  869.4 19.5 %slice-start = ((s8[8388608]{0:T(1024)(128)(4,1)}), s8[4194304]{0:T(1024)(128)(4,1)S(1)}, s32[]{:S(2)}) async-start(s8[8388608]{0:T(1024)(128)(4,1)} %bitcast.200), calls=%async_computation | async-start | bytes 8388608
  893.5 135.4 %copy-start.57 = (f32[3584]{0:T(1024)S(1)}, f32[3584]{0:T(1024)}, u32[]{:S(2)}) copy-start(f32[3584]{0:T(1024)} %param.43) | copy-start | bytes 43012
  893.5 135.4 %copy-start.60 = (f32[3584]{0:T(1024)S(1)}, f32[3584]{0:T(1024)}, u32[]{:S(2)}) copy-start(f32[3584]{0:T(1024)} %param.55) | copy-start | bytes 43012
  893.5 135.4 %copy-start.61 = (f32[3584]{0:T(1024)S(1)}, f32[3584]{0:T(1024)}, u32[]{:S(2)}) copy-start(f32[3584]{0:T(1024)} %param.49) | copy-start | bytes 43012
  893.5 136.1 %copy-start.42 = (f32[6,2048]{1,0:T(8,128)S(1)}, f32[6,2048]{1,0:T(8,128)}, u32[]{:S(2)}) copy-start(f32[6,2048]{1,0:T(8,128)} %param.42) | copy-start | bytes 147460
  893.5 136.0 %copy-start.48 = (f32[6,2048]{1,0:T(8,128)S(1)}, f32[6,2048]{1,0:T(8,128)}, u32[]{:S(2)}) copy-start(f32[6,2048]{1,0:T(8,128)} %param.54) | copy-start | bytes 147460
  893.5 136.0 %copy-start.49 = (f32[6,2048]{1,0:T(8,128)S(1)}, f32[6,2048]{1,0:T(8,128)}, u32[]{:S(2)}) copy-start(f32[6,2048]{1,0:T(8,128)} %param.48) | copy-start | bytes 147460
  (47 other events, 262.4 us)

commit v2 on v1

--- a/solution.py
+++ b/solution.py
@@ -13,6 +13,7 @@
 STEP = 3
 SPLIT = 4
 QUARTERS = 4
+AHEAD = 3
 
 
 EPS_NORM = 1e-05
@@ -144,15 +145,22 @@
                 )
             )
     first = {}
-    for m in range(4):
-        for s in range(1, SPLIT):
-            first[m, s] = remote(
-                src(m, (here.o + s) % SPLIT),
-                dst(m, here.dp),
-                send_o.at[m, s - 1],
-                recv_o.at[m, s - 1],
-                here.outer_peer(s),
-            )
+    order = [(m, s) for m in range(4) for s in (2, 1, 3)]
+
+    def send_on(number):
+        if number >= len(order):
+            return
+        m, s = order[number]
+        first[m, s] = remote(
+            src(m, (here.o + s) % SPLIT),
+            dst(m, here.dp),
+            send_o.at[m, s - 1],
+            recv_o.at[m, s - 1],
+            here.outer_peer(s),
+        )
+
+    for number in range(0 if with_tokens else AHEAD):
+        send_on(number)
     own = []
     for m in range(4):
         own.append(pltpu.make_async_copy(src(m, here.o), dst(m, here.dp), local.at[m]))
@@ -181,6 +189,7 @@
     if with_tokens:
         for s in range(1, SPLIT):
             token_copies[s - 1].wait_recv()
+            send_on(s - 1)
             part = (here.o + SPLIT - s) % SPLIT
             across[s] = remote(
                 piece(part, here.t),
@@ -198,20 +207,20 @@
                     here.near_peer(),
                 )
             )
-    for m in range(4):
-        for s in range(1, SPLIT):
-            first[m, s].wait_recv()
-            index = ((here.o + SPLIT - s) % SPLIT) * inner + here.i
-            for r in range(1, inner):
-                waits.append(
-                    remote(
-                        dst(m, index),
-                        dst(m, index),
-                        send_i.at[m, s, r - 1],
-                        recv_i.at[m, s, r - 1],
-                        here.inner_peer(r),
-                    )
+    for number, (m, s) in enumerate(order):
+        first[m, s].wait_recv()
+        send_on(number + AHEAD)
+        index = ((here.o + SPLIT - s) % SPLIT) * inner + here.i
+        for r in range(1, inner):
+            waits.append(
+                remote(
+                    dst(m, index),
+                    dst(m, index),
+                    send_i.at[m, s, r - 1],
+                    recv_i.at[m, s, r - 1],
+                    here.inner_peer(r),
                 )
+            )
     if with_tokens:
         for s in range(1, SPLIT):
             across[s].wait_recv()
@@ -287,63 +296,78 @@
     return value.astype(F32)
 
 
-def reduce_rows(here, part_ref, near_in, far_in, far_out, outer_in, outer_out, sems, last):
-    rows = far_out.shape[1]
-    near_send, near_recv, far_send, far_recv, outer_send, outer_recv = sems
-
-    def rows_of(step, quarter):
-        block = (here.o + 1 + step) % SPLIT
-        return pl.ds((block * QUARTERS + quarter) * rows, rows)
-
-    near = {}
-    for step in range(SPLIT):
-        for side, quarter in enumerate(((here.near + 2) % QUARTERS, here.near)):
-            near[step, side] = remote(
-                part_ref.at[rows_of(step, quarter), :],
-                near_in.at[step, side],
-                near_send.at[step, side],
-                near_recv.at[step, side],
-                here.near_peer(),
-            )
-    far = []
-    for step in range(SPLIT):
-        near[step, 0].wait_recv()
-        far_out[step] = (f32(part_ref[rows_of(step, here.far), :]) + f32(near_in[step, 0])).astype(
-            BF16
-        )
-        far.append(
-            remote(
-                far_out.at[step],
-                far_in.at[step],
-                far_send.at[step],
-                far_recv.at[step],
-                here.far_peer(),
-            )
-        )
-    outer = []
-    for step in range(SPLIT):
-        near[step, 1].wait_recv()
-        far[step].wait_recv()
-        total = (
-            f32(part_ref[rows_of(step, here.t), :]) + f32(near_in[step, 1]) + f32(far_in[step])
-        )
-        if step < SPLIT - 1:
-            outer_out[step] = total.astype(BF16)
-            outer.append(
-                remote(
-                    outer_out.at[step],
-                    outer_in.at[step],
-                    outer_send.at[step],
-                    outer_recv.at[step],
-                    here.outer_peer(step + 1),
+class RowSum:
+    def __init__(self, here, part_ref, total, near_in, far_in, far_out, outer_in, outer_out, *sems):
+        self.here, self.part, self.total = here, part_ref, total
+        self.near_in, self.far_in, self.far_out = near_in, far_in, far_out
+        self.outer_in, self.outer_out = outer_in, outer_out
+        self.near_sems, self.far_sems, self.outer_sems = sems[0:2], sems[2:4], sems[4:6]
+        self.quarter_sems = sems[6:8]
+        self.rows = far_out.shape[1]
+        self.near, self.far, self.outer = {}, {}, {}
+
+    def rows_of(self, step, quarter):
+        block = (self.here.o + 1 + step) % SPLIT
+        return pl.ds((block * QUARTERS + quarter) * self.rows, self.rows)
+
+    def start(self):
+        here = self.here
+        for step in range(SPLIT):
+            for side, quarter in enumerate(((here.near + 2) % QUARTERS, here.near)):
+                self.near[step, side] = remote(
+                    self.part.at[self.rows_of(step, quarter), :],
+                    self.near_in.at[step, side],
+                    self.near_sems[0].at[step, side],
+                    self.near_sems[1].at[step, side],
+                    here.near_peer(),
                 )
-            )
-        else:
-            last(total)
-    for copy in outer:
-        copy.wait_recv()
-    for copy in list(near.values()) + far + outer:
-        copy.wait_send()
+
+    def across(self, step):
+        here = self.here
+        self.near[step, 0].wait_recv()
+        self.far_out[step] = (
+            f32(self.part[self.rows_of(step, here.far), :]) + f32(self.near_in[step, 0])
+        ).astype(BF16)
+        self.far[step] = remote(
+            self.far_out.at[step],
+            self.far_in.at[step],
+            self.far_sems[0].at[step],
+            self.far_sems[1].at[step],
+            here.far_peer(),
+        )
+
+    def along(self, step):
+        here = self.here
+        self.near[step, 1].wait_recv()
+        self.far[step].wait_recv()
+        value = (
+            f32(self.part[self.rows_of(step, here.t), :])
+            + f32(self.near_in[step, 1])
+            + f32(self.far_in[step])
+        )
+        if step == SPLIT - 1:
+            self.total[...] = value
+            return
+        self.outer_out[step] = value.astype(BF16)
+        self.outer[step] = remote(
+            self.outer_out.at[step],
+            self.outer_in.at[step],
+            self.outer_sems[0].at[step],
+            self.outer_sems[1].at[step],
+            here.outer_peer(step + 1),
+        )
+
+    def value(self):
+        value = self.total[...]
+        for step in range(SPLIT - 1):
+            self.outer[step].wait_recv()
+            value = value + f32(self.outer_in[step])
+        return value
+
+    def finish(self):
+        for copies in (self.near, self.far, self.outer):
+            for copy in copies.values():
+                copy.wait_send()
 
 
 def gather_quarters(here, ref, rows, send, recv):
@@ -364,50 +388,29 @@
     return [here.outer_peer(s) for s in range(1, SPLIT)] + [here.far_peer(), here.near_peer()]
 
 
-def branch_kernel(inner, part_ref, tokens_ref, rows_ref, final_ref, total, *scratch):
+def branch_kernel(inner, part_ref, tokens_ref, rows_ref, final_ref, *scratch):
     here = Place(inner)
-    buffers, sems, (send, recv) = scratch[:5], scratch[5:11], scratch[11:]
-    rows = total.shape[0]
+    sums = RowSum(here, part_ref, *scratch)
     greet(reduce_peers(here))
-    mine = pl.ds(here.t * rows, rows)
-
-    def last(value):
-        total[...] = value
-
-    reduce_rows(here, part_ref, *buffers, sems, last)
-    outer_in = buffers[3]
-    branch = total[...]
-    for step in range(SPLIT - 1):
-        branch = branch + f32(outer_in[step])
-    branch = branch + rows_ref[0:1, :] + rows_ref[1:2, :]
+    mine = pl.ds(here.t * sums.rows, sums.rows)
+    sums.start()
+    for step in range(SPLIT):
+        sums.across(step)
+    for step in range(SPLIT):
+        sums.along(step)
+    branch = sums.value() + rows_ref[0:1, :] + rows_ref[1:2, :]
     final_ref[mine, :] = (f32(tokens_ref[mine, :]) + branch).astype(BF16)
-    gather_quarters(here, final_ref, rows, send, recv)
-
-
-def input_kernel(inner, part_ref, tokens_ref, final_grad_ref, grad_ref, total, *scratch):
-    here = Place(inner)
-    buffers, sems, (send, recv) = scratch[:5], scratch[5:11], scratch[11:]
-    rows = total.shape[0]
-    greet(reduce_peers(here))
-    mine = pl.ds(here.t * rows, rows)
-
-    def last(value):
-        total[...] = value
-
-    reduce_rows(here, part_ref, *buffers, sems, last)
-    outer_in = buffers[3]
-    scaled = total[...]
-    for step in range(SPLIT - 1):
-        scaled = scaled + f32(outer_in[step])
-    values = f32(tokens_ref[mine, :])
+    gather_quarters(here, final_ref, sums.rows, *sums.quarter_sems)
+    sums.finish()
+
+
+def input_change(values, scaled):
     centre = values - jnp.mean(values, axis=1, keepdims=True)
     spread = jnp.mean(centre * centre, axis=1, keepdims=True)
     scale = lax.rsqrt(spread + EPS_NORM)
     normed = centre * scale
     along = jnp.mean(scaled * normed, axis=1, keepdims=True)
-    change = scale * (scaled - jnp.mean(scaled, axis=1, keepdims=True) - normed * along)
-    grad_ref[mine, :] = (final_grad_ref[...] + change).astype(BF16)
-    gather_quarters(here, grad_ref, rows, send, recv)
+    return scale * (scaled - jnp.mean(scaled, axis=1, keepdims=True) - normed * along)
 
 
 def reduce_scratch(rows, width):
@@ -430,10 +433,10 @@
     ]
 
 
-def reduce_call(body, inner, part, tokens, extra, number):
+def branch_call(inner, part, tokens, extra, number):
     block, width = tokens.shape
     return pl.pallas_call(
-        functools.partial(body, inner),
+        functools.partial(branch_kernel, inner),
         out_shape=jax.ShapeDtypeStruct((block, width), BF16),
         in_specs=[VMEM_SPEC] * 3,
         out_specs=VMEM_SPEC,
@@ -551,13 +554,101 @@
     )(part)
 
 
-def weight_grads_kernel(inner, qkv, up, low, *refs):
+class AllSum:
+    def __init__(self, here, mine, near_in, far_in, outer, inner, send, recv):
+        self.here, self.mine, self.near_in, self.far_in = here, mine, near_in, far_in
+        self.outer, self.inner, self.send, self.recv = outer, inner, send, recv
+        self.copies = []
+
+    def pair(self, stage, target, peer):
+        copy = remote(
+            self.mine.at[stage], target, self.send.at[stage], self.recv.at[stage], peer
+        )
+        self.copies.append(copy)
+        return copy
+
+    def near(self, value):
+        self.mine[0] = value
+        self.waiting = [self.pair(0, self.near_in, self.here.near_peer())]
+
+    def far(self):
+        self.waiting[0].wait_recv()
+        self.mine[1] = self.mine[0] + self.near_in[...]
+        self.waiting = [self.pair(1, self.far_in, self.here.far_peer())]
+
+    def group(self, buffer, index, first, peers):
+        self.waiting = []
+        for number, peer in enumerate(peers):
+            copy = remote(
+                buffer.at[index],
+                buffer.at[index],
+                self.send.at[first + number],
+                self.recv.at[first + number],
+                peer,
+            )
+            self.waiting.append(copy)
+            self.copies.append(copy)
+
+    def along_outer(self):
+        self.waiting[0].wait_recv()
+        here = self.here
+        self.outer[here.o] = self.mine[1] + self.far_in[...]
+        self.group(self.outer, here.o, 2, [here.outer_peer(s) for s in range(1, SPLIT)])
+
+    def along_inner(self):
+        here = self.here
+        for copy in self.waiting:
+            copy.wait_recv()
+        value = self.outer[0]
+        for part in range(1, SPLIT):
+            value = value + self.outer[part]
+        self.inner[here.i] = value
+        peers = [here.inner_peer(r) for r in range(1, here.inner)]
+        self.group(self.inner, here.i, 1 + SPLIT, peers)
+
+    def value(self):
+        for copy in self.waiting:
+            copy.wait_recv()
+        value = self.inner[0]
+        for part in range(1, self.here.inner):
+            value = value + self.inner[part]
+        for copy in self.copies:
+            copy.wait_send()
+        return value
+
+
+def all_sum_scratch(shape, inner):
+    dma = pltpu.SemaphoreType.DMA
+    return [
+        pltpu.VMEM((2, *shape), F32),
+        pltpu.VMEM(shape, F32),
+        pltpu.VMEM(shape, F32),
+        pltpu.VMEM((SPLIT, *shape), F32),
+        pltpu.VMEM((inner, *shape), F32),
+        dma((SPLIT + inner,)),
+        dma((SPLIT + inner,)),
+    ]
+
+
+def whole_sum(value):
+    return jnp.sum(jnp.sum(value, axis=1, keepdims=True), axis=0, keepdims=True)
+
+
+def finish_kernel(
+    inner, part_ref, tokens_ref, quarter_ref, qkv, up, low, rows_ref, bias_ref,
+    grad_ref, qkv_out, up_out, out_out, down_out, rows_out, bias_out, norm_ref, *scratch,
+):
     here = Place(inner)
-    outs, inputs, sends = refs[:4], refs[4:8], refs[8:12]
-    send_i, recv_i, send_o, recv_o, local = refs[12:]
-    shard = outs[0].shape[0]
-    width_out = outs[2].shape[0] // SPLIT
-    width_down = outs[3].shape[0] // SPLIT
+    sums = RowSum(here, part_ref, *scratch[:14])
+    inputs, sends = scratch[14:18], scratch[18:22]
+    send_i, recv_i, send_o, recv_o, local = scratch[22:27]
+    small = AllSum(here, *scratch[27:34])
+    squares = AllSum(here, *scratch[34:41])
+    bias_in, bias_send, bias_recv = scratch[41:44]
+    outs = (qkv_out, up_out, out_out, down_out)
+    shard = qkv_out.shape[0]
+    width_out = out_out.shape[0] // SPLIT
+    width_down = down_out.shape[0] // SPLIT
 
     def src(m, index):
         where = pl.ds(index * shard, shard)
@@ -575,45 +666,122 @@
         width = outs[m].shape[0] // SPLIT
         return outs[m].at[pl.ds(here.o * width, width), :]
 
-    peers = [here.outer_peer(s) for s in range(1, SPLIT)]
-    peers += [here.inner_peer(r) for r in range(1, inner)]
+    peers = reduce_peers(here) + [here.inner_peer(r) for r in range(1, inner)]
     greet(peers)
-    order = (2, 3, 1, 0)
-    first = {}
-    for m in order:
-        for s in range(SPLIT):
-            part = (here.o + s) % SPLIT
-            for r in range(1, inner):
-                first[m, s, r] = remote(
-                    src(m, part * inner + (here.i + r) % inner),
-                    inputs[m].at[s, r - 1],
-                    send_i.at[m, s, r - 1],
-                    recv_i.at[m, s, r - 1],
-                    here.inner_peer(r),
+    first, last, own = {}, [], []
+
+    order = [(m, s) for m in (2, 3, 1, 0) for s in (2, 1, 3, 0)]
+
+    def trade(number):
+        if number >= len(order):
+            return
+        m, s = order[number]
+        part = (here.o + s) % SPLIT
+        for r in range(1, inner):
+            first[m, s, r] = remote(
+                src(m, part * inner + (here.i + r) % inner),
+                inputs[m].at[s, r - 1],
+                send_i.at[m, s, r - 1],
+                recv_i.at[m, s, r - 1],
+                here.inner_peer(r),
+            )
+
+    def settle(number):
+        m, s = order[number]
+        part = (here.o + s) % SPLIT
+        total = f32(src(m, part * inner + here.i)[...])
+        for r in range(1, inner):
+            first[m, s, r].wait_recv()
+        trade(number + AHEAD)
+        for r in range(1, inner):
+            total = total + f32(inputs[m][s, r - 1])
+        sends[m][s] = total.astype(BF16)
+        if s:
+            last.append(
+                remote(
+                    sends[m].at[s],
+                    dst(m),
+                    send_o.at[m, s - 1],
+                    recv_o.at[m, s - 1],
+                    here.outer_peer(s),
                 )
-    last, own = [], []
-    for m in order:
-        for s in range(SPLIT):
-            part = (here.o + s) % SPLIT
-            total = f32(src(m, part * inner + here.i)[...])
-            for r in range(1, inner):
-                first[m, s, r].wait_recv()
-                total = total + f32(inputs[m][s, r - 1])
-            sends[m][s] = total.astype(BF16)
-            if s:
-                last.append(
-                    remote(
-                        sends[m].at[s],
-                        dst(m),
-                        send_o.at[m, s - 1],
-                        recv_o.at[m, s - 1],
-                        here.outer_peer(s),
-                    )
-                )
-            else:
-                copy = pltpu.make_async_copy(sends[m].at[0], dst(m), local.at[m])
-                copy.start()
-                own.append(copy)
+            )
+        else:
+            copy = pltpu.make_async_copy(sends[m].at[0], dst(m), local.at[m])
+            copy.start()
+            own.append(copy)
+        return whole_sum(total * total)
+
+    for number in range(AHEAD):
+        trade(number)
+    sums.start()
+    small.near(rows_ref[...])
+    bias_in[here.i] = bias_ref[...]
+    bias_inner = [
+        remote(
+            bias_in.at[here.i],
+            bias_in.at[here.i],
+            bias_send.at[SPLIT + r],
+            bias_recv.at[SPLIT + r],
+            here.inner_peer(r),
+        )
+        for r in range(1, inner)
+    ]
+    square = settle(0)
+    square = square + settle(1)
+    for step in range(SPLIT):
+        sums.across(step)
+        square = square + settle(2 + step)
+    small.far()
+    sums.along(0)
+    square = square + settle(6)
+    square = square + settle(7)
+    small.along_outer()
+    for copy in bias_inner:
+        copy.wait_recv()
+    bias = bias_in[0]
+    for part in range(1, inner):
+        bias = bias + bias_in[part]
+    bias_out[here.o] = bias
+    bias_outer = [
+        remote(
+            bias_out.at[here.o],
+            bias_out.at[here.o],
+            bias_send.at[s],
+            bias_recv.at[s],
+            here.outer_peer(s),
+        )
+        for s in range(1, SPLIT)
+    ]
+    square = square + whole_sum(bias * bias) / inner
+    sums.along(1)
+    square = square + settle(8)
+    square = square + settle(9)
+    small.along_inner()
+    sums.along(2)
+    square = square + settle(10)
+    square = square + settle(11)
+    rows_out[...] = small.value()
+    sums.along(3)
+    for number in range(12, len(order)):
+        square = square + settle(number)
+    squares.near(jnp.broadcast_to(square, norm_ref.shape))
+    squares.far()
+    squares.along_outer()
+    squares.along_inner()
+    norm = squares.value()
+    rows = rows_out[...]
+    doubled = lax.broadcasted_iota(jnp.int32, rows.shape, 0) == 4
+    norm_ref[...] = norm + whole_sum(rows * rows * jnp.where(doubled, 2.0, 1.0))
+    mine = pl.ds(here.t * sums.rows, sums.rows)
+    change = input_change(f32(tokens_ref[mine, :]), sums.value())
+    grad_ref[mine, :] = (quarter_ref[...] + change).astype(BF16)
+    gather_quarters(here, grad_ref, sums.rows, *sums.quarter_sems)
+    sums.finish()
+    for copy in bias_outer:
+        copy.wait_recv()
+    for copy in bias_inner + bias_outer:
+        copy.wait_send()
     for copy in last:
         copy.wait()
     for copy in own:
@@ -622,7 +790,7 @@
         copy.wait_send()
 
 
-def weight_grads_call(grads, shards, inner, number):
+def finish_call(part, tokens, quarter, grads, rows, bias, shards, inner, number):
     dma = pltpu.SemaphoreType.DMA
     qkv, out, up, down = shards
     ordered = (qkv, up, out, down)
@@ -636,12 +804,21 @@
         (down[0] // SPLIT, down[1]),
     ]
     peers = max(inner - 1, 1)
+    block, width = tokens.shape
+    tile = (8, 128)
     return pl.pallas_call(
-        functools.partial(weight_grads_kernel, inner),
-        out_shape=[jax.ShapeDtypeStruct(shape, BF16) for shape in ordered],
-        in_specs=[VMEM_SPEC] * 3,
-        out_specs=[ANY_SPEC] * 4,
-        scratch_shapes=[pltpu.VMEM((SPLIT, peers, *piece), BF16) for piece in pieces]
+        functools.partial(finish_kernel, inner),
+        out_shape=[
+            jax.ShapeDtypeStruct((block, width), BF16),
+            *(jax.ShapeDtypeStruct(shape, BF16) for shape in ordered),
+            jax.ShapeDtypeStruct(rows.shape, F32),
+            jax.ShapeDtypeStruct((SPLIT, *bias.shape), F32),
+            jax.ShapeDtypeStruct(tile, F32),
+        ],
+        in_specs=[VMEM_SPEC] * 8,
+        out_specs=[VMEM_SPEC] + [ANY_SPEC] * 4 + [VMEM_SPEC] * 3,
+        scratch_shapes=reduce_scratch(block // QUARTERS, width)
+        + [pltpu.VMEM((SPLIT, peers, *piece), BF16) for piece in pieces]
         + [pltpu.VMEM((SPLIT, *piece), BF16) for piece in pieces]
         + [
             dma((4, SPLIT, peers)),
@@ -649,19 +826,96 @@
             dma((4, SPLIT - 1)),
             dma((4, SPLIT - 1)),
             dma((4,)),
+        ]
+        + all_sum_scratch(rows.shape, inner)
+        + all_sum_scratch(tile, inner)
+        + [
+            pltpu.VMEM((inner, *bias.shape), F32),
+            dma((SPLIT + inner,)),
+            dma((SPLIT + inner,)),
         ],
         compiler_params=pltpu.CompilerParams(
-            collective_id=number, has_side_effects=True, vmem_limit_bytes=48 * 1024 * 1024
+            collective_id=number, has_side_effects=True, vmem_limit_bytes=60 * 1024 * 1024
         ),
-    )(*grads)
-
-
-def combined_all(value, axis, join):
-    pieces = jax.tree.map(lambda part: lax.all_gather(part, axis), value)
-    head = jax.tree.map(lambda part: part[0], pieces)
-    tail = jax.tree.map(lambda part: part[1:], pieces)
-    total, _ = lax.scan(lambda total, section: (join(total, section), None), head, tail)
-    return total
+    )(part, tokens, quarter, *grads, rows, bias)
+
+
+def reward_kernel(
+    inner, stats_ref, member_ref, label_ref, out_ref, stats, outer_in, inner_in,
+    send, recv, send_o, recv_o, send_i, recv_i,
+):
+    here = Place(inner)
+    tensor_peers = [(here.dp, (here.t + s) % QUARTERS) for s in range(1, QUARTERS)]
+    outer_peers = [here.outer_peer(s) for s in range(1, SPLIT)]
+    inner_peers = [here.inner_peer(r) for r in range(1, inner)]
+    greet(tensor_peers + outer_peers + inner_peers)
+
+    def share(buffer, index, sends, recvs, peers):
+        return [
+            remote(buffer.at[index], buffer.at[index], sends.at[n], recvs.at[n], peer)
+            for n, peer in enumerate(peers)
+        ]
+
+    stats[here.t] = stats_ref[...]
+    copies = share(stats, here.t, send, recv, tensor_peers)
+    for copy in copies:
+        copy.wait_recv()
+    quarters = [stats[q] for q in range(QUARTERS)]
+    highest = functools.reduce(jnp.maximum, quarters)
+    summed = functools.reduce(lambda a, b: a + b, [jnp.exp(q - highest) for q in quarters])
+    totals = highest + jnp.log(summed)
+    picks = functools.reduce(lambda a, b: a + b, quarters)
+    log_probs = picks - totals_to_picks(totals)
+    member = member_ref[...]
+    policy_docs = jnp.sum(member * log_probs[1:2, :], axis=1, keepdims=True)
+    frozen_docs = jnp.sum(member * log_probs[3:4, :], axis=1, keepdims=True)
+    reward = policy_docs - frozen_docs
+    outer_in[here.o] = jnp.broadcast_to(whole_sum(reward), outer_in.shape[1:])
+    more = share(outer_in, here.o, send_o, recv_o, outer_peers)
+    for copy in more:
+        copy.wait_recv()
+    inner_in[here.i] = functools.reduce(lambda a, b: a + b, [outer_in[n] for n in range(SPLIT)])
+    rest = share(inner_in, here.i, send_i, recv_i, inner_peers)
+    for copy in rest:
+        copy.wait_recv()
+    total = functools.reduce(lambda a, b: a + b, [inner_in[n] for n in range(inner)])
+    seq_count = inner * SPLIT * SEGS
+    shift = total[:, 0:1] / seq_count
+    sigmoid_value = 1.0 / (1.0 + jnp.exp(-BETA_KTO * (reward - shift)))
+    labels = label_ref[:, 0:1]
+    doc_grad = BETA_KTO * sigmoid_value * (1.0 - sigmoid_value) * (1.0 - 2.0 * labels) / seq_count
+    out_ref[0:1, :] = jnp.sum(member * doc_grad, axis=0, keepdims=True)
+    out_ref[1:2, :] = totals[0:1, :]
+    for copy in copies + more + rest:
+        copy.wait_send()
+
+
+def totals_to_picks(totals):
+    return jnp.concatenate([totals[0:1], totals[0:1], totals[2:3], totals[2:3], totals[4:]], axis=0)
+
+
+def reward_call(stats, member, labels, inner, number):
+    dma = pltpu.SemaphoreType.DMA
+    tile = (8, 128)
+    peers = max(inner - 1, 1)
+    return pl.pallas_call(
+        functools.partial(reward_kernel, inner),
+        out_shape=jax.ShapeDtypeStruct((2, stats.shape[1]), F32),
+        in_specs=[VMEM_SPEC] * 3,
+        out_specs=VMEM_SPEC,
+        scratch_shapes=[
+            pltpu.VMEM((QUARTERS, *stats.shape), F32),
+            pltpu.VMEM((SPLIT, *tile), F32),
+            pltpu.VMEM((inner, *tile), F32),
+            dma((QUARTERS - 1,)),
+            dma((QUARTERS - 1,)),
+            dma((SPLIT - 1,)),
+            dma((SPLIT - 1,)),
+            dma((peers,)),
+            dma((peers,)),
+        ],
+        compiler_params=pltpu.CompilerParams(collective_id=number, has_side_effects=True),
+    )(stats, member, labels)
 
 
 def rotate(values, positions, direction):
@@ -794,15 +1048,6 @@
     chosen = column == targets[:, None]
     picked = jnp.sum(jnp.where(chosen, logits, 0.0), axis=1)
     return (logits, log_total, picked, chosen)
-
-
-def combine_totals(first_set, second_set):
-    return (
-        jnp.logaddexp(first_set[0], second_set[0]),
-        first_set[1] + second_set[1],
-        jnp.logaddexp(first_set[2], second_set[2]),
-        first_set[3] + second_set[3],
-    )
 
 
 def adam_step(master, mean_old, square_old, gradient, factor, rate, decay_rate):
@@ -881,7 +1126,7 @@
     policy_part, kept_values = attention_mlp(
         one_low, two_low, *own_bias(hidden_bias), policy_set, positions, allowed
     )
-    final_low = reduce_call(branch_kernel, inner, policy_part, inputs, vectors[4:6], 2)
+    final_low = branch_call(inner, policy_part, inputs, vectors[4:6], 2)
     frozen_part, _ = attention_mlp(
         normed_rows(normed, vectors_frozen[0], vectors_frozen[1]),
         normed_rows(normed, vectors_frozen[2], vectors_frozen[3]),
@@ -890,25 +1135,19 @@
         positions,
         allowed,
     )
-    frozen_low = reduce_call(branch_kernel, inner, frozen_part, inputs, vectors_frozen[4:6], 3)
+    frozen_low = branch_call(inner, frozen_part, inputs, vectors_frozen[4:6], 3)
     vocab_start = lax.axis_index("tensor") * head_weight.shape[1]
     policy_logits, policy_total, policy_pick, chosen = vocab_stats(
         final_low, head_weight, targets, vocab_start
     )
     _, frozen_total, frozen_pick, _ = vocab_stats(frozen_low, head_weight, targets, vocab_start)
-    policy_total, policy_pick, frozen_total, frozen_pick = combined_all(
-        (policy_total, policy_pick, frozen_total, frozen_pick), "tensor", combine_totals
-    )
-    doc_weights = member.astype(F32)
-    policy_docs = jnp.sum(doc_weights * (policy_pick - policy_total)[:, None], axis=0)
-    frozen_docs = jnp.sum(doc_weights * (frozen_pick - frozen_total)[:, None], axis=0)
-    reward = policy_docs - frozen_docs
-    seq_count = dp_size * SEGS
-    reward_shift = lax.psum(jnp.sum(reward), "dp") / seq_count
-    sigmoid_value = jax.nn.sigmoid(BETA_KTO * (reward - reward_shift))
-    labels = desirable[0].astype(F32)
-    doc_grad = BETA_KTO * sigmoid_value * (1.0 - sigmoid_value) * (1.0 - 2.0 * labels) / seq_count
-    token_grad = jnp.sum(doc_weights * doc_grad[None, :], axis=1)
+    none = jnp.zeros_like(policy_total)
+    stats = jnp.stack(
+        [policy_total, policy_pick, frozen_total, frozen_pick, none, none, none, none]
+    )
+    doc_rows = jnp.zeros((8, block), F32).at[:SEGS].set(f32(member).T)
+    labels = jnp.zeros((8, 128), F32).at[:SEGS].set(f32(desirable[0])[:, None])
+    token_grad, policy_total = reward_call(stats, doc_rows, labels, inner, 6)
     logit_grad = (
         token_grad[:, None]
         * (chosen.astype(F32) - jnp.exp(policy_logits - policy_total[:, None]))
@@ -920,50 +1159,44 @@
         branch_low, kept_values, policy_set, positions, allowed
     )
     scaled_part = (one_part * vectors[0] + two_part * vectors[2]).astype(BF16)
-    input_grad = f32(reduce_call(input_kernel, inner, scaled_part, inputs, final_quarter, 5))
     shards = tuple(w.shape for w in masters)
     grads = (
         contract_rows(one_low, mixed_grad).astype(BF16),
         contract_rows(two_low, hidden_low).astype(BF16),
         contract_rows(joined, branch_low).astype(BF16),
     )
-    qkv_grad, up_grad, out_grad, down_grad = weight_grads_call(grads, shards, inner, 6)
-    branch_bias = jnp.sum(f32(final_quarter.astype(BF16)), axis=0)
-    vector_grad = jnp.stack(
+    none = jnp.zeros_like(vectors[0])
+    vector_part = jnp.stack(
         [
             jnp.sum(one_part * normed, axis=0),
             jnp.sum(one_part, axis=0),
             jnp.sum(two_part * normed, axis=0),
             jnp.sum(two_part, axis=0),
-            branch_bias,
-            branch_bias,
+            jnp.sum(f32(final_quarter.astype(BF16)), axis=0),
+            none,
+            none,
+            none,
         ]
     )
-    bias_grad = jnp.concatenate(
-        [
-            lax.dynamic_update_slice(
-                jnp.zeros((cut,), F32),
-                jnp.sum(mixed_grad, axis=0, dtype=F32),
-                (outer_index * width_qkv,),
-            ),
-            lax.dynamic_update_slice(
-                jnp.zeros((up_master.shape[1],), F32),
-                jnp.sum(hidden_low, axis=0, dtype=F32),
-                (outer_index * width_up,),
-            ),
-        ]
-    )
-    vector_grad, hidden_grad = (
-        f32(lax.psum(vector_grad.astype(BF16), ("dp", "tensor"))),
-        f32(lax.psum(bias_grad.astype(BF16), "dp")),
-    )
-    local_square = sum(jnp.sum(f32(g) * f32(g)) for g in (qkv_grad, out_grad, up_grad, down_grad))
-    local_square = (
-        local_square
-        + jnp.sum(vector_grad * vector_grad) / (dp_size * tensor_size)
-        + jnp.sum(hidden_grad * hidden_grad) / dp_size
-    )
-    grad_norm = jnp.sqrt(lax.psum(local_square, ("dp", "tensor")))
+    bias_part = jnp.concatenate(
+        [jnp.sum(mixed_grad, axis=0, dtype=F32), jnp.sum(hidden_low, axis=0, dtype=F32)]
+    )
+    bias_rows = (width_qkv + width_up) // 128
+    bias_tile = (
+        jnp.zeros((-(-bias_rows // 8) * 8, 128), F32)
+        .at[:bias_rows]
+        .set(bias_part.reshape(bias_rows, 128))
+    )
+    input_grad, qkv_grad, up_grad, out_grad, down_grad, vector_sum, bias_sum, square = finish_call(
+        scaled_part, inputs, final_quarter, grads, vector_part, bias_tile, shards, inner, 5
+    )
+    input_grad = f32(input_grad)
+    vector_grad = jnp.concatenate([vector_sum[:5], vector_sum[4:5]], axis=0)
+    bias_sum = bias_sum[:, :bias_rows].reshape(SPLIT, bias_rows * 128)
+    hidden_grad = jnp.concatenate(
+        [bias_sum[:, :width_qkv].reshape(-1), bias_sum[:, width_qkv:].reshape(-1)]
+    )
+    grad_norm = jnp.sqrt(square[0, 0])
     factor = jnp.minimum(1.0, CLIP_NORM / (grad_norm + 1e-06))
     qkv_state = adam_step(
         qkv_master, qkv_mean, qkv_square, qkv_grad, factor, LEARN_RATE, WEIGHT_DECAY

time: 1140 us -> 990 us (0.87)
  blocking collectives: 150 us -> 0 us
    psum x4 -> x0, blocking collectives: 129 us -> none  [the longest x1 42.5 us: on_device(): grad_norm = jnp.sqrt(lax.psum(local_square, ('dp', 'tensor')))]
    all_gather x4 -> x0, blocking collectives: 20.6 us -> none  [combined_all(): pieces = jax.tree.map(lambda part: lax.all_gather(part, axis), value)]
    pallas_call x4, Pallas kernels: 336 us -> 350 us  [the longest x1 170 us: finish_call(): pl.pallas_call(functools.partial(finish_kernel, inner), out_shape=[jax.Sh...]
where the time goes in v2:
time: 990 us; the launch traced here: 985 us
  Pallas kernels  644 us (65%)
  matrix products  208 us (21%)
  other arithmetic  66.5 us (7%)
  local copies, waits for them, and re-layouts  59.7 us (6%)
    pallas_call x2, Pallas kernels, spread_weights(): pl.pallas_call(functools.partial(spread_weights_kernel, inner, tokens is...  216 us
    pallas_call x1, Pallas kernels, finish_call(): pl.pallas_call(functools.partial(finish_kernel, inner), out_shape=[jax.Sh...  170 us
    pallas_call x2, Pallas kernels, branch_call(): pl.pallas_call(functools.partial(branch_kernel, inner), out_shape=jax.Sha...  166 us
    pallas_call x1, Pallas kernels, final_grad_call(): pl.pallas_call(functools.partial(final_grad_kernel, inner), out_shape=[ja...  78.5 us
    dot_general x4, matrix products, contract_cols(): lax.dot_general(left_rows, right_rows, (((1,), (1,)), ((), ())), preferre...  57.7 us
    dot_general x2, matrix products, vocab_stats(): logits = jnp.dot(final_low, head_weight, preferred_element_type=F32)  45.6 us
    dot_general x2, matrix products, attention_mlp(): hidden = jnp.dot(two_low, up_all, preferred_element_type=F32) + up_bias  34.5 us
    dot_general x3, matrix products, contract_rows(): lax.dot_general(left_rows, right_rows, (((0,), (0,)), ((), ())), preferre...  25.6 us

profile of v2, /device:TPU:0, one launch (start us, length us, event | category | flops | bytes accessed | tf_op | source)
XLA Modules:
  0.0 985.2 jit_solution(10237129174720023918)
XLA Ops:
  7.9 133.6 %shard_map.436 = (bf16[2048,384]{1,0:T(8,128)(2,1)}, bf16[2048,512]{1,0:T(8,128)(2,1)}, bf16[640,2048]{1,0:T(8,128)(2,1)}, bf16[2048,2048]{1,0:T(8,128)(2,1)}, s32[4,8,128]{2,1,0:T(8,128)}) custom-call(bf16[256,1536]{1,0:T(8,128)(2,1)} %convert_element_type.209.refs_0_, bf16[512,256]{1,0:T(8,128)(2,1)} %convert_element_type.210.refs_1_, ...), custom_call_target="tpu_custom_call" | custom-call | tf_op jit(solution)/shard_map/pallas_call | solution.py:282
  149.6 82.3 %shard_map.438 = (bf16[2048,384]{1,0:T(8,128)(2,1)}, bf16[2048,512]{1,0:T(8,128)(2,1)}, bf16[640,2048]{1,0:T(8,128)(2,1)}) custom-call(bf16[256,1536]{1,0:T(8,128)(2,1)} %refs_0_.1, bf16[512,256]{1,0:T(8,128)(2,1)} %refs_1_.1, bf16[256,2048]{1,0:T(8,128)(2,1)} %refs_2_.1, bf16[2048,256]{1,0:T(8,128)(2,1)} %refs_3_.1), custom_call_target="tpu_custom_call" | custom-call | tf_op jit(solution)/shard_map/pallas_call | solution.py:282
  231.9 8.1 fusion.67
  251.7 9.7 fusion.9
  299.4 17.2 %fusion.43 = bf16[2048,512]{1,0:T(8,128)(2,1)S(1)} fusion(bf16[2048,512]{1,0:T(8,128)(2,1)} %get-tuple-element.93, bf16[2048,2048]{1,0:T(8,128)(2,1)} %get-tuple-element.87, f32[2048]{0:T(1024)S(1)} %bitcast.223, f32[2048]{0:T(1024)S(1)} %bitcast.222, f32[2048]{0:T(1024)S(1)} %add_rsqrt_fusion, f32[2048]{0:T(1024)S(1)} %broadcast_multiply_fusion, ...), kind=kOutput, calls=%fused_computation.53 | convolution fusion | flops 4389339136 | bytes 12617728 | tf_op jit(solution)/shard_map/dot_general | solution.py:995
  316.7 8.9 convolution_convert_fusion.part_ref
  327.1 80.6 %shard_map.439 = bf16[512,2048]{1,0:T(8,128)(2,1)} custom-call(bf16[2048,2048]{1,0:T(8,128)(2,1)} %convolution_convert_fusion.part_ref, bf16[512,2048]{1,0:T(8,128)(2,1)} %tokens_ref.5, f32[2,2048]{1,0:T(2,128)} %slice.264.rows_ref), custom_call_target="tpu_custom_call" | custom-call | tf_op jit(solution)/shard_map/pallas_call | solution.py:438
  407.8 22.7 %fusion.196 = (f32[512]{0:T(512)S(1)}, f32[512,6400]{1,0:T(8,128)}) fusion(bf16[512,2048]{1,0:T(8,128)(2,1)} %shard_map.439, bf16[2048,6400]{1,0:T(8,128)(2,1)} %param.41), kind=kOutput, calls=%fused_computation.295 | convolution fusion | flops 13425049600 | bytes 41420800 | tf_op jit(solution)/shard_map/dot_general | solution.py:1044
  442.8 17.3 %fusion.40 = (bf16[2048,512]{1,0:T(8,128)(2,1)S(1)}, f32[2048,512]{1,0:T(8,128)}) fusion(f32[512]{0:T(512)S(1)} %dynamic_slice.13, bf16[2048,2048]{1,0:T(8,128)(2,1)} %get-tuple-element.148, bf16[2048,512]{1,0:T(8,128)(2,1)} %get-tuple-element.90), kind=kOutput, calls=%fused_computation.50 | convolution fusion | flops 4364173312 | bytes 16779264 | tf_op jit(solution)/shard_map/dot_general | solution.py:995
  460.1 8.9 convolution_convert_fusion.1.part_ref
  470.4 85.5 %shard_map.437 = bf16[512,2048]{1,0:T(8,128)(2,1)} custom-call(bf16[2048,2048]{1,0:T(8,128)(2,1)} %convolution_convert_fusion.1.part_ref, bf16[512,2048]{1,0:T(8,128)(2,1)} %tokens_ref.5, f32[2,2048]{1,0:T(2,128)} %slice.250.rows_ref), custom_call_target="tpu_custom_call" | custom-call | tf_op jit(solution)/shard_map/pallas_call | solution.py:438
  556.0 22.9 %fusion.195 = (f32[512]{0:T(512)S(1)}, f32[512,6400]{1,0:T(8,128)}) fusion(bf16[512,2048]{1,0:T(8,128)(2,1)} %shard_map.437, bf16[2048,6400]{1,0:T(8,128)(2,1)} %param.41), kind=kOutput, calls=%fused_computation.294 | convolution fusion | flops 13425049600 | bytes 41420800 | tf_op jit(solution)/shard_map/dot_general | solution.py:1044
  579.0 11.5 %fusion.20 = (f32[512]{0:T(512)S(1)}, f32[512]{0:T(512)S(1)}, f32[512]{0:T(512)S(1)}, f32[512]{0:T(512)S(1)}) fusion(f32[512,6400]{1,0:T(8,128)} %get-tuple-element.194, s32[6400]{0:T(1024)S(1)} %iota_add_fusion, s32[512]{0:T(512)S(1)} %copy-done.65, f32[512]{0:T(512)S(1)} %get-tuple-element.193, f32[512,6400]{1,0:T(8,128)} %get-tuple-element.190, ...), kind=kLoop, calls=%fused_computation.26 | loop fusion | flops 29489152 | bytes 26254336 | tf_op jit(solution)/shard_map/reduce_sum | solution.py:1049
  597.1 13.4 %shard_map.440 = f32[2,512]{1,0:T(2,128)} custom-call(f32[8,512]{1,0:T(8,128)} %stack.71.stats_ref, f32[8,512]{1,0:T(8,128)} %pad_convert_fusion.member_ref, f32[8,128]{1,0:T(8,128)} %scatter.28.label_ref), custom_call_target="tpu_custom_call" | custom-call | tf_op jit(solution)/shard_map/pallas_call | solution.py:901
  611.3 22.4 %fusion.32.part_ref = f32[512,2048]{1,0:T(8,128)} fusion(bf16[2048,6400]{1,0:T(8,128)(2,1)} %param.41, f32[512,6400]{1,0:T(8,128)} %get-tuple-element.190, f32[512]{0:T(512)S(1)} %bitcast.228, f32[512]{0:T(512)S(1)} %bitcast.227, s32[6400]{0:T(1024)S(1)} %iota_add_fusion, s32[512]{0:T(512)S(1)} %copy-done.65), kind=kOutput, calls=%fused_computation.40 | convolution fusion | flops 13441433600 | bytes 43547648 | tf_op jit(solution)/shard_map/dot_general | solution.py:968
  635.9 78.5 %shard_map.441 = (f32[128,2048]{1,0:T(8,128)S(1)}, bf16[2048,2048]{1,0:T(8,128)(2,1)}) custom-call(f32[512,2048]{1,0:T(8,128)S(1)} %copy-done.1), custom_call_target="tpu_custom_call" | custom-call | tf_op jit(solution)/shard_map/pallas_call | solution.py:529
  714.4 9.7 fusion.197
  735.9 8.5 fusion.198
  744.4 17.0 %fusion.178 = (f32[2048]{0:T(1024)S(1)}, f32[2048]{0:T(1024)S(1)}, bf16[2048,2048]{1,0:T(8,128)(2,1)}, f32[2048]{0:T(1024)S(1)}, f32[2048]{0:T(1024)S(1)}) fusion(f32[2048]{0:T(1024)S(1)} %copy-done.53, f32[2048]{0:T(1024)S(1)} %copy-done.48, bf16[2048,2048]{1,0:T(8,128)(2,1)} %get-tuple-element.87, f32[2048]{0:T(1024)S(1)} %bitcast.210, ...), kind=kOutput, calls=%fused_computation.284 | convolution fusion | flops 4349485056 | bytes 37814272 | tf_op jit(solution)/shard_map/dot_general | solution.py:968
  762.2 9.9 %convolution_convert_fusion.2.low = bf16[640,2048]{1,0:T(8,128)(2,1)} fusion(bf16[2048,2048]{1,0:T(8,128)(2,1)} %get-tuple-element.95, bf16[2048,512]{1,0:T(8,128)(2,1)} %copy-done.70, bf16[2048,128]{1,0:T(8,128)(2,1)S(1)} %bitcast.198), kind=kOutput, calls=%fused_computation.101 | convolution fusion | flops 5375262720 | bytes 13631488 | tf_op jit(solution)/shard_map/dot_general | solution.py:962
  772.1 9.6 convolution_convert_fusion.3.up
  781.7 6.1 convolution_convert_fusion.4.qkv
  787.9 170.4 %shard_map.442 = (bf16[512,2048]{1,0:T(8,128)(2,1)}, bf16[256,1536]{1,0:T(8,128)(2,1)}, bf16[256,2048]{1,0:T(8,128)(2,1)}, bf16[512,256]{1,0:T(8,128)(2,1)}, bf1...) custom-call(bf16[2048,2048]{1,0:T(8,128)(2,1)} %get-tuple-element.144.part_ref, ...), custom_call_target="tpu_custom_call" | custom-call | tf_op jit(solution)/shard_map/pallas_call | solution.py:809
  964.1 6.5 multiply_subtract_fusion
  (249 shorter events, 117.4 us)
Async XLA Ops:
  147.2 152.2 %copy-start.47 = (f32[2048]{0:T(1024)}, f32[2048]{0:T(1024)S(1)}, u32[]{:S(2)}) copy-start(f32[2048]{0:T(1024)S(1)} %broadcast_multiply_fusion) | copy-start | bytes 24580
  149.6 149.8 %copy-start.52 = (f32[2048]{0:T(1024)}, f32[2048]{0:T(1024)S(1)}, u32[]{:S(2)}) copy-start(f32[2048]{0:T(1024)S(1)} %add_rsqrt_fusion) | copy-start | bytes 24580
  249.1 12.4 %copy-start.14 = (f32[4,512,1,1,128]{1,4,0,3,2:T(8,128)}, f32[4,512,1,1,128]{1,4,0,3,2:T(8,128)S(1)}, u32[]{:S(2)}) copy-start(f32[4,512,1,1,128]{1,4,0,3,2:T(8,128)S(1)} %copy.184) | copy-start | bytes 3145732
  251.7 13.1 %copy-start.24 = (bf16[2048,384]{1,0:T(8,128)(2,1)S(1)}, bf16[2048,384]{1,0:T(8,128)(2,1)}, u32[]{:S(2)}) copy-start(bf16[2048,384]{1,0:T(8,128)(2,1)} %get-tuple-element.88) | copy-start | bytes 4718596
  299.4 17.3 %copy-start.68 = (bf16[640,2048]{1,0:T(8,128)(2,1)S(1)}, bf16[640,2048]{1,0:T(8,128)(2,1)}, u32[]{:S(2)}) copy-start(bf16[640,2048]{1,0:T(8,128)(2,1)} %get-tuple-element.94) | copy-start | bytes 7864324
  407.7 22.9 %copy-start.29 = (pred[512,512]{0,1:T(8,128)(4,1)S(1)}, pred[512,512]{0,1:T(8,128)(4,1)}, u32[]{:S(2)}) copy-start(pred[512,512]{0,1:T(8,128)(4,1)} %copy-done.28) | copy-start | bytes 786436
  407.7 22.9 %copy-start.34 = (bf16[4,512,16]{1,2,0:T(8,128)(2,1)S(1)}, bf16[4,512,16]{1,2,0:T(8,128)(2,1)}, u32[]{:S(2)}) copy-start(bf16[4,512,16]{1,2,0:T(8,128)(2,1)} %get-tuple-element.173) | copy-start | bytes 196612
  407.7 22.9 %copy-start.36 = (bf16[4,512,16]{1,2,0:T(8,128)(2,1)S(1)}, bf16[4,512,16]{1,2,0:T(8,128)(2,1)}, u32[]{:S(2)}) copy-start(bf16[4,512,16]{1,2,0:T(8,128)(2,1)} %get-tuple-element.174) | copy-start | bytes 196612
  407.7 22.9 %copy-start.38 = (bf16[4,512,16]{1,2,0:T(8,128)(2,1)S(1)}, bf16[4,512,16]{1,2,0:T(8,128)(2,1)}, u32[]{:S(2)}) copy-start(bf16[4,512,16]{1,2,0:T(8,128)(2,1)} %get-tuple-element.177) | copy-start | bytes 196612
  407.7 22.9 %copy-start.40 = (bf16[4,512,16]{1,2,0:T(8,128)(2,1)S(1)}, bf16[4,512,16]{1,2,0:T(8,128)(2,1)}, u32[]{:S(2)}) copy-start(bf16[4,512,16]{1,2,0:T(8,128)(2,1)} %get-tuple-element.178) | copy-start | bytes 196612
  442.8 17.3 %copy-start.66 = (bf16[640,2048]{1,0:T(8,128)(2,1)S(1)}, bf16[640,2048]{1,0:T(8,128)(2,1)}, u32[]{:S(2)}) copy-start(bf16[640,2048]{1,0:T(8,128)(2,1)} %get-tuple-element.91) | copy-start | bytes 7864324
  556.0 22.9 %copy-start.65 = (s32[512]{0:T(512)S(1)}, s32[512]{0:T(512)}, u32[]{:S(2)}) copy-start(s32[512]{0:T(512)} %param.38) | copy-start | bytes 6148
  578.9 12.2 %copy-start.60 = (s32[1,4]{1,0:T(1,128)S(1)}, s32[1,4]{1,0:T(1,128)}, u32[]{:S(2)}) copy-start(s32[1,4]{1,0:T(1,128)} %param.39) | copy-start | bytes 52
  578.9 17.5 %copy-start.69 = (s32[1,4]{1,0:T(1,128)S(1)}, s32[1,4]{1,0:T(1,128)}, u32[]{:S(2)}) copy-start(s32[1,4]{1,0:T(1,128)} %param.40) | copy-start | bytes 52
  635.9 78.5 %copy-start.67 = (bf16[640,2048]{1,0:T(8,128)(2,1)S(1)}, bf16[640,2048]{1,0:T(8,128)(2,1)}, u32[]{:S(2)}) copy-start(bf16[640,2048]{1,0:T(8,128)(2,1)} %get-tuple-element.91) | copy-start | bytes 7864324
  714.4 47.0 %copy-start = (f32[128,2048]{1,0:T(8,128)}, f32[128,2048]{1,0:T(8,128)S(1)}, u32[]{:S(2)}) copy-start(f32[128,2048]{1,0:T(8,128)S(1)} %get-tuple-element.96.quarter_ref) | copy-start | bytes 3145732
  762.2 19.5 %slice-start = ((s8[8388608]{0:T(1024)(128)(4,1)}), s8[4194304]{0:T(1024)(128)(4,1)S(1)}, s32[]{:S(2)}) async-start(s8[8388608]{0:T(1024)(128)(4,1)} %bitcast.184), calls=%async_computation | async-start | bytes 8388608
  787.8 173.2 %copy-start.58 = (f32[3584]{0:T(1024)S(1)}, f32[3584]{0:T(1024)}, u32[]{:S(2)}) copy-start(f32[3584]{0:T(1024)} %param.47) | copy-start | bytes 43012
  787.8 173.2 %copy-start.61 = (f32[3584]{0:T(1024)S(1)}, f32[3584]{0:T(1024)}, u32[]{:S(2)}) copy-start(f32[3584]{0:T(1024)} %param.59) | copy-start | bytes 43012
  787.8 173.2 %copy-start.62 = (f32[3584]{0:T(1024)S(1)}, f32[3584]{0:T(1024)}, u32[]{:S(2)}) copy-start(f32[3584]{0:T(1024)} %param.53) | copy-start | bytes 43012
  787.8 174.7 %copy-start.44 = (f32[6,2048]{1,0:T(8,128)S(1)}, f32[6,2048]{1,0:T(8,128)}, u32[]{:S(2)}) copy-start(f32[6,2048]{1,0:T(8,128)} %param.46) | copy-start | bytes 147460
  787.8 174.7 %copy-start.49 = (f32[6,2048]{1,0:T(8,128)S(1)}, f32[6,2048]{1,0:T(8,128)}, u32[]{:S(2)}) copy-start(f32[6,2048]{1,0:T(8,128)} %param.58) | copy-start | bytes 147460
  787.8 174.7 %copy-start.50 = (f32[6,2048]{1,0:T(8,128)S(1)}, f32[6,2048]{1,0:T(8,128)}, u32[]{:S(2)}) copy-start(f32[6,2048]{1,0:T(8,128)} %param.52) | copy-start | bytes 147460
  787.9 176.2 %copy-start.7 = (f32[2048,256]{1,0:T(8,128)S(1)}, f32[2048,256]{1,0:T(8,128)}, u32[]{:S(2)}) copy-start(f32[2048,256]{1,0:T(8,128)} %param.45) | copy-start | bytes 6291460
  (49 other events, 245.2 us)

commit v3 on v2

--- a/solution.py
+++ b/solution.py
@@ -81,176 +81,173 @@
     return copy
 
 
-def spread_weights_kernel(inner, with_tokens, *refs):
-    here = Place(inner)
-    if with_tokens:
-        (qkv, out, up, down, tokens, lengths, qkv_all, up_all, low_all, tokens_all, lengths_all,
-         send_o, recv_o, send_i, recv_i, local, send_t, recv_t, send_l, recv_l) = refs
-    else:
-        qkv, out, up, down, qkv_all, up_all, low_all, send_o, recv_o, send_i, recv_i, local = refs
-    shard = qkv.shape[0]
-    width_qkv, width_up = qkv.shape[1] // SPLIT, up.shape[1] // SPLIT
-    width_out, width_down = out.shape[0] // SPLIT, down.shape[0] // SPLIT
-
-    def src(m, part):
-        if m == 0:
-            return qkv.at[:, pl.ds(part * width_qkv, width_qkv)]
-        if m == 1:
-            return up.at[:, pl.ds(part * width_up, width_up)]
-        if m == 2:
-            return out.at[pl.ds(part * width_out, width_out), :]
-        return down.at[pl.ds(part * width_down, width_down), :]
-
-    def dst(m, index):
+class Spread:
+    def __init__(self, here, shards, wholes, send_o, recv_o, send_i, recv_i, local):
+        self.here = here
+        self.qkv, self.out, self.up, self.down = shards
+        self.qkv_all, self.up_all, self.low_all = wholes
+        self.send_o, self.recv_o, self.send_i, self.recv_i = send_o, recv_o, send_i, recv_i
+        self.local = local
+        self.first, self.own, self.passed = {}, [], []
+        self.order = [(m, s) for m in range(4) for s in (2, 1, 3)]
+
+    def src(self, m, part):
+        shard = (self.qkv, self.up, self.out, self.down)[m]
+        width = shard.shape[1 if m < 2 else 0] // SPLIT
+        where = pl.ds(part * width, width)
+        return shard.at[:, where] if m < 2 else shard.at[where, :]
+
+    def dst(self, m, index):
+        shard = self.qkv.shape[0]
         where = pl.ds(index * shard, shard)
-        if m == 0:
-            return qkv_all.at[where, :]
-        if m == 1:
-            return up_all.at[where, :]
+        if m < 2:
+            return (self.qkv_all, self.up_all)[m].at[where, :]
+        width_out, width_down = self.out.shape[0] // SPLIT, self.down.shape[0] // SPLIT
         rows = pl.ds(0, width_out) if m == 2 else pl.ds(width_out, width_down)
+        low_all = self.low_all
         return low_all.at[rows, where] if aligned(shard) else low_all.at[index, rows, :]
 
-    peers = [here.outer_peer(s) for s in range(1, SPLIT)]
-    peers += [here.inner_peer(r) for r in range(1, inner)]
-    if with_tokens:
-        peers += [here.far_peer(), here.near_peer()]
-    greet(peers)
-
-    waits = []
-    token_copies = []
-    if with_tokens:
-        rows = tokens.shape[0] // QUARTERS
-
-        def piece(part, quarter):
-            return tokens_all.at[pl.ds((part * QUARTERS + quarter) * rows, rows), :]
-
-        for s in range(1, SPLIT):
-            token_copies.append(
+    def peers(self):
+        here = self.here
+        peers = [here.outer_peer(s) for s in range(1, SPLIT)]
+        return peers + [here.inner_peer(r) for r in range(1, here.inner)]
+
+    def send_on(self, number):
+        if number >= len(self.order):
+            return
+        m, s = self.order[number]
+        self.first[m, s] = remote(
+            self.src(m, (self.here.o + s) % SPLIT),
+            self.dst(m, self.here.dp),
+            self.send_o.at[m, s - 1],
+            self.recv_o.at[m, s - 1],
+            self.here.outer_peer(s),
+        )
+
+    def pass_on(self, m, s, source, index):
+        here = self.here
+        for r in range(1, here.inner):
+            self.passed.append(
                 remote(
-                    tokens.at[pl.ds(here.t * rows, rows), :],
-                    piece(here.o, here.t),
-                    send_t.at[0, s - 1],
-                    recv_t.at[0, s - 1],
-                    here.outer_peer(s),
-                )
-            )
-        for s in range(1, SPLIT):
-            waits.append(
-                remote(
-                    lengths,
-                    lengths_all.at[here.o],
-                    send_l.at[s - 1],
-                    recv_l.at[s - 1],
-                    here.outer_peer(s),
-                )
-            )
-    first = {}
-    order = [(m, s) for m in range(4) for s in (2, 1, 3)]
-
-    def send_on(number):
-        if number >= len(order):
-            return
-        m, s = order[number]
-        first[m, s] = remote(
-            src(m, (here.o + s) % SPLIT),
-            dst(m, here.dp),
-            send_o.at[m, s - 1],
-            recv_o.at[m, s - 1],
-            here.outer_peer(s),
-        )
-
-    for number in range(0 if with_tokens else AHEAD):
-        send_on(number)
-    own = []
-    for m in range(4):
-        own.append(pltpu.make_async_copy(src(m, here.o), dst(m, here.dp), local.at[m]))
-    if with_tokens:
-        block = tokens.shape[0]
-        own.append(
-            pltpu.make_async_copy(
-                tokens, tokens_all.at[pl.ds(here.o * block, block), :], local.at[4]
-            )
-        )
-        own.append(pltpu.make_async_copy(lengths, lengths_all.at[here.o], local.at[5]))
-    for copy in own:
-        copy.start()
-    for m in range(4):
-        for r in range(1, inner):
-            waits.append(
-                remote(
-                    src(m, here.o),
-                    dst(m, here.dp),
-                    send_i.at[m, 0, r - 1],
-                    recv_i.at[m, 0, r - 1],
+                    source,
+                    self.dst(m, index),
+                    self.send_i.at[m, s, r - 1],
+                    self.recv_i.at[m, s, r - 1],
                     here.inner_peer(r),
                 )
             )
-    across = {}
-    if with_tokens:
-        for s in range(1, SPLIT):
-            token_copies[s - 1].wait_recv()
-            send_on(s - 1)
-            part = (here.o + SPLIT - s) % SPLIT
-            across[s] = remote(
+
+    def start_own(self):
+        here = self.here
+        for m in range(4):
+            source = self.src(m, here.o)
+            copy = pltpu.make_async_copy(source, self.dst(m, here.dp), self.local.at[m])
+            copy.start()
+            self.own.append(copy)
+            self.pass_on(m, 0, source, here.dp)
+
+    def step(self, number):
+        here = self.here
+        m, s = self.order[number]
+        self.first[m, s].wait_recv()
+        self.send_on(number + AHEAD)
+        index = ((here.o + SPLIT - s) % SPLIT) * here.inner + here.i
+        self.pass_on(m, s, self.dst(m, index), index)
+
+    def finish(self):
+        for copy in self.first.values():
+            copy.wait_send()
+        for copy in self.own:
+            copy.wait()
+        for copy in self.passed:
+            copy.wait()
+
+
+def spread_weights_kernel(
+    inner, qkv, out, up, down, tokens, lengths, qkv_all, up_all, low_all, tokens_all, lengths_all,
+    send_o, recv_o, send_i, recv_i, local, send_t, recv_t, send_l, recv_l,
+):
+    here = Place(inner)
+    spread = Spread(
+        here, (qkv, out, up, down), (qkv_all, up_all, low_all), send_o, recv_o, send_i, recv_i, local
+    )
+    greet(spread.peers() + [here.far_peer(), here.near_peer()])
+    rows, block = tokens.shape[0] // QUARTERS, tokens.shape[0]
+
+    def piece(part, quarter):
+        return tokens_all.at[pl.ds((part * QUARTERS + quarter) * rows, rows), :]
+
+    waits, token_copies, across, own = [], {}, {}, []
+    for s in (2, 1, 3):
+        token_copies[s] = remote(
+            tokens.at[pl.ds(here.t * rows, rows), :],
+            piece(here.o, here.t),
+            send_t.at[0, s - 1],
+            recv_t.at[0, s - 1],
+            here.outer_peer(s),
+        )
+        waits.append(
+            remote(
+                lengths,
+                lengths_all.at[here.o],
+                send_l.at[s - 1],
+                recv_l.at[s - 1],
+                here.outer_peer(s),
+            )
+        )
+    own.append(
+        pltpu.make_async_copy(
+            tokens, tokens_all.at[pl.ds(here.o * block, block), :], local.at[4]
+        )
+    )
+    own.append(pltpu.make_async_copy(lengths, lengths_all.at[here.o], local.at[5]))
+    for copy in own:
+        copy.start()
+    spread.start_own()
+    for number, s in enumerate((2, 1, 3)):
+        token_copies[s].wait_recv()
+        spread.send_on(number)
+        part = (here.o + SPLIT - s) % SPLIT
+        for stage, peer in ((1, here.far_peer()), (2, here.near_peer())):
+            copy = remote(
                 piece(part, here.t),
                 piece(part, here.t),
-                send_t.at[1, s - 1],
-                recv_t.at[1, s - 1],
-                here.far_peer(),
+                send_t.at[stage, s - 1],
+                recv_t.at[stage, s - 1],
+                peer,
             )
-            waits.append(
-                remote(
-                    piece(part, here.t),
-                    piece(part, here.t),
-                    send_t.at[2, s - 1],
-                    recv_t.at[2, s - 1],
-                    here.near_peer(),
-                )
+            if stage == 1:
+                across[s] = copy
+            else:
+                waits.append(copy)
+    for number in range(len(spread.order)):
+        spread.step(number)
+    for s in (2, 1, 3):
+        across[s].wait_recv()
+        part = (here.o + SPLIT - s) % SPLIT
+        waits.append(
+            remote(
+                piece(part, here.far),
+                piece(part, here.far),
+                send_t.at[3, s - 1],
+                recv_t.at[3, s - 1],
+                here.near_peer(),
             )
-    for number, (m, s) in enumerate(order):
-        first[m, s].wait_recv()
-        send_on(number + AHEAD)
-        index = ((here.o + SPLIT - s) % SPLIT) * inner + here.i
-        for r in range(1, inner):
-            waits.append(
-                remote(
-                    dst(m, index),
-                    dst(m, index),
-                    send_i.at[m, s, r - 1],
-                    recv_i.at[m, s, r - 1],
-                    here.inner_peer(r),
-                )
-            )
-    if with_tokens:
-        for s in range(1, SPLIT):
-            across[s].wait_recv()
-            part = (here.o + SPLIT - s) % SPLIT
-            waits.append(
-                remote(
-                    piece(part, here.far),
-                    piece(part, here.far),
-                    send_t.at[3, s - 1],
-                    recv_t.at[3, s - 1],
-                    here.near_peer(),
-                )
-            )
-        for copy in token_copies:
-            copy.wait_send()
-        for copy in across.values():
-            copy.wait_send()
-    for copy in first.values():
+        )
+    for copy in list(token_copies.values()) + list(across.values()):
         copy.wait_send()
     for copy in own:
         copy.wait()
+    spread.finish()
     for copy in waits:
         copy.wait()
 
 
-def spread_weights(shards, inner, tokens, lengths, number):
+def whole_shapes(shards, inner):
     qkv, out, up, down = shards
     d_model = out.shape[1] * SPLIT * inner
     width = out.shape[0] // SPLIT + down.shape[0] // SPLIT
-    shapes = [
+    return [
         jax.ShapeDtypeStruct((d_model, qkv.shape[1] // SPLIT), BF16),
         jax.ShapeDtypeStruct((d_model, up.shape[1] // SPLIT), BF16),
         jax.ShapeDtypeStruct(
@@ -258,38 +255,46 @@
             BF16,
         ),
     ]
+
+
+def joined_columns(low_all):
+    if low_all.ndim == 3:
+        low_all = jnp.swapaxes(low_all, 0, 1).reshape(low_all.shape[1], -1)
+    return low_all
+
+
+def spread_scratch(inner):
     dma = pltpu.SemaphoreType.DMA
-    scratch = [
+    return [
         dma((4, SPLIT - 1)),
         dma((4, SPLIT - 1)),
         dma((4, SPLIT, max(inner - 1, 1))),
         dma((4, SPLIT, max(inner - 1, 1))),
         dma((6,)),
     ]
-    operands = [qkv, out, up, down]
-    if tokens is not None:
-        operands += [tokens, lengths]
-        shapes += [
-            jax.ShapeDtypeStruct((tokens.shape[0] * SPLIT, tokens.shape[1]), BF16),
-            jax.ShapeDtypeStruct((SPLIT, *lengths.shape), lengths.dtype),
-        ]
-        scratch += [
+
+
+def spread_weights(shards, inner, tokens, lengths, number):
+    dma = pltpu.SemaphoreType.DMA
+    shapes = whole_shapes(shards, inner) + [
+        jax.ShapeDtypeStruct((tokens.shape[0] * SPLIT, tokens.shape[1]), BF16),
+        jax.ShapeDtypeStruct((SPLIT, *lengths.shape), lengths.dtype),
+    ]
+    qkv_all, up_all, low_all, *gathered = pl.pallas_call(
+        functools.partial(spread_weights_kernel, inner),
+        out_shape=shapes,
+        in_specs=[ANY_SPEC] * 6,
+        out_specs=[ANY_SPEC] * len(shapes),
+        scratch_shapes=spread_scratch(inner)
+        + [
             dma((4, SPLIT - 1)),
             dma((4, SPLIT - 1)),
             dma((SPLIT - 1,)),
             dma((SPLIT - 1,)),
-        ]
-    qkv_all, up_all, low_all, *gathered = pl.pallas_call(
-        functools.partial(spread_weights_kernel, inner, tokens is not None),
-        out_shape=shapes,
-        in_specs=[ANY_SPEC] * len(operands),
-        out_specs=[ANY_SPEC] * len(shapes),
-        scratch_shapes=scratch,
+        ],
         compiler_params=pltpu.CompilerParams(collective_id=number, has_side_effects=True),
-    )(*operands)
-    if low_all.ndim == 3:
-        low_all = jnp.swapaxes(low_all, 0, 1).reshape(width, d_model)
-    return (qkv_all, up_all, low_all, *gathered)
+    )(*shards, tokens, lengths)
+    return (qkv_all, up_all, joined_columns(low_all), *gathered)
 
 
 def f32(value):
@@ -310,17 +315,16 @@
         block = (self.here.o + 1 + step) % SPLIT
         return pl.ds((block * QUARTERS + quarter) * self.rows, self.rows)
 
-    def start(self):
+    def start(self, step):
         here = self.here
-        for step in range(SPLIT):
-            for side, quarter in enumerate(((here.near + 2) % QUARTERS, here.near)):
-                self.near[step, side] = remote(
-                    self.part.at[self.rows_of(step, quarter), :],
-                    self.near_in.at[step, side],
-                    self.near_sems[0].at[step, side],
-                    self.near_sems[1].at[step, side],
-                    here.near_peer(),
-                )
+        for side, quarter in enumerate(((here.near + 2) % QUARTERS, here.near)):
+            self.near[step, side] = remote(
+                self.part.at[self.rows_of(step, quarter), :],
+                self.near_in.at[step, side],
+                self.near_sems[0].at[step, side],
+                self.near_sems[1].at[step, side],
+                here.near_peer(),
+            )
 
     def across(self, step):
         here = self.here
@@ -388,20 +392,216 @@
     return [here.outer_peer(s) for s in range(1, SPLIT)] + [here.far_peer(), here.near_peer()]
 
 
-def branch_kernel(inner, part_ref, tokens_ref, rows_ref, final_ref, *scratch):
+def dot(left, right):
+    return jnp.dot(left, right, preferred_element_type=F32)
+
+
+def dot_cols(left, right):
+    return lax.dot_general(left, right, (((1,), (1,)), ((), ())), preferred_element_type=F32)
+
+
+def error_function(value):
+    value = jnp.clip(value, -3.832506856900711, 3.832506856900711)
+    square = value * value
+    above = jnp.full_like(square, 0.00022905065861350646)
+    for term in (0.0034082910107109506, 0.050955695062380861, 0.18520832239976145, 1.128379143519084):
+        above = above * square + term
+    below = jnp.full_like(square, -1.1791602954361697e-7)
+    for term in (
+        0.000023547966471313185, 0.0010179625278914885, 0.014070470171167667,
+        0.11098505178285362, 0.49746925110067538, 1.0,
+    ):
+        below = below * square + term
+    return value * above / below
+
+
+def turn(values, tables, where, direction):
+    cosine, sine_first, sine_second = (table[where, :] for table in tables)
+    ahead = pltpu.roll(values, values.shape[1] - ROT // 2, 1)
+    behind = pltpu.roll(values, ROT // 2, 1)
+    return values * cosine + direction * (ahead * sine_first + behind * sine_second)
+
+
+def row_tiles(start, count, tile, body):
+    @pl.loop(0, count // tile)
+    def _(n):
+        body(pl.ds(pl.multiple_of(start + n * tile, tile), tile), pl.ds(pl.multiple_of(n * tile, tile), tile))
+
+
+def forward_kernel(inner, keep, background, *refs):
     here = Place(inner)
-    sums = RowSum(here, part_ref, *scratch)
-    greet(reduce_peers(here))
-    mine = pl.ds(here.t * sums.rows, sums.rows)
-    sums.start()
+    (tokens_ref, rows_ref, qkv_ref, up_ref, low_ref, qkv_bias, up_bias, cosine, sine_first,
+     sine_second, doc_col, doc_row, *refs) = refs
+    tables = (cosine, sine_first, sine_second)
+    shards = refs[:4] if background else []
+    refs = refs[len(shards):]
+    final_ref, *refs = refs
+    if keep:
+        slope_ref, mixed_ref, total_ref, joined_ref, *refs = refs
+    wholes = refs[:3] if background else []
+    refs = refs[len(wholes):]
+    if not keep:
+        mixed_ref, joined_ref, *refs = refs
+    one_ref, two_ref, hidden_ref, part_ref, *refs = refs
+    sums = RowSum(here, part_ref, *refs[:14])
+    refs = refs[14:]
+    block = one_ref.shape[0]
+    heads = qkv_ref.shape[1] // (3 * HD)
+    cut = heads * HD
+    peers = reduce_peers(here)
+    spread = None
+    if background:
+        spread = Spread(here, shards, wholes, *refs)
+        peers = spread.peers() + [here.far_peer(), here.near_peer()]
+    greet(peers)
+    events = []
+    if background:
+        for number in range(AHEAD):
+            spread.send_on(number)
+        spread.start_own()
+        events = list(range(len(spread.order)))
+
+    def serve():
+        if events:
+            spread.step(events.pop(0))
+
     for step in range(SPLIT):
-        sums.across(step)
-    for step in range(SPLIT):
-        sums.along(step)
-    branch = sums.value() + rows_ref[0:1, :] + rows_ref[1:2, :]
-    final_ref[mine, :] = (f32(tokens_ref[mine, :]) + branch).astype(BF16)
+        start = ((here.o + 1 + step) % SPLIT) * block
+        kept = start if keep else 0
+
+        def norm(where, own):
+            values = f32(tokens_ref[where, :])
+            centre = values - jnp.mean(values, axis=1, keepdims=True)
+            spread_of = jnp.mean(centre * centre, axis=1, keepdims=True)
+            normed = centre * lax.rsqrt(spread_of + EPS_NORM)
+            one_ref[own, :] = (normed * rows_ref[0:1, :] + rows_ref[1:2, :]).astype(BF16)
+            two_ref[own, :] = (normed * rows_ref[2:3, :] + rows_ref[3:4, :]).astype(BF16)
+
+        row_tiles(start, block, 16, norm)
+        serve()
+        if step:
+            sums.across(step - 1)
+        whole = pl.ds(pl.multiple_of(start, block), block)
+        mine = pl.ds(pl.multiple_of(kept, block), block)
+        mixed = dot(one_ref[...], qkv_ref[...]) + qkv_bias[...]
+        for head in range(heads):
+            at = head * 3 * HD
+            for offset in (0, HD):
+                mixed_ref[mine, at + offset : at + offset + HD] = turn(
+                    mixed[:, at + offset : at + offset + HD], tables, whole, 1.0
+                ).astype(BF16)
+            mixed_ref[mine, at + 2 * HD : at + 3 * HD] = mixed[:, at + 2 * HD : at + 3 * HD].astype(
+                BF16
+            )
+        hidden_ref[...] = dot(two_ref[...], up_ref[...])
+        serve()
+        for head in range(heads):
+            at = head * 3 * HD
+            for first in range(0, block, 128):
+                queries = pl.ds(pl.multiple_of(kept + first, 128), 128)
+                tokens_at = pl.ds(pl.multiple_of(start + first, 128), 128)
+                keys = pl.ds(pl.multiple_of(kept, 128), first + 128)
+                scores = dot_cols(
+                    mixed_ref[queries, at : at + HD], mixed_ref[keys, at + HD : at + 2 * HD]
+                ) * HD ** (-0.5)
+                own_block = (here.o + 1 + step) % SPLIT
+                same = doc_col[tokens_at, :] == doc_row[own_block][:, : first + 128]
+                earlier = first + lax.broadcasted_iota(
+                    jnp.int32, scores.shape, 0
+                ) >= lax.broadcasted_iota(jnp.int32, scores.shape, 1)
+                scores = jnp.where(same & earlier, scores, MASKED)
+                highest = jnp.max(scores, axis=1, keepdims=True)
+                total = highest + jnp.log(
+                    jnp.sum(jnp.exp(scores - highest), axis=1, keepdims=True)
+                )
+                if keep:
+                    total_ref[tokens_at, head : head + 1] = total
+                probs = jnp.exp(scores - total).astype(BF16)
+                joined_ref[queries, head * HD : (head + 1) * HD] = dot(
+                    probs, mixed_ref[keys, at + 2 * HD : at + 3 * HD]
+                ).astype(BF16)
+        if step > 1:
+            sums.along(step - 2)
+
+        def activate(where, own):
+            hidden = hidden_ref[own, :] + up_bias[...]
+            share = 0.5 * (1.0 + error_function(hidden * 0.7071067811865476))
+            joined_ref[where, cut:] = (hidden * share).astype(BF16)
+            if keep:
+                density = jnp.exp(-0.5 * hidden * hidden) * 0.3989422804014327
+                slope_ref[where, :] = share + hidden * density
+
+        row_tiles(kept, block, 32, activate)
+        serve()
+        columns = 512
+
+        @pl.loop(0, part_ref.shape[1] // columns)
+        def _(n):
+            at = pl.ds(pl.multiple_of(n * columns, columns), columns)
+            part_ref[whole, at] = dot(joined_ref[mine, :], low_ref[:, at]).astype(BF16)
+
+        sums.start(step)
+    sums.across(SPLIT - 1)
+    while events:
+        serve()
+    sums.along(SPLIT - 2)
+    sums.along(SPLIT - 1)
+    branch = sums.value() + rows_ref[4:5, :] + rows_ref[5:6, :]
+    quarter = pl.ds(pl.multiple_of(here.o * block + here.t * sums.rows, sums.rows), sums.rows)
+    final_ref[pl.ds(pl.multiple_of(here.t * sums.rows, sums.rows), sums.rows), :] = (
+        f32(tokens_ref[quarter, :]) + branch
+    ).astype(BF16)
     gather_quarters(here, final_ref, sums.rows, *sums.quarter_sems)
     sums.finish()
+    if background:
+        spread.finish()
+
+
+def forward_call(tokens, rows, weights, biases, layout, block, inner, keep, shards, number):
+    total_rows, d_model = tokens.shape
+    qkv_all, up_all, low_all = weights
+    heads = qkv_all.shape[1] // (3 * HD)
+    background = shards is not None
+    outs = [jax.ShapeDtypeStruct((block, d_model), BF16)]
+    if keep:
+        outs += [
+            jax.ShapeDtypeStruct((total_rows, up_all.shape[1]), F32),
+            jax.ShapeDtypeStruct((total_rows, qkv_all.shape[1]), BF16),
+            jax.ShapeDtypeStruct((total_rows, heads), F32),
+            jax.ShapeDtypeStruct((total_rows, low_all.shape[0]), BF16),
+        ]
+    specs = [VMEM_SPEC] * len(outs)
+    scratch = []
+    if not keep:
+        scratch += [
+            pltpu.VMEM((block, qkv_all.shape[1]), BF16),
+            pltpu.VMEM((block, low_all.shape[0]), BF16),
+        ]
+    scratch += [
+        pltpu.VMEM((block, d_model), BF16),
+        pltpu.VMEM((block, d_model), BF16),
+        pltpu.VMEM((block, up_all.shape[1]), F32),
+        pltpu.VMEM((total_rows, d_model), BF16),
+    ]
+    scratch += reduce_scratch(block // QUARTERS, d_model)
+    operands = [tokens, rows, qkv_all, up_all, low_all, *biases, *layout]
+    in_specs = [VMEM_SPEC] * len(operands)
+    if background:
+        operands += shards
+        in_specs += [ANY_SPEC] * 4
+        outs += whole_shapes(shards, inner)
+        specs += [ANY_SPEC] * 3
+        scratch += spread_scratch(inner)
+    return pl.pallas_call(
+        functools.partial(forward_kernel, inner, keep, background),
+        out_shape=outs,
+        in_specs=in_specs,
+        out_specs=specs,
+        scratch_shapes=scratch,
+        compiler_params=pltpu.CompilerParams(
+            collective_id=number, has_side_effects=True, vmem_limit_bytes=60 * 1024 * 1024
+        ),
+    )(*operands)
 
 
 def input_change(values, scaled):
@@ -431,20 +631,6 @@
         dma((3,)),
         dma((3,)),
     ]
-
-
-def branch_call(inner, part, tokens, extra, number):
-    block, width = tokens.shape
-    return pl.pallas_call(
-        functools.partial(branch_kernel, inner),
-        out_shape=jax.ShapeDtypeStruct((block, width), BF16),
-        in_specs=[VMEM_SPEC] * 3,
-        out_specs=VMEM_SPEC,
-        scratch_shapes=reduce_scratch(block // QUARTERS, width),
-        compiler_params=pltpu.CompilerParams(
-            collective_id=number, has_side_effects=True, vmem_limit_bytes=56 * 1024 * 1024
-        ),
-    )(part, tokens, extra)
 
 
 def final_grad_kernel(
@@ -714,7 +900,8 @@
 
     for number in range(AHEAD):
         trade(number)
-    sums.start()
+    for step in range(SPLIT):
+        sums.start(step)
     small.near(rows_ref[...])
     bias_in[here.i] = bias_ref[...]
     bias_inner = [
@@ -918,12 +1105,26 @@
     )(stats, member, labels)
 
 
-def rotate(values, positions, direction):
+def turn_tables(positions):
+    half = ROT // 2
+    frequency = 10000.0 ** (-2.0 * jnp.arange(half, dtype=F32) / ROT)
+    angles = positions.reshape(-1).astype(F32)[:, None] * frequency
+    cosine, sine = jnp.cos(angles), jnp.sin(angles)
+    none = jnp.zeros((angles.shape[0], HD - ROT), F32)
+    empty = jnp.zeros_like(sine)
+    return (
+        jnp.concatenate([cosine, cosine, none + 1.0], axis=1),
+        jnp.concatenate([-sine, empty, none], axis=1),
+        jnp.concatenate([empty, sine, none], axis=1),
+    )
+
+
+def rotate_back(values, positions):
     half_rot = ROT // 2
     frequency = 10000.0 ** (-2.0 * jnp.arange(half_rot, dtype=F32) / ROT)
     angles = positions.astype(F32)[..., None] * frequency
     cosine = jnp.cos(angles)[..., None, :]
-    sine_part = direction * jnp.sin(angles)[..., None, :]
+    sine_part = -jnp.sin(angles)[..., None, :]
     first_half = values[..., :half_rot]
     second_half = values[..., half_rot:ROT]
     return jnp.concatenate(
@@ -974,42 +1175,17 @@
     return (normed * gain_row + shift_row).astype(BF16)
 
 
-def attention_mlp(one_low, two_low, qkv_bias, up_bias, weight_set, positions, allowed):
-    qkv_all, up_all, low_all = weight_set
-    blocks, block = positions.shape
-    heads_local = qkv_bias.shape[0] // (3 * HD)
-    mixed_proj = jnp.dot(one_low, qkv_all, preferred_element_type=F32) + qkv_bias
-    mixed_proj = mixed_proj.reshape(blocks, block, heads_local, 3, HD)
-    query_low = rotate(mixed_proj[:, :, :, 0], positions, 1.0).astype(BF16)
-    key_low = rotate(mixed_proj[:, :, :, 1], positions, 1.0).astype(BF16)
-    value_low = mixed_proj[:, :, :, 2].astype(BF16)
-    scores = jnp.einsum(
-        "bqhd,bkhd->bhqk", query_low, key_low, preferred_element_type=F32
-    ) * HD ** (-0.5)
-    scores = jnp.where(allowed[:, None], scores, MASKED)
-    highest = jnp.max(scores, axis=3, keepdims=True)
-    log_total = highest + jnp.log(jnp.sum(jnp.exp(scores - highest), axis=3, keepdims=True))
-    probs_low = jnp.exp(scores - log_total).astype(BF16)
-    attended = jnp.einsum("bhqk,bkhd->bqhd", probs_low, value_low, preferred_element_type=F32)
-    attended = attended.reshape(blocks * block, heads_local * HD).astype(BF16)
-    hidden = jnp.dot(two_low, up_all, preferred_element_type=F32) + up_bias
-    active = jax.nn.gelu(hidden, approximate=False).astype(BF16)
-    joined = jnp.concatenate([attended, active], axis=1)
-    branch_part = jnp.dot(joined, low_all, preferred_element_type=F32).astype(BF16)
-    kept_values = (query_low, key_low, value_low, log_total, hidden, joined)
-    return (branch_part, kept_values)
-
-
 def layer_backward(branch_low, kept_values, weight_set, positions, allowed):
     qkv_all, up_all, low_all = weight_set
-    query_low, key_low, value_low, log_total, hidden, joined = kept_values
-    blocks, block, heads_local, _ = query_low.shape
+    slope, mixed_low, log_total, joined = kept_values
+    blocks, block = positions.shape
+    heads_local = log_total.shape[1]
+    mixed_low = mixed_low.reshape(blocks, block, heads_local, 3, HD)
+    query_low, key_low, value_low = (mixed_low[:, :, :, n] for n in range(3))
+    log_total = log_total.reshape(blocks, block, heads_local).swapaxes(1, 2)[..., None]
     cut = heads_local * HD
     joined_grad = contract_cols(branch_low, low_all)
-    active_grad = joined_grad[:, cut:]
-    cumulative = 0.5 * (1.0 + lax.erf(hidden * 0.7071067811865476))
-    density = jnp.exp(-0.5 * hidden * hidden) * 0.3989422804014327
-    hidden_low = (active_grad * (cumulative + hidden * density)).astype(BF16)
+    hidden_low = (joined_grad[:, cut:] * slope).astype(BF16)
     attended_grad = joined_grad[:, :cut].reshape(blocks, block, heads_local, HD).astype(BF16)
     score_scale = HD ** (-0.5)
     scores = (
@@ -1032,7 +1208,7 @@
         * score_scale
     )
     mixed_grad = jnp.stack(
-        [rotate(query_grad, positions, -1.0), rotate(key_grad, positions, -1.0), value_grad], axis=3
+        [rotate_back(query_grad, positions), rotate_back(key_grad, positions), value_grad], axis=3
     )
     mixed_grad = mixed_grad.reshape(blocks * block, heads_local * 3 * HD).astype(BF16)
     one_part = contract_cols(mixed_grad, qkv_all)
@@ -1060,6 +1236,10 @@
         mean_hat / (jnp.sqrt(square_hat) + ADAM_EPS) + decay_rate * master
     )
     return (mean_new, square_new, master_new)
+
+
+def eight_rows(rows):
+    return jnp.zeros((8, rows.shape[1]), F32).at[: rows.shape[0]].set(rows)
 
 
 def on_device(
@@ -1101,9 +1281,7 @@
     lengths_tile = jnp.zeros((8, 128), jnp.int32).at[0, :SEGS].set(doc_lengths[0])
     masters = tuple(w.astype(BF16) for w in (qkv_master, out_master, up_master, down_master))
     *policy_set, tokens_all, lengths_all = spread_weights(masters, inner, inputs, lengths_tile, 0)
-    frozen_set = spread_weights(
-        (qkv_frozen, out_frozen, up_frozen, down_frozen), inner, None, None, 1
-    )
+    frozen_shards = (qkv_frozen, out_frozen, up_frozen, down_frozen)
     member, _, _ = doc_layout(doc_lengths[0], block)
     _, positions, doc_of = jax.vmap(lambda row: doc_layout(row, block))(lengths_all[:, 0, :SEGS])
     allowed = allowed_keys(doc_of)
@@ -1113,8 +1291,8 @@
 
     def own_bias(bias):
         return (
-            lax.dynamic_slice(bias, (outer_index * width_qkv,), (width_qkv,)),
-            lax.dynamic_slice(bias, (cut + outer_index * width_up,), (width_up,)),
+            lax.dynamic_slice(bias, (outer_index * width_qkv,), (width_qkv,))[None],
+            lax.dynamic_slice(bias, (cut + outer_index * width_up,), (width_up,))[None],
         )
 
     values = f32(tokens_all)
@@ -1123,19 +1301,21 @@
     normed = centre * scale
     one_low = normed_rows(normed, vectors[0], vectors[1])
     two_low = normed_rows(normed, vectors[2], vectors[3])
-    policy_part, kept_values = attention_mlp(
-        one_low, two_low, *own_bias(hidden_bias), policy_set, positions, allowed
-    )
-    final_low = branch_call(inner, policy_part, inputs, vectors[4:6], 2)
-    frozen_part, _ = attention_mlp(
-        normed_rows(normed, vectors_frozen[0], vectors_frozen[1]),
-        normed_rows(normed, vectors_frozen[2], vectors_frozen[3]),
-        *own_bias(hidden_frozen),
-        frozen_set,
-        positions,
-        allowed,
-    )
-    frozen_low = branch_call(inner, frozen_part, inputs, vectors_frozen[4:6], 3)
+    layout = (
+        *turn_tables(positions),
+        doc_of.reshape(-1, 1),
+        doc_of[:, None, :],
+    )
+    final_low, *kept = forward_call(
+        tokens_all, eight_rows(vectors), policy_set, own_bias(hidden_bias), layout, block, inner,
+        True, frozen_shards, 2,
+    )
+    kept_values = tuple(kept[:4])
+    frozen_set = (*kept[4:6], joined_columns(kept[6]))
+    (frozen_low,) = forward_call(
+        tokens_all, eight_rows(vectors_frozen), frozen_set, own_bias(hidden_frozen), layout, block,
+        inner, False, None, 3,
+    )
     vocab_start = lax.axis_index("tensor") * head_weight.shape[1]
     policy_logits, policy_total, policy_pick, chosen = vocab_stats(
         final_low, head_weight, targets, vocab_start
@@ -1154,7 +1334,7 @@
     ).astype(BF16)
     final_part = contract_cols(logit_grad, head_weight)
     final_quarter, branch_low = final_grad_call(final_part, inner, 4)
-    joined = kept_values[5]
+    joined = kept_values[3]
     one_part, two_part, mixed_grad, hidden_low = layer_backward(
         branch_low, kept_values, policy_set, positions, allowed
     )

time: 990 us -> 904 us (0.913)
  matrix products: 208 us -> 142 us
  local copies, waits for them, and re-layouts: 59.7 us -> 33.5 us
  Pallas kernels: 644 us -> 662 us
  other arithmetic: 66.5 us -> 54.6 us
    dot_general x10 -> x1, matrix products: 76.2 us -> 3.79 us  [layer_backward(): jnp.einsum('bqhd,bkhd->bhqk', query_low, key_low, preferred_element_type=...]
    slice x10 -> x4, local copies, waits for them, and re-layouts: 20.3 us -> 3.33 us  [the longest x1 3.21 us: layer_backward(): query_low, key_low, value_low = (mixed_low[:, :, :, n] for n in range(3))]
    pallas_call x4 -> x3, Pallas kernels: 382 us -> 394 us  [the longest x2 260 us: forward_call(): pl.pallas_call(functools.partial(forward_kernel, inner, keep, background)...]
    unnamed x158 -> x93, local copies, waits for them, and re-layouts: 19.6 us -> 9.2 us
where the time goes in v3:
time: 904 us; the launch traced here: 898 us
  Pallas kernels  662 us (73%)
  matrix products  142 us (16%)
  other arithmetic  54.6 us (6%)
  local copies, waits for them, and re-layouts  33.5 us (4%)
    pallas_call x2, Pallas kernels, forward_call(): pl.pallas_call(functools.partial(forward_kernel, inner, keep, background)...  260 us
    pallas_call x1, Pallas kernels, finish_call(): pl.pallas_call(functools.partial(finish_kernel, inner), out_shape=[jax.Sh...  170 us
    pallas_call x1, Pallas kernels, spread_weights(): pl.pallas_call(functools.partial(spread_weights_kernel, inner), out_shape...  133 us
    pallas_call x1, Pallas kernels, final_grad_call(): pl.pallas_call(functools.partial(final_grad_kernel, inner), out_shape=[ja...  78.5 us
    dot_general x4, matrix products, contract_cols(): lax.dot_general(left_rows, right_rows, (((1,), (1,)), ((), ())), preferre...  57.8 us
    dot_general x2, matrix products, vocab_stats(): logits = jnp.dot(final_low, head_weight, preferred_element_type=F32)  45.1 us
    dot_general x3, matrix products, contract_rows(): lax.dot_general(left_rows, right_rows, (((0,), (0,)), ((), ())), preferre...  30.5 us
    pallas_call x1, Pallas kernels, reward_call(): pl.pallas_call(functools.partial(reward_kernel, inner), out_shape=jax.Sha...  19.2 us

profile of v3, /device:TPU:0, one launch (start us, length us, event | category | flops | bytes accessed | tf_op | source)
XLA Modules:
  0.0 897.8 jit_solution(4762454875716643988)
XLA Ops:
  10.3 133.0 %shard_map.436 = (bf16[2048,384]{1,0:T(8,128)(2,1)}, bf16[2048,512]{1,0:T(8,128)(2,1)}, bf16[640,2048]{1,0:T(8,128)(2,1)}, bf16[2048,2048]{1,0:T(8,128)(2,1)}, s32[4,8,128]{2,1,0:T(8,128)}) custom-call(bf16[256,1536]{1,0:T(8,128)(2,1)} %convert_element_type.133.qkv, bf16[512,256]{1,0:T(8,128)(2,1)} %convert_element_type.134.out, ...), custom_call_target="tpu_custom_call" | custom-call | tf_op jit(solution)/shard_map/pallas_call | solution.py:283
  144.4 3.7 multiply_sine_fusion
  153.5 141.9 %shard_map.437 = (bf16[512,2048]{1,0:T(8,128)(2,1)}, f32[2048,512]{1,0:T(8,128)}, bf16[2048,384]{1,0:T(8,128)(2,1)}, f32[2048,1]{1,0:T(8,128)}, bf16[2048,640]{1...) custom-call(bf16[2048,2048]{1,0:T(8,128)(2,1)} %get-tuple-element.116.refs_0_, ...), custom_call_target="tpu_custom_call" | custom-call | tf_op jit(solution)/shard_map/pallas_call | solution.py:595
  298.7 118.6 %shard_map.438 = bf16[512,2048]{1,0:T(8,128)(2,1)} custom-call(bf16[2048,2048]{1,0:T(8,128)(2,1)} %get-tuple-element.116.refs_0_, f32[8,2048]{1,0:T(8,128)} %scatter.36.refs_1_, bf16[2048,384]{1,0:T(8,128)(2,1)} %get-tuple-element.124.refs_2_, bf16[2048,512]{1,0:T(8,128)(2,1)} %get-tuple-element.125.refs_3_, bf16[640,2048]{1,0:T(8,128)(2,1)} %get-tuple-element.126.refs_4_, ...), custom_call_target="tpu_custom_call" | custom-call | tf_op jit(solution)/shard_map/pallas_call | solution.py:595
  417.3 22.7 %fusion.86 = (f32[512]{0:T(512)S(1)}, f32[512,6400]{1,0:T(8,128)}) fusion(bf16[512,2048]{1,0:T(8,128)(2,1)} %shard_map.438, bf16[2048,6400]{1,0:T(8,128)(2,1)} %param.45), kind=kOutput, calls=%fused_computation.153 | convolution fusion | flops 13425049600 | bytes 41420800 | tf_op jit(solution)/shard_map/dot_general | solution.py:1220
  440.0 22.5 %fusion.85 = (f32[512]{0:T(512)S(1)}, f32[512,6400]{1,0:T(8,128)}) fusion(bf16[512,2048]{1,0:T(8,128)(2,1)S(1)} %copy-done.16, bf16[2048,6400]{1,0:T(8,128)(2,1)} %param.45), kind=kOutput, calls=%fused_computation.152 | convolution fusion | flops 13425049600 | bytes 41420800 | tf_op jit(solution)/shard_map/dot_general | solution.py:1220
  462.5 11.5 %fusion.14 = (f32[512]{0:T(512)S(1)}, f32[512]{0:T(512)S(1)}, f32[512]{0:T(512)S(1)}, f32[512]{0:T(512)S(1)}) fusion(f32[512,6400]{1,0:T(8,128)} %get-tuple-element.210, s32[6400]{0:T(1024)S(1)} %iota_add_fusion, s32[512]{0:T(512)S(1)} %copy-done.37, f32[512]{0:T(512)S(1)} %get-tuple-element.209, f32[512,6400]{1,0:T(8,128)} %get-tuple-element.208, ...), kind=kLoop, calls=%fused_computation.20 | loop fusion | flops 29489152 | bytes 26254336 | tf_op jit(solution)/shard_map/reduce_sum | solution.py:1225
  480.6 19.2 %shard_map.439 = f32[2,512]{1,0:T(2,128)} custom-call(f32[8,512]{1,0:T(8,128)} %stack.71.stats_ref, f32[8,512]{1,0:T(8,128)} %pad_convert_fusion.member_ref, f32[8,128]{1,0:T(8,128)} %scatter.40.label_ref), custom_call_target="tpu_custom_call" | custom-call | tf_op jit(solution)/shard_map/pallas_call | solution.py:1088
  500.6 22.4 %fusion.26.part_ref = f32[512,2048]{1,0:T(8,128)} fusion(bf16[2048,6400]{1,0:T(8,128)(2,1)} %param.45, f32[512,6400]{1,0:T(8,128)} %get-tuple-element.208, f32[512]{0:T(512)S(1)} %bitcast.159, f32[512]{0:T(512)S(1)} %bitcast.158, s32[6400]{0:T(1024)S(1)} %iota_add_fusion, s32[512]{0:T(512)S(1)} %copy-done.37), kind=kOutput, calls=%fused_computation.32 | convolution fusion | flops 13441433600 | bytes 43547648 | tf_op jit(solution)/shard_map/dot_general | solution.py:1169
  525.2 78.5 %shard_map.440 = (f32[128,2048]{1,0:T(8,128)S(1)}, bf16[2048,2048]{1,0:T(8,128)(2,1)}) custom-call(f32[512,2048]{1,0:T(8,128)S(1)} %copy-done.1), custom_call_target="tpu_custom_call" | custom-call | tf_op jit(solution)/shard_map/pallas_call | solution.py:715
  603.8 9.8 %fusion.87 = f32[2048,640]{1,0:T(8,128)S(1)} fusion(bf16[2048,2048]{1,0:T(8,128)(2,1)} %get-tuple-element.127, bf16[640,2048]{1,0:T(8,128)(2,1)S(1)} %copy-done.12), kind=kOutput, calls=%fused_computation.154 | convolution fusion | flops 5368709120 | bytes 16252928 | tf_op jit(solution)/shard_map/dot_general | solution.py:1169
  616.4 3.9 reshape.518
  620.3 3.2 fusion.81
  623.6 2.7 fusion.50
  628.0 3.8 multiply_reduce_fusion
  639.8 8.2 fusion.88
  651.6 17.4 %fusion.71 = (f32[2048]{0:T(1024)S(1)}, f32[2048]{0:T(1024)S(1)}, bf16[2048,2048]{1,0:T(8,128)(2,1)}, f32[2048]{0:T(1024)S(1)}, f32[2048]{0:T(1024)S(1)}) fusion(f32[2048]{0:T(1024)S(1)} %add_rsqrt_fusion, f32[2048]{0:T(1024)S(1)} %broadcast_multiply_fusion, bf16[2048,2048]{1,0:T(8,128)(2,1)} %get-tuple-element.116.refs_0_, f32[2048]{0:T(1024)S(1)} %bitcast.155, ...), kind=kOutput, calls=%fused_computation.145 | convolution fusion | flops 4349485056 | bytes 37814272 | tf_op jit(solution)/shard_map/dot_general | solution.py:1169
  669.8 11.0 %fusion.33.up = bf16[2048,512]{1,0:T(8,128)(2,1)} fusion(bf16[2048,512]{1,0:T(8,128)(2,1)} %get-tuple-element.172, bf16[2048,2048]{1,0:T(8,128)(2,1)} %get-tuple-element.116.refs_0_, f32[2048]{0:T(1024)S(1)} %bitcast.154, f32[2048]{0:T(1024)S(1)} %add_rsqrt_fusion, f32[2048]{0:T(1024)S(1)} %broadcast_multiply_fusion, f32[2048]{0:T(1024)S(1)} %bitcast.156), kind=kOutput, calls=%fused_computation.48 | convolution fusion | flops 4321181696 | bytes 12615680 | tf_op jit(solution)/shard_map/dot_general | solution.py:1163
  680.8 10.2 %fusion.36.qkv = bf16[2048,384]{1,0:T(8,128)(2,1)} fusion(bf16[2048,384]{0,1:T(8,128)(2,1)S(1)} %bitcast.126, bf16[2048,2048]{1,0:T(8,128)(2,1)} %get-tuple-element.116.refs_0_, f32[2048]{0:T(1024)S(1)} %bitcast.151, f32[2048]{0:T(1024)S(1)} %add_rsqrt_fusion, f32[2048]{0:T(1024)S(1)} %broadcast_multiply_fusion, f32[2048]{0:T(1024)S(1)} %bitcast.153), kind=kOutput, calls=%fused_computation.49 | convolution fusion | flops 3247177728 | bytes 11567104 | tf_op jit(solution)/shard_map/dot_general | solution.py:1163
  691.0 9.3 %convolution_convert_fusion.low = bf16[640,2048]{1,0:T(8,128)(2,1)} fusion(bf16[2048,640]{1,0:T(8,128)(2,1)S(1)} %copy-done.38, bf16[2048,2048]{1,0:T(8,128)(2,1)} %get-tuple-element.127), kind=kOutput, calls=%fused_computation.43 | convolution fusion | flops 5370019840 | bytes 13631488 | tf_op jit(solution)/shard_map/dot_general | solution.py:1163
  700.4 170.4 %shard_map.441 = (bf16[512,2048]{1,0:T(8,128)(2,1)}, bf16[256,1536]{1,0:T(8,128)(2,1)}, bf16[256,2048]{1,0:T(8,128)(2,1)}, bf16[512,256]{1,0:T(8,128)(2,1)}, bf1...) custom-call(bf16[2048,2048]{1,0:T(8,128)(2,1)} %get-tuple-element.178.part_ref, ...), custom_call_target="tpu_custom_call" | custom-call | tf_op jit(solution)/shard_map/pallas_call | solution.py:996
  876.6 6.5 multiply_subtract_fusion
  883.2 3.9 multiply_subtract_fusion.1
  889.5 3.1 multiply_subtract_fusion.2
  (170 shorter events, 54.5 us)
Async XLA Ops:
  0.7 5.6 copy-start.3
  148.3 4.5 copy-start.28
  153.5 144.6 %copy-start.30 = (f32[6,2048]{1,0:T(8,128)S(1)}, f32[6,2048]{1,0:T(8,128)}, u32[]{:S(2)}) copy-start(f32[6,2048]{1,0:T(8,128)} %param.68) | copy-start | bytes 147460
  417.3 22.7 %copy-start.16 = (bf16[512,2048]{1,0:T(8,128)(2,1)S(1)}, bf16[512,2048]{1,0:T(8,128)(2,1)}, u32[]{:S(2)}) copy-start(bf16[512,2048]{1,0:T(8,128)(2,1)} %get-tuple-element.235) | copy-start | bytes 6291460
  440.0 22.5 %copy-start.37 = (s32[512]{0:T(512)S(1)}, s32[512]{0:T(512)}, u32[]{:S(2)}) copy-start(s32[512]{0:T(512)} %param.42) | copy-start | bytes 6148
  462.5 17.5 %copy-start.39 = (s32[1,4]{1,0:T(1,128)S(1)}, s32[1,4]{1,0:T(1,128)}, u32[]{:S(2)}) copy-start(s32[1,4]{1,0:T(1,128)} %param.44) | copy-start | bytes 52
  525.2 78.5 %copy-start.12 = (bf16[640,2048]{1,0:T(8,128)(2,1)S(1)}, bf16[640,2048]{1,0:T(8,128)(2,1)}, u32[]{:S(2)}) copy-start(bf16[640,2048]{1,0:T(8,128)(2,1)} %get-tuple-element.119.refs_4_) | copy-start | bytes 7864324
  603.7 65.3 %copy-start = (f32[128,2048]{1,0:T(8,128)}, f32[128,2048]{1,0:T(8,128)S(1)}, u32[]{:S(2)}) copy-start(f32[128,2048]{1,0:T(8,128)S(1)} %get-tuple-element.129.quarter_ref) | copy-start | bytes 3145732
  603.8 9.8 %copy-start.11 = (f32[2048,512]{1,0:T(8,128)S(1)}, f32[2048,512]{1,0:T(8,128)}, u32[]{:S(2)}) copy-start(f32[2048,512]{1,0:T(8,128)} %get-tuple-element.128) | copy-start | bytes 12582916
  637.1 10.9 %slice-start = ((s8[8388608]{0:T(1024)(128)(4,1)}), s8[4194304]{0:T(1024)(128)(4,1)S(1)}, s32[]{:S(2)}) async-start(s8[8388608]{0:T(1024)(128)(4,1)} %bitcast.121), calls=%async_computation | async-start | bytes 8388608
  639.8 8.2 slice-start.1
  680.8 10.2 %copy-start.38 = (bf16[2048,640]{1,0:T(8,128)(2,1)S(1)}, bf16[2048,640]{1,0:T(8,128)(2,1)}, u32[]{:S(2)}) copy-start(bf16[2048,640]{1,0:T(8,128)(2,1)} %get-tuple-element.130) | copy-start | bytes 7864324
  700.3 173.2 %copy-start.33 = (f32[3584]{0:T(1024)S(1)}, f32[3584]{0:T(1024)}, u32[]{:S(2)}) copy-start(f32[3584]{0:T(1024)} %param.51) | copy-start | bytes 43012
  700.3 173.2 %copy-start.35 = (f32[3584]{0:T(1024)S(1)}, f32[3584]{0:T(1024)}, u32[]{:S(2)}) copy-start(f32[3584]{0:T(1024)} %param.63) | copy-start | bytes 43012
  700.3 173.2 %copy-start.36 = (f32[3584]{0:T(1024)S(1)}, f32[3584]{0:T(1024)}, u32[]{:S(2)}) copy-start(f32[3584]{0:T(1024)} %param.57) | copy-start | bytes 43012
  700.3 174.7 %copy-start.31 = (f32[6,2048]{1,0:T(8,128)S(1)}, f32[6,2048]{1,0:T(8,128)}, u32[]{:S(2)}) copy-start(f32[6,2048]{1,0:T(8,128)} %param.62) | copy-start | bytes 147460
  700.4 174.7 %copy-start.32 = (f32[6,2048]{1,0:T(8,128)S(1)}, f32[6,2048]{1,0:T(8,128)}, u32[]{:S(2)}) copy-start(f32[6,2048]{1,0:T(8,128)} %param.56) | copy-start | bytes 147460
  700.4 176.2 %copy-start.4 = (f32[2048,256]{1,0:T(8,128)S(1)}, f32[2048,256]{1,0:T(8,128)}, u32[]{:S(2)}) copy-start(f32[2048,256]{1,0:T(8,128)} %param.49) | copy-start | bytes 6291460
  876.6 6.5 copy-start.5
  876.6 6.5 copy-start.20
  876.6 6.5 copy-start.21
  876.6 6.5 copy-start.24
  883.2 5.4 copy-start.23
  883.2 5.4 copy-start.25
  (18 other events, 52.6 us)

commit v4 on v3

--- a/solution.py
+++ b/solution.py
@@ -13,6 +13,7 @@
 STEP = 3
 SPLIT = 4
 QUARTERS = 4
+MEAN, SCALE, FACTS = 6, 7, 8
 AHEAD = 3
 
 
@@ -82,12 +83,12 @@
 
 
 class Spread:
-    def __init__(self, here, shards, wholes, send_o, recv_o, send_i, recv_i, local):
+    def __init__(self, here, shards, wholes, send_o, recv_o, send_i, recv_i, local, *held):
         self.here = here
         self.qkv, self.out, self.up, self.down = shards
         self.qkv_all, self.up_all, self.low_all = wholes
         self.send_o, self.recv_o, self.send_i, self.recv_i = send_o, recv_o, send_i, recv_i
-        self.local = local
+        self.local, self.held = local, held
         self.first, self.own, self.passed = {}, [], []
         self.order = [(m, s) for m in range(4) for s in (2, 1, 3)]
 
@@ -139,12 +140,18 @@
 
     def start_own(self):
         here = self.here
-        for m in range(4):
-            source = self.src(m, here.o)
-            copy = pltpu.make_async_copy(source, self.dst(m, here.dp), self.local.at[m])
+        loads = [
+            pltpu.make_async_copy(self.src(m, here.o), self.held[m], self.local.at[m])
+            for m in range(4)
+        ]
+        for load in loads:
+            load.start()
+        for m, load in enumerate(loads):
+            load.wait()
+            self.pass_on(m, 0, self.held[m], here.dp)
+            copy = pltpu.make_async_copy(self.held[m], self.dst(m, here.dp), self.local.at[4 + m])
             copy.start()
             self.own.append(copy)
-            self.pass_on(m, 0, source, here.dp)
 
     def step(self, number):
         here = self.here
@@ -165,11 +172,13 @@
 
 def spread_weights_kernel(
     inner, qkv, out, up, down, tokens, lengths, qkv_all, up_all, low_all, tokens_all, lengths_all,
-    send_o, recv_o, send_i, recv_i, local, send_t, recv_t, send_l, recv_l,
+    send_o, recv_o, send_i, recv_i, local, held_0, held_1, held_2, held_3,
+    send_t, recv_t, send_l, recv_l,
 ):
     here = Place(inner)
     spread = Spread(
-        here, (qkv, out, up, down), (qkv_all, up_all, low_all), send_o, recv_o, send_i, recv_i, local
+        here, (qkv, out, up, down), (qkv_all, up_all, low_all),
+        send_o, recv_o, send_i, recv_i, local, held_0, held_1, held_2, held_3,
     )
     greet(spread.peers() + [here.far_peer(), here.near_peer()])
     rows, block = tokens.shape[0] // QUARTERS, tokens.shape[0]
@@ -197,10 +206,10 @@
         )
     own.append(
         pltpu.make_async_copy(
-            tokens, tokens_all.at[pl.ds(here.o * block, block), :], local.at[4]
-        )
-    )
-    own.append(pltpu.make_async_copy(lengths, lengths_all.at[here.o], local.at[5]))
+            tokens, tokens_all.at[pl.ds(here.o * block, block), :], local.at[8]
+        )
+    )
+    own.append(pltpu.make_async_copy(lengths, lengths_all.at[here.o], local.at[9]))
     for copy in own:
         copy.start()
     spread.start_own()
@@ -263,14 +272,22 @@
     return low_all
 
 
-def spread_scratch(inner):
+def spread_scratch(shards, inner):
     dma = pltpu.SemaphoreType.DMA
+    qkv, out, up, down = shards
+    pieces = [
+        (qkv.shape[0], qkv.shape[1] // SPLIT),
+        (up.shape[0], up.shape[1] // SPLIT),
+        (out.shape[0] // SPLIT, out.shape[1]),
+        (down.shape[0] // SPLIT, down.shape[1]),
+    ]
     return [
         dma((4, SPLIT - 1)),
         dma((4, SPLIT - 1)),
         dma((4, SPLIT, max(inner - 1, 1))),
         dma((4, SPLIT, max(inner - 1, 1))),
-        dma((6,)),
+        dma((10,)),
+        *(pltpu.VMEM(piece, BF16) for piece in pieces),
     ]
 
 
@@ -283,9 +300,9 @@
     qkv_all, up_all, low_all, *gathered = pl.pallas_call(
         functools.partial(spread_weights_kernel, inner),
         out_shape=shapes,
-        in_specs=[ANY_SPEC] * 6,
+        in_specs=[ANY_SPEC] * 4 + [VMEM_SPEC] * 2,
         out_specs=[ANY_SPEC] * len(shapes),
-        scratch_shapes=spread_scratch(inner)
+        scratch_shapes=spread_scratch(shards, inner)
         + [
             dma((4, SPLIT - 1)),
             dma((4, SPLIT - 1)),
@@ -310,9 +327,14 @@
         self.quarter_sems = sems[6:8]
         self.rows = far_out.shape[1]
         self.near, self.far, self.outer = {}, {}, {}
+        self.slots = None
+
+    def recycle(self, step):
+        for side in range(2):
+            self.near.pop((step, side)).wait_send()
 
     def rows_of(self, step, quarter):
-        block = (self.here.o + 1 + step) % SPLIT
+        block = self.slots[step] if self.slots else (self.here.o + 1 + step) % SPLIT
         return pl.ds((block * QUARTERS + quarter) * self.rows, self.rows)
 
     def start(self, step):
@@ -416,10 +438,11 @@
 
 
 def turn(values, tables, where, direction):
-    cosine, sine_first, sine_second = (table[where, :] for table in tables)
+    cosine, sine = (table[where, :] for table in tables)
     ahead = pltpu.roll(values, values.shape[1] - ROT // 2, 1)
     behind = pltpu.roll(values, ROT // 2, 1)
-    return values * cosine + direction * (ahead * sine_first + behind * sine_second)
+    first = lax.broadcasted_iota(jnp.int32, values.shape, 1) < ROT // 2
+    return values * cosine + direction * (jnp.where(first, ahead, behind) * sine)
 
 
 def row_tiles(start, count, tile, body):
@@ -430,14 +453,16 @@
 
 def forward_kernel(inner, keep, background, *refs):
     here = Place(inner)
-    (tokens_ref, rows_ref, qkv_ref, up_ref, low_ref, qkv_bias, up_bias, cosine, sine_first,
-     sine_second, doc_col, doc_row, *refs) = refs
-    tables = (cosine, sine_first, sine_second)
+    (tokens_ref, rows_ref, qkv_ref, up_ref, low_ref, qkv_bias, up_bias, cosine, sine,
+     doc_col, doc_row, *refs) = refs
+    if not keep:
+        facts_ref, *refs = refs
+    tables = (cosine, sine)
     shards = refs[:4] if background else []
     refs = refs[len(shards):]
     final_ref, *refs = refs
     if keep:
-        slope_ref, mixed_ref, total_ref, joined_ref, *refs = refs
+        slope_ref, mixed_ref, facts_ref, joined_ref, *refs = refs
     wholes = refs[:3] if background else []
     refs = refs[len(wholes):]
     if not keep:
@@ -471,9 +496,17 @@
 
         def norm(where, own):
             values = f32(tokens_ref[where, :])
-            centre = values - jnp.mean(values, axis=1, keepdims=True)
-            spread_of = jnp.mean(centre * centre, axis=1, keepdims=True)
-            normed = centre * lax.rsqrt(spread_of + EPS_NORM)
+            if keep:
+                mean = jnp.mean(values, axis=1, keepdims=True)
+                centre = values - mean
+                scale = lax.rsqrt(jnp.mean(centre * centre, axis=1, keepdims=True) + EPS_NORM)
+                facts_ref[where, MEAN : MEAN + 1] = mean
+                facts_ref[where, SCALE : SCALE + 1] = scale
+                normed = centre * scale
+            else:
+                normed = (values - facts_ref[where, MEAN : MEAN + 1]) * facts_ref[
+                    where, SCALE : SCALE + 1
+                ]
             one_ref[own, :] = (normed * rows_ref[0:1, :] + rows_ref[1:2, :]).astype(BF16)
             two_ref[own, :] = (normed * rows_ref[2:3, :] + rows_ref[3:4, :]).astype(BF16)
 
@@ -515,7 +548,7 @@
                     jnp.sum(jnp.exp(scores - highest), axis=1, keepdims=True)
                 )
                 if keep:
-                    total_ref[tokens_at, head : head + 1] = total
+                    facts_ref[tokens_at, head : head + 1] = total
                 probs = jnp.exp(scores - total).astype(BF16)
                 joined_ref[queries, head * HD : (head + 1) * HD] = dot(
                     probs, mixed_ref[keys, at + 2 * HD : at + 3 * HD]
@@ -557,17 +590,16 @@
         spread.finish()
 
 
-def forward_call(tokens, rows, weights, biases, layout, block, inner, keep, shards, number):
+def forward_call(tokens, rows, weights, biases, layout, block, inner, facts, shards, number):
     total_rows, d_model = tokens.shape
     qkv_all, up_all, low_all = weights
-    heads = qkv_all.shape[1] // (3 * HD)
-    background = shards is not None
+    background, keep = shards is not None, facts is None
     outs = [jax.ShapeDtypeStruct((block, d_model), BF16)]
     if keep:
         outs += [
             jax.ShapeDtypeStruct((total_rows, up_all.shape[1]), F32),
             jax.ShapeDtypeStruct((total_rows, qkv_all.shape[1]), BF16),
-            jax.ShapeDtypeStruct((total_rows, heads), F32),
+            jax.ShapeDtypeStruct((total_rows, FACTS), F32),
             jax.ShapeDtypeStruct((total_rows, low_all.shape[0]), BF16),
         ]
     specs = [VMEM_SPEC] * len(outs)
@@ -585,13 +617,15 @@
     ]
     scratch += reduce_scratch(block // QUARTERS, d_model)
     operands = [tokens, rows, qkv_all, up_all, low_all, *biases, *layout]
+    if not keep:
+        operands.append(facts)
     in_specs = [VMEM_SPEC] * len(operands)
     if background:
         operands += shards
         in_specs += [ANY_SPEC] * 4
         outs += whole_shapes(shards, inner)
         specs += [ANY_SPEC] * 3
-        scratch += spread_scratch(inner)
+        scratch += spread_scratch(shards, inner)
     return pl.pallas_call(
         functools.partial(forward_kernel, inner, keep, background),
         out_shape=outs,
@@ -633,111 +667,253 @@
     ]
 
 
-def final_grad_kernel(
-    inner, part_ref, quarter_ref, branch_all, near_in, far_in, far_out, low, near_out,
-    near_send, near_recv, far_send, far_recv, send, recv, local,
+def dot_rows(left, right):
+    return lax.dot_general(left, right, (((0,), (0,)), ((), ())), preferred_element_type=F32)
+
+
+def backward_kernel(
+    inner, final_part, tokens_hbm, rows_ref, qkv_ref, up_ref, low_ref, slope_ref, mixed_ref,
+    facts_ref, cosine, sine, doc_col, doc_row,
+    grad_ref, branch_all, mixed_grad, hidden_grad, rows_out, bias_out,
+    near_in, far_in, far_out, low, quarter, tokens_ref, own_tokens, joined_ref, key_ref, value_ref,
+    part_ref,
+    near_send, near_recv, far_send, far_recv, send, recv, local, *scratch,
 ):
     here = Place(inner)
-    rows = quarter_ref.shape[0]
+    tables = (cosine, sine)
+    sums = RowSum(here, part_ref, *scratch)
+    rows = sums.rows
+    block = rows * QUARTERS
+    heads = qkv_ref.shape[1] // (3 * HD)
+    cut = heads * HD
     greet(reduce_peers(here))
 
-    def rows_of(quarter):
-        return pl.ds(quarter * rows, rows)
+    def rows_of(number):
+        return pl.ds(pl.multiple_of(number * rows, rows), rows)
 
     near = []
-    for side, quarter in enumerate(((here.near + 2) % QUARTERS, here.near)):
-        near_out[side] = part_ref[rows_of(quarter), :].astype(BF16)
+    for side, number in enumerate(((here.near + 2) % QUARTERS, here.near)):
         near.append(
             remote(
-                near_out.at[side],
+                final_part.at[rows_of(number), :],
                 near_in.at[side],
                 near_send.at[side],
                 near_recv.at[side],
                 here.near_peer(),
             )
         )
+
+    shifts = (1, 3, 2, 0)
+
+    def fetch(position):
+        copy = pltpu.make_async_copy(
+            tokens_hbm.at[pl.ds(((here.o + SPLIT - shifts[position]) % SPLIT) * block, block), :],
+            tokens_ref,
+            local.at[0],
+        )
+        copy.start()
+        return copy
+
+    fetched = fetch(0)
+    own_copy = pltpu.make_async_copy(
+        tokens_hbm.at[rows_of(here.o * QUARTERS + here.t), :], own_tokens, local.at[1]
+    )
+    own_copy.start()
     near[0].wait_recv()
-    far_out[...] = (part_ref[rows_of(here.far), :] + f32(near_in[0])).astype(BF16)
+    far_out[...] = (f32(final_part[rows_of(here.far), :]) + f32(near_in[0])).astype(BF16)
     far = remote(far_out, far_in, far_send, far_recv, here.far_peer())
     near[1].wait_recv()
     far.wait_recv()
-    quarter_ref[...] = part_ref[rows_of(here.t), :] + f32(near_in[1]) + f32(far_in[...])
-    low[...] = quarter_ref[...].astype(BF16)
+    quarter[...] = f32(final_part[rows_of(here.t), :]) + f32(near_in[1]) + f32(far_in[...])
+    low[...] = quarter[...].astype(BF16)
+    rows_out[...] = jnp.zeros_like(rows_out)
+    bias_out[...] = jnp.zeros_like(bias_out)
+    rows_out[4:5, :] = jnp.sum(f32(low[...]), axis=0, keepdims=True)
+
+    def piece(s, number):
+        part = (here.o + SPLIT - s) % SPLIT
+        return branch_all.at[rows_of(part * QUARTERS + number), :]
+
+    outer, across, beside, beyond = {}, {}, {}, {}
+
+    def send_out(s):
+        outer[s] = remote(low, piece(0, here.t), send.at[0, s], recv.at[0, s], here.outer_peer(s))
+
+    send_out(1)
+    send_out(3)
+    own = pltpu.make_async_copy(low, piece(0, here.t), local.at[2])
+    own.start()
+
+    def arrived(s):
+        if s:
+            outer[s].wait_recv()
+        if s == 1:
+            send_out(2)
+        source = piece(s, here.t) if s else low
+        across[s] = remote(
+            source, piece(s, here.t), send.at[1, s], recv.at[1, s], here.far_peer()
+        )
+        beside[s] = remote(
+            source, piece(s, here.t), send.at[2, s], recv.at[2, s], here.near_peer()
+        )
+
+    def crossed(s):
+        across[s].wait_recv()
+        beyond[s] = remote(
+            piece(s, here.far), piece(s, here.far), send.at[3, s], recv.at[3, s], here.near_peer()
+        )
+
+    arrived(0)
+    crossed(0)
+    arrived(1)
+    crossed(1)
+    own.wait()
+    steps = [SPLIT - 1 - s for s in shifts]
+    sums.slots = {step: position % 2 for position, step in enumerate(steps)}
+    events = [
+        (arrived, 3), None, (crossed, 3), (arrived, 2), None, (crossed, 2),
+    ]
+
+    def serve():
+        event = events.pop(0) if events else None
+        if event:
+            event[0](event[1])
+
+    for position, s in enumerate(shifts):
+        step = steps[position]
+        part = (here.o + SPLIT - s) % SPLIT
+        start = pl.multiple_of(part * block, block)
+        whole = pl.ds(start, block)
+        beside[s].wait_recv()
+        beyond[s].wait_recv()
+        joined_ref[...] = dot_cols(branch_all[whole, :], low_ref[...])
+
+        def activate(where, mine):
+            hidden_grad[where, :] = (joined_ref[mine, cut:] * slope_ref[where, :]).astype(BF16)
+
+        row_tiles(start, block, 64, activate)
+        serve()
+        if position:
+            sums.across(steps[position - 1])
+        for head in range(heads):
+            at = head * 3 * HD
+            key_ref[...] = jnp.zeros_like(key_ref)
+            value_ref[...] = jnp.zeros_like(value_ref)
+            for first in range(0, block, 128):
+                queries = pl.ds(pl.multiple_of(start + first, 128), 128)
+                width = first + 128
+                keys = pl.ds(start, width)
+                query = mixed_ref[queries, at : at + HD]
+                key = mixed_ref[keys, at + HD : at + 2 * HD]
+                scores = dot_cols(query, key) * HD ** (-0.5)
+                same = doc_col[queries, :] == doc_row[part][:, :width]
+                earlier = first + lax.broadcasted_iota(
+                    jnp.int32, scores.shape, 0
+                ) >= lax.broadcasted_iota(jnp.int32, scores.shape, 1)
+                scores = jnp.where(same & earlier, scores, MASKED)
+                probs = jnp.exp(scores - facts_ref[queries, head : head + 1])
+                attended_grad = joined_ref[
+                    first : first + 128, head * HD : (head + 1) * HD
+                ].astype(BF16)
+                prob_grad = dot_cols(attended_grad, mixed_ref[keys, at + 2 * HD : at + 3 * HD])
+                mean = jnp.sum(probs * prob_grad, axis=1, keepdims=True)
+                score_grad = (probs * (prob_grad - mean)).astype(BF16)
+                mixed_grad[queries, at : at + HD] = turn(
+                    dot(score_grad, key) * HD ** (-0.5), tables, queries, -1.0
+                ).astype(BF16)
+                key_ref[:width, :] += dot_rows(score_grad, query)
+                value_ref[:width, :] += dot_rows(probs.astype(BF16), attended_grad)
+            mixed_grad[whole, at + HD : at + 2 * HD] = turn(
+                key_ref[...] * HD ** (-0.5), tables, whole, -1.0
+            ).astype(BF16)
+            mixed_grad[whole, at + 2 * HD : at + 3 * HD] = value_ref[...].astype(BF16)
+        bias_out[0:1, : mixed_grad.shape[1]] += jnp.sum(
+            f32(mixed_grad[whole, :]), axis=0, keepdims=True
+        )
+        bias_out[0:1, mixed_grad.shape[1] :] += jnp.sum(
+            f32(hidden_grad[whole, :]), axis=0, keepdims=True
+        )
+        serve()
+        if position > 1:
+            sums.along(steps[position - 2])
+            sums.recycle(steps[position - 2])
+        fetched.wait()
+        columns = 256
+        target = pl.ds((position % 2) * block, block)
+
+        @pl.loop(0, part_ref.shape[1] // columns)
+        def _(n):
+            at = pl.ds(pl.multiple_of(n * columns, columns), columns)
+            one = dot_cols(mixed_grad[whole, :], qkv_ref[at, :])
+            two = dot_cols(hidden_grad[whole, :], up_ref[at, :])
+            normed = (f32(tokens_ref[:, at]) - facts_ref[whole, MEAN : MEAN + 1]) * facts_ref[
+                whole, SCALE : SCALE + 1
+            ]
+            part_ref[target, at] = (one * rows_ref[0:1, at] + two * rows_ref[2:3, at]).astype(BF16)
+            for row, value in enumerate((one * normed, one, two * normed, two)):
+                rows_out[row : row + 1, at] += jnp.sum(value, axis=0, keepdims=True)
+
+        sums.start(step)
+        if position + 1 < SPLIT:
+            fetched = fetch(position + 1)
+        serve()
+    sums.across(steps[3])
+    sums.along(steps[2])
+    sums.along(steps[3])
+    own_copy.wait()
+    change = input_change(f32(own_tokens[...]), sums.value())
+    grad_ref[rows_of(here.t), :] = (quarter[...] + change).astype(BF16)
+    gather_quarters(here, grad_ref, rows, *sums.quarter_sems)
+    sums.finish()
     for copy in near + [far]:
         copy.wait_send()
-
-    def piece(part, quarter):
-        return branch_all.at[pl.ds((part * QUARTERS + quarter) * rows, rows), :]
-
-    outer = [
-        remote(
-            low, piece(here.o, here.t), send.at[0, s], recv.at[0, s], here.outer_peer(s)
-        )
-        for s in range(1, SPLIT)
-    ]
-    own = pltpu.make_async_copy(low, piece(here.o, here.t), local)
-    own.start()
-    across, beside = [], []
-    for s in range(SPLIT):
-        part = (here.o + SPLIT - s) % SPLIT
-        if s:
-            outer[s - 1].wait_recv()
-        source = piece(part, here.t) if s else low
-        across.append(
-            remote(source, piece(part, here.t), send.at[1, s], recv.at[1, s], here.far_peer())
-        )
-        beside.append(
-            remote(source, piece(part, here.t), send.at[2, s], recv.at[2, s], here.near_peer())
-        )
-    for s in range(SPLIT):
-        part = (here.o + SPLIT - s) % SPLIT
-        across[s].wait_recv()
-        beside.append(
-            remote(
-                piece(part, here.far),
-                piece(part, here.far),
-                send.at[3, s],
-                recv.at[3, s],
-                here.near_peer(),
-            )
-        )
-    for copy in beside:
-        copy.wait_recv()
-    for copy in outer + across + beside:
-        copy.wait_send()
-    own.wait()
-
-
-def final_grad_call(part, inner, number):
+    for copies in (outer, across, beside, beyond):
+        for copy in copies.values():
+            copy.wait_send()
+
+
+def backward_call(part, tokens, rows, weights, kept, layout, inner, number):
     block, width = part.shape
-    rows = block // QUARTERS
+    quarter = block // QUARTERS
+    slope, mixed, facts, joined = kept
     dma = pltpu.SemaphoreType.DMA
     return pl.pallas_call(
-        functools.partial(final_grad_kernel, inner),
+        functools.partial(backward_kernel, inner),
         out_shape=[
-            jax.ShapeDtypeStruct((rows, width), F32),
+            jax.ShapeDtypeStruct((block, width), BF16),
             jax.ShapeDtypeStruct((SPLIT * block, width), BF16),
+            jax.ShapeDtypeStruct(mixed.shape, BF16),
+            jax.ShapeDtypeStruct(slope.shape, BF16),
+            jax.ShapeDtypeStruct(rows.shape, F32),
+            jax.ShapeDtypeStruct((1, mixed.shape[1] + slope.shape[1]), F32),
         ],
-        in_specs=[VMEM_SPEC],
-        out_specs=[VMEM_SPEC, ANY_SPEC],
+        in_specs=[VMEM_SPEC, ANY_SPEC] + [VMEM_SPEC] * 11,
+        out_specs=[VMEM_SPEC] * 6,
         scratch_shapes=[
-            pltpu.VMEM((2, rows, width), BF16),
-            pltpu.VMEM((rows, width), BF16),
-            pltpu.VMEM((rows, width), BF16),
-            pltpu.VMEM((rows, width), BF16),
-            pltpu.VMEM((2, rows, width), BF16),
+            pltpu.VMEM((2, quarter, width), BF16),
+            pltpu.VMEM((quarter, width), BF16),
+            pltpu.VMEM((quarter, width), BF16),
+            pltpu.VMEM((quarter, width), BF16),
+            pltpu.VMEM((quarter, width), F32),
+            pltpu.VMEM((block, width), BF16),
+            pltpu.VMEM((quarter, width), BF16),
+            pltpu.VMEM((block, joined.shape[1]), F32),
+            pltpu.VMEM((block, HD), F32),
+            pltpu.VMEM((block, HD), F32),
+            pltpu.VMEM((2 * block, width), BF16),
             dma((2,)),
             dma((2,)),
             dma,
             dma,
             dma((4, SPLIT)),
             dma((4, SPLIT)),
-            dma,
-        ],
+            dma((3,)),
+        ]
+        + reduce_scratch(quarter, width),
         compiler_params=pltpu.CompilerParams(
-            collective_id=number, has_side_effects=True, vmem_limit_bytes=48 * 1024 * 1024
+            collective_id=number, has_side_effects=True, vmem_limit_bytes=60 * 1024 * 1024
         ),
-    )(part)
+    )(part, tokens, rows, *weights, slope, mixed, facts, *layout)
 
 
 class AllSum:
@@ -821,29 +997,39 @@
 
 
 def finish_kernel(
-    inner, part_ref, tokens_ref, quarter_ref, qkv, up, low, rows_ref, bias_ref,
-    grad_ref, qkv_out, up_out, out_out, down_out, rows_out, bias_out, norm_ref, *scratch,
+    inner, tokens_ref, branch_ref, gains_ref, joined_ref, mixed_ref, hidden_ref, facts_ref,
+    rows_ref, bias_ref, qkv_out, up_out, out_out, down_out, rows_out, bias_out, norm_ref, *scratch,
 ):
     here = Place(inner)
-    sums = RowSum(here, part_ref, *scratch[:14])
-    inputs, sends = scratch[14:18], scratch[18:22]
-    send_i, recv_i, send_o, recv_o, local = scratch[22:27]
-    small = AllSum(here, *scratch[27:34])
-    squares = AllSum(here, *scratch[34:41])
-    bias_in, bias_send, bias_recv = scratch[41:44]
+    sends, inputs, totals = scratch[:3], scratch[3:6], scratch[6:9]
+    turned, send_i, recv_i, send_o, recv_o, local, held = scratch[9:16]
+    small = AllSum(here, *scratch[16:23])
+    squares = AllSum(here, *scratch[23:30])
+    bias_in, bias_send, bias_recv = scratch[30:33]
     outs = (qkv_out, up_out, out_out, down_out)
     shard = qkv_out.shape[0]
     width_out = out_out.shape[0] // SPLIT
-    width_down = down_out.shape[0] // SPLIT
-
-    def src(m, index):
-        where = pl.ds(index * shard, shard)
-        if m == 0:
-            return qkv.at[where, :]
-        if m == 1:
-            return up.at[where, :]
-        rows = pl.ds(0, width_out) if m == 2 else pl.ds(width_out, width_down)
-        return low.at[rows, where] if aligned(shard) else low.at[index, rows, :]
+
+    def columns_of(ref, index):
+        if ref.ndim == 3:
+            return ref[index]
+        return ref[:, pl.ds(pl.multiple_of(index * shard, shard), shard)]
+
+    def gradient(kind, index):
+        if kind == 2:
+            return dot(turned[...], columns_of(branch_ref, index))
+        if tokens_ref.ndim == 3:
+            copy = pltpu.make_async_copy(tokens_ref.at[index], held, local.at[4])
+            copy.start()
+            copy.wait()
+            values = f32(held[...])
+        else:
+            values = f32(columns_of(tokens_ref, index))
+        normed = (values - facts_ref[:, MEAN : MEAN + 1]) * facts_ref[:, SCALE : SCALE + 1]
+        rows = columns_of(gains_ref, index)
+        at = 2 * kind
+        layer_in = (normed * rows[at : at + 1, :] + rows[at + 1 : at + 2, :]).astype(BF16)
+        return dot_rows(layer_in, (mixed_ref, hidden_ref)[kind][...])
 
     def dst(m):
         if m < 2:
@@ -852,56 +1038,57 @@
         width = outs[m].shape[0] // SPLIT
         return outs[m].at[pl.ds(here.o * width, width), :]
 
-    peers = reduce_peers(here) + [here.inner_peer(r) for r in range(1, inner)]
-    greet(peers)
+    greet(reduce_peers(here) + [here.inner_peer(r) for r in range(1, inner)])
     first, last, own = {}, [], []
-
-    order = [(m, s) for m in (2, 3, 1, 0) for s in (2, 1, 3, 0)]
+    order = [(kind, s) for kind in (2, 1, 0) for s in (2, 1, 3, 0)]
+    turned[...] = jnp.transpose(joined_ref[...])
 
     def trade(number):
         if number >= len(order):
             return
-        m, s = order[number]
+        kind, s = order[number]
         part = (here.o + s) % SPLIT
         for r in range(1, inner):
-            first[m, s, r] = remote(
-                src(m, part * inner + (here.i + r) % inner),
-                inputs[m].at[s, r - 1],
-                send_i.at[m, s, r - 1],
-                recv_i.at[m, s, r - 1],
+            sends[kind][s, r - 1] = gradient(kind, part * inner + (here.i + r) % inner).astype(BF16)
+            first[kind, s, r] = remote(
+                sends[kind].at[s, r - 1],
+                inputs[kind].at[s, r - 1],
+                send_i.at[kind, s, r - 1],
+                recv_i.at[kind, s, r - 1],
                 here.inner_peer(r),
             )
 
     def settle(number):
-        m, s = order[number]
+        kind, s = order[number]
         part = (here.o + s) % SPLIT
-        total = f32(src(m, part * inner + here.i)[...])
+        total = gradient(kind, part * inner + here.i)
         for r in range(1, inner):
-            first[m, s, r].wait_recv()
+            first[kind, s, r].wait_recv()
+            total = total + f32(inputs[kind][s, r - 1])
+        totals[kind][s] = total.astype(BF16)
+        source = totals[kind].at[s]
+        pieces = [(kind, source)]
+        if kind == 2:
+            pieces = [
+                (2, source.at[pl.ds(0, width_out), :]),
+                (3, source.at[pl.ds(width_out, total.shape[0] - width_out), :]),
+            ]
+        for m, piece in pieces:
+            if s:
+                last.append(
+                    remote(
+                        piece, dst(m), send_o.at[m, s - 1], recv_o.at[m, s - 1], here.outer_peer(s)
+                    )
+                )
+            else:
+                copy = pltpu.make_async_copy(piece, dst(m), local.at[m])
+                copy.start()
+                own.append(copy)
         trade(number + AHEAD)
-        for r in range(1, inner):
-            total = total + f32(inputs[m][s, r - 1])
-        sends[m][s] = total.astype(BF16)
-        if s:
-            last.append(
-                remote(
-                    sends[m].at[s],
-                    dst(m),
-                    send_o.at[m, s - 1],
-                    recv_o.at[m, s - 1],
-                    here.outer_peer(s),
-                )
-            )
-        else:
-            copy = pltpu.make_async_copy(sends[m].at[0], dst(m), local.at[m])
-            copy.start()
-            own.append(copy)
         return whole_sum(total * total)
 
     for number in range(AHEAD):
         trade(number)
-    for step in range(SPLIT):
-        sums.start(step)
     small.near(rows_ref[...])
     bias_in[here.i] = bias_ref[...]
     bias_inner = [
@@ -916,13 +1103,9 @@
     ]
     square = settle(0)
     square = square + settle(1)
-    for step in range(SPLIT):
-        sums.across(step)
-        square = square + settle(2 + step)
     small.far()
-    sums.along(0)
-    square = square + settle(6)
-    square = square + settle(7)
+    for number in range(2, 5):
+        square = square + settle(number)
     small.along_outer()
     for copy in bias_inner:
         copy.wait_recv()
@@ -941,16 +1124,13 @@
         for s in range(1, SPLIT)
     ]
     square = square + whole_sum(bias * bias) / inner
-    sums.along(1)
+    square = square + settle(5)
+    square = square + settle(6)
+    small.along_inner()
+    square = square + settle(7)
     square = square + settle(8)
-    square = square + settle(9)
-    small.along_inner()
-    sums.along(2)
-    square = square + settle(10)
-    square = square + settle(11)
     rows_out[...] = small.value()
-    sums.along(3)
-    for number in range(12, len(order)):
+    for number in range(9, len(order)):
         square = square + settle(number)
     squares.near(jnp.broadcast_to(square, norm_ref.shape))
     squares.far()
@@ -960,11 +1140,6 @@
     rows = rows_out[...]
     doubled = lax.broadcasted_iota(jnp.int32, rows.shape, 0) == 4
     norm_ref[...] = norm + whole_sum(rows * rows * jnp.where(doubled, 2.0, 1.0))
-    mine = pl.ds(here.t * sums.rows, sums.rows)
-    change = input_change(f32(tokens_ref[mine, :]), sums.value())
-    grad_ref[mine, :] = (quarter_ref[...] + change).astype(BF16)
-    gather_quarters(here, grad_ref, sums.rows, *sums.quarter_sems)
-    sums.finish()
     for copy in bias_outer:
         copy.wait_recv()
     for copy in bias_inner + bias_outer:
@@ -977,44 +1152,45 @@
         copy.wait_send()
 
 
-def finish_call(part, tokens, quarter, grads, rows, bias, shards, inner, number):
+def finish_call(tokens, branch, rows, kept, grads, sums, bias, shards, inner, number):
     dma = pltpu.SemaphoreType.DMA
     qkv, out, up, down = shards
     ordered = (qkv, up, out, down)
-    if not aligned(out[1]):
-        low = grads[2].reshape(grads[2].shape[0], SPLIT * inner, out[1])
-        grads = (*grads[:2], jnp.swapaxes(low, 0, 1))
+    facts, joined = kept
+    shard = out[1]
+    wide = [tokens, branch, rows]
+    if not aligned(shard):
+        wide = [jnp.swapaxes(w.reshape(w.shape[0], -1, shard), 0, 1) for w in wide]
     pieces = [
-        (qkv[0], qkv[1] // SPLIT),
-        (up[0], up[1] // SPLIT),
-        (out[0] // SPLIT, out[1]),
-        (down[0] // SPLIT, down[1]),
+        (shard, grads[0].shape[1]),
+        (shard, grads[1].shape[1]),
+        (joined.shape[1], shard),
     ]
     peers = max(inner - 1, 1)
-    block, width = tokens.shape
     tile = (8, 128)
     return pl.pallas_call(
         functools.partial(finish_kernel, inner),
         out_shape=[
-            jax.ShapeDtypeStruct((block, width), BF16),
             *(jax.ShapeDtypeStruct(shape, BF16) for shape in ordered),
-            jax.ShapeDtypeStruct(rows.shape, F32),
+            jax.ShapeDtypeStruct(sums.shape, F32),
             jax.ShapeDtypeStruct((SPLIT, *bias.shape), F32),
             jax.ShapeDtypeStruct(tile, F32),
         ],
-        in_specs=[VMEM_SPEC] * 8,
-        out_specs=[VMEM_SPEC] + [ANY_SPEC] * 4 + [VMEM_SPEC] * 3,
-        scratch_shapes=reduce_scratch(block // QUARTERS, width)
+        in_specs=[VMEM_SPEC if aligned(shard) else ANY_SPEC] + [VMEM_SPEC] * 8,
+        out_specs=[ANY_SPEC] * 4 + [VMEM_SPEC] * 3,
+        scratch_shapes=[pltpu.VMEM((SPLIT, peers, *piece), BF16) for piece in pieces]
         + [pltpu.VMEM((SPLIT, peers, *piece), BF16) for piece in pieces]
         + [pltpu.VMEM((SPLIT, *piece), BF16) for piece in pieces]
         + [
-            dma((4, SPLIT, peers)),
-            dma((4, SPLIT, peers)),
+            pltpu.VMEM(joined.shape[::-1], BF16),
+            dma((3, SPLIT, peers)),
+            dma((3, SPLIT, peers)),
             dma((4, SPLIT - 1)),
             dma((4, SPLIT - 1)),
-            dma((4,)),
+            dma((5,)),
+            pltpu.VMEM((16, 128) if aligned(shard) else (tokens.shape[0], shard), BF16),
         ]
-        + all_sum_scratch(rows.shape, inner)
+        + all_sum_scratch(sums.shape, inner)
         + all_sum_scratch(tile, inner)
         + [
             pltpu.VMEM((inner, *bias.shape), F32),
@@ -1024,7 +1200,7 @@
         compiler_params=pltpu.CompilerParams(
             collective_id=number, has_side_effects=True, vmem_limit_bytes=60 * 1024 * 1024
         ),
-    )(part, tokens, quarter, *grads, rows, bias)
+    )(*wide, joined, *grads, facts, sums, bias)
 
 
 def reward_kernel(
@@ -1071,8 +1247,10 @@
     sigmoid_value = 1.0 / (1.0 + jnp.exp(-BETA_KTO * (reward - shift)))
     labels = label_ref[:, 0:1]
     doc_grad = BETA_KTO * sigmoid_value * (1.0 - sigmoid_value) * (1.0 - 2.0 * labels) / seq_count
-    out_ref[0:1, :] = jnp.sum(member * doc_grad, axis=0, keepdims=True)
-    out_ref[1:2, :] = totals[0:1, :]
+    token_grad = jnp.sum(member * doc_grad, axis=0, keepdims=True)
+    out_ref[...] = jnp.transpose(
+        jnp.concatenate([token_grad, totals[0:1, :], jnp.zeros((6, totals.shape[1]), F32)], axis=0)
+    )
     for copy in copies + more + rest:
         copy.wait_send()
 
@@ -1087,7 +1265,7 @@
     peers = max(inner - 1, 1)
     return pl.pallas_call(
         functools.partial(reward_kernel, inner),
-        out_shape=jax.ShapeDtypeStruct((2, stats.shape[1]), F32),
+        out_shape=jax.ShapeDtypeStruct((stats.shape[1], 8), F32),
         in_specs=[VMEM_SPEC] * 3,
         out_specs=VMEM_SPEC,
         scratch_shapes=[
@@ -1111,29 +1289,9 @@
     angles = positions.reshape(-1).astype(F32)[:, None] * frequency
     cosine, sine = jnp.cos(angles), jnp.sin(angles)
     none = jnp.zeros((angles.shape[0], HD - ROT), F32)
-    empty = jnp.zeros_like(sine)
     return (
         jnp.concatenate([cosine, cosine, none + 1.0], axis=1),
-        jnp.concatenate([-sine, empty, none], axis=1),
-        jnp.concatenate([empty, sine, none], axis=1),
-    )
-
-
-def rotate_back(values, positions):
-    half_rot = ROT // 2
-    frequency = 10000.0 ** (-2.0 * jnp.arange(half_rot, dtype=F32) / ROT)
-    angles = positions.astype(F32)[..., None] * frequency
-    cosine = jnp.cos(angles)[..., None, :]
-    sine_part = -jnp.sin(angles)[..., None, :]
-    first_half = values[..., :half_rot]
-    second_half = values[..., half_rot:ROT]
-    return jnp.concatenate(
-        [
-            first_half * cosine - second_half * sine_part,
-            second_half * cosine + first_half * sine_part,
-            values[..., ROT:],
-        ],
-        axis=-1,
+        jnp.concatenate([-sine, sine, none], axis=1),
     )
 
 
@@ -1152,78 +1310,153 @@
     return (member, positions, doc_of)
 
 
-def allowed_keys(doc_of):
-    index_rows = jnp.arange(doc_of.shape[-1], dtype=jnp.int32)
-    return (doc_of[..., :, None] == doc_of[..., None, :]) & (
-        index_rows[:, None] >= index_rows[None, :]
-    )
-
-
-def contract_rows(left_rows, right_rows):
-    return lax.dot_general(
-        left_rows, right_rows, (((0,), (0,)), ((), ())), preferred_element_type=F32
-    )
-
-
-def contract_cols(left_rows, right_rows):
-    return lax.dot_general(
-        left_rows, right_rows, (((1,), (1,)), ((), ())), preferred_element_type=F32
-    )
-
-
-def normed_rows(normed, gain_row, shift_row):
-    return (normed * gain_row + shift_row).astype(BF16)
-
-
-def layer_backward(branch_low, kept_values, weight_set, positions, allowed):
-    qkv_all, up_all, low_all = weight_set
-    slope, mixed_low, log_total, joined = kept_values
-    blocks, block = positions.shape
-    heads_local = log_total.shape[1]
-    mixed_low = mixed_low.reshape(blocks, block, heads_local, 3, HD)
-    query_low, key_low, value_low = (mixed_low[:, :, :, n] for n in range(3))
-    log_total = log_total.reshape(blocks, block, heads_local).swapaxes(1, 2)[..., None]
-    cut = heads_local * HD
-    joined_grad = contract_cols(branch_low, low_all)
-    hidden_low = (joined_grad[:, cut:] * slope).astype(BF16)
-    attended_grad = joined_grad[:, :cut].reshape(blocks, block, heads_local, HD).astype(BF16)
-    score_scale = HD ** (-0.5)
-    scores = (
-        jnp.einsum("bqhd,bkhd->bhqk", query_low, key_low, preferred_element_type=F32) * score_scale
-    )
-    scores = jnp.where(allowed[:, None], scores, MASKED)
-    probs = jnp.exp(scores - log_total)
-    prob_grad = jnp.einsum("bqhd,bkhd->bhqk", attended_grad, value_low, preferred_element_type=F32)
-    value_grad = jnp.einsum(
-        "bhqk,bqhd->bkhd", probs.astype(BF16), attended_grad, preferred_element_type=F32
-    )
-    score_grad = (probs * (prob_grad - jnp.sum(probs * prob_grad, axis=3, keepdims=True))).astype(
-        BF16
-    )
-    query_grad = (
-        jnp.einsum("bhqk,bkhd->bqhd", score_grad, key_low, preferred_element_type=F32) * score_scale
-    )
-    key_grad = (
-        jnp.einsum("bhqk,bqhd->bkhd", score_grad, query_low, preferred_element_type=F32)
-        * score_scale
-    )
-    mixed_grad = jnp.stack(
-        [rotate_back(query_grad, positions), rotate_back(key_grad, positions), value_grad], axis=3
-    )
-    mixed_grad = mixed_grad.reshape(blocks * block, heads_local * 3 * HD).astype(BF16)
-    one_part = contract_cols(mixed_grad, qkv_all)
-    two_part = contract_cols(hidden_low, up_all)
-    return (one_part, two_part, mixed_grad, hidden_low)
-
-
-def vocab_stats(final_low, head_weight, targets, vocab_start):
-    logits = jnp.dot(final_low, head_weight, preferred_element_type=F32)
-    highest = jnp.max(logits, axis=1)
-    log_total = highest + jnp.log(jnp.sum(jnp.exp(logits - highest[:, None]), axis=1))
-    column = vocab_start + lax.broadcasted_iota(jnp.int32, logits.shape, 1)
-    chosen = column == targets[:, None]
-    picked = jnp.sum(jnp.where(chosen, logits, 0.0), axis=1)
-    return (logits, log_total, picked, chosen)
+def chunk_of(width):
+    return next(n for n in (1280, 640, 512, 256, 128) if width % n == 0)
+
+
+def head_kernel(policy_ref, frozen_ref, head_ref, target_ref, logits_ref, stats_ref, other_ref, high_ref, sum_ref, pick_ref):
+    chunk = pl.program_id(0)
+    rows, columns = logits_ref.shape
+
+    @pl.when(chunk == 0)
+    def _():
+        high_ref[...] = jnp.full_like(high_ref, MASKED)
+        sum_ref[...] = jnp.zeros_like(sum_ref)
+        pick_ref[...] = jnp.zeros_like(pick_ref)
+
+    def fold(which, values_ref, begin, width):
+        for first in range(0, rows, 64):
+            own = pl.ds(first, 64)
+            high = high_ref[which, own, :]
+            lanes = [values_ref[own, n : n + 128] for n in range(begin, begin + width, 128)]
+            highest = functools.reduce(jnp.maximum, lanes, high)
+            total = sum_ref[which, own, :] * jnp.exp(high - highest)
+            picked = pick_ref[which, own, :]
+            target = target_ref[own, :] - (chunk * columns + begin)
+            lane = lax.broadcasted_iota(jnp.int32, highest.shape, 1)
+            for n, value in enumerate(lanes):
+                total = total + jnp.exp(value - highest)
+                picked = picked + jnp.where(lane + n * 128 == target, value, 0.0)
+            high_ref[which, own, :] = highest
+            sum_ref[which, own, :] = total
+            pick_ref[which, own, :] = picked
+
+    width = 256 if columns % 256 == 0 else 128
+    last = None
+    for begin in range(0, columns, width):
+        for which, (low_ref, values_ref) in enumerate(
+            ((policy_ref, logits_ref), (frozen_ref, other_ref))
+        ):
+            values_ref[:, begin : begin + width] = dot(
+                low_ref[...], head_ref[:, begin : begin + width]
+            )
+            if last:
+                fold(*last)
+            last = (which, values_ref, begin, width)
+    fold(*last)
+
+    @pl.when(chunk == pl.num_programs(0) - 1)
+    def _():
+        found = []
+        for which in range(2):
+            high = jnp.max(high_ref[which], axis=1, keepdims=True)
+            total = jnp.sum(
+                sum_ref[which] * jnp.exp(high_ref[which] - high), axis=1, keepdims=True
+            )
+            found.append(high + jnp.log(total))
+            found.append(jnp.sum(pick_ref[which], axis=1, keepdims=True))
+        lane = lax.broadcasted_iota(jnp.int32, (rows, 128), 1)
+        joined = jnp.zeros((rows, 128), F32)
+        for n, value in enumerate(found):
+            joined = jnp.where(lane == n, value, joined)
+        stats_ref[...] = jnp.transpose(joined)[:8, :]
+
+
+def head_call(policy_low, frozen_low, head_weight, targets):
+    rows, depth = policy_low.shape
+    width = head_weight.shape[1]
+    columns = chunk_of(width)
+    return pl.pallas_call(
+        head_kernel,
+        grid=(width // columns,),
+        out_shape=[
+            jax.ShapeDtypeStruct((rows, width), F32),
+            jax.ShapeDtypeStruct((8, rows), F32),
+        ],
+        in_specs=[
+            pl.BlockSpec((rows, depth), lambda n: (0, 0)),
+            pl.BlockSpec((rows, depth), lambda n: (0, 0)),
+            pl.BlockSpec((depth, columns), lambda n: (0, n)),
+            pl.BlockSpec((rows, 1), lambda n: (0, 0)),
+        ],
+        out_specs=[
+            pl.BlockSpec((rows, columns), lambda n: (0, n)),
+            pl.BlockSpec((8, rows), lambda n: (0, 0)),
+        ],
+        scratch_shapes=[
+            pltpu.VMEM((rows, columns), F32),
+            pltpu.VMEM((2, rows, 128), F32),
+            pltpu.VMEM((2, rows, 128), F32),
+            pltpu.VMEM((2, rows, 128), F32),
+        ],
+        cost_estimate=pl.CostEstimate(
+            flops=4 * rows * depth * width,
+            bytes_accessed=2 * depth * width + 4 * rows * width,
+            transcendentals=2 * rows * width,
+        ),
+        compiler_params=pltpu.CompilerParams(vmem_limit_bytes=56 * 1024 * 1024),
+    )(policy_low, frozen_low, head_weight, targets)
+
+
+def logit_grad_kernel(logits_ref, head_ref, target_ref, token_ref, part_ref, low_ref, sum_ref):
+    chunk = pl.program_id(0)
+    rows, columns = logits_ref.shape
+
+    for first in range(0, rows, 32):
+        own = pl.ds(first, 32)
+        values = logits_ref[own, :]
+        target = target_ref[own, :] - chunk * columns
+        chosen = lax.broadcasted_iota(jnp.int32, values.shape, 1) == target
+        probs = jnp.exp(values - token_ref[own, 1:2])
+        low_ref[own, :] = (token_ref[own, 0:1] * (jnp.where(chosen, 1.0, 0.0) - probs)).astype(BF16)
+    value = dot_cols(low_ref[...], head_ref[...])
+
+    @pl.when(chunk == 0)
+    def _():
+        sum_ref[...] = value
+
+    @pl.when(chunk > 0)
+    def _():
+        sum_ref[...] += value
+
+    @pl.when(chunk == pl.num_programs(0) - 1)
+    def _():
+        part_ref[...] = sum_ref[...].astype(BF16)
+
+
+def logit_grad_call(logits, head_weight, targets, tokens):
+    rows, width = logits.shape
+    depth = head_weight.shape[0]
+    columns = chunk_of(width)
+    return pl.pallas_call(
+        logit_grad_kernel,
+        grid=(width // columns,),
+        out_shape=jax.ShapeDtypeStruct((rows, depth), BF16),
+        in_specs=[
+            pl.BlockSpec((rows, columns), lambda n: (0, n)),
+            pl.BlockSpec((depth, columns), lambda n: (0, n)),
+            pl.BlockSpec((rows, 1), lambda n: (0, 0)),
+            pl.BlockSpec((rows, tokens.shape[1]), lambda n: (0, 0)),
+        ],
+        out_specs=pl.BlockSpec((rows, depth), lambda n: (0, 0)),
+        scratch_shapes=[pltpu.VMEM((rows, columns), BF16), pltpu.VMEM((rows, depth), F32)],
+        cost_estimate=pl.CostEstimate(
+            flops=2 * rows * depth * width,
+            bytes_accessed=2 * depth * width + 4 * rows * width,
+            transcendentals=rows * width,
+        ),
+        compiler_params=pltpu.CompilerParams(vmem_limit_bytes=56 * 1024 * 1024),
+    )(logits, head_weight, targets, tokens)
 
 
 def adam_step(master, mean_old, square_old, gradient, factor, rate, decay_rate):
@@ -1284,7 +1517,6 @@
     frozen_shards = (qkv_frozen, out_frozen, up_frozen, down_frozen)
     member, _, _ = doc_layout(doc_lengths[0], block)
     _, positions, doc_of = jax.vmap(lambda row: doc_layout(row, block))(lengths_all[:, 0, :SEGS])
-    allowed = allowed_keys(doc_of)
 
     cut = qkv_master.shape[1]
     width_qkv, width_up = cut // SPLIT, up_master.shape[1] // SPLIT
@@ -1295,12 +1527,6 @@
             lax.dynamic_slice(bias, (cut + outer_index * width_up,), (width_up,))[None],
         )
 
-    values = f32(tokens_all)
-    centre = values - jnp.mean(values, axis=1, keepdims=True)
-    scale = lax.rsqrt(jnp.mean(centre * centre, axis=1, keepdims=True) + EPS_NORM)
-    normed = centre * scale
-    one_low = normed_rows(normed, vectors[0], vectors[1])
-    two_low = normed_rows(normed, vectors[2], vectors[3])
     layout = (
         *turn_tables(positions),
         doc_of.reshape(-1, 1),
@@ -1308,67 +1534,34 @@
     )
     final_low, *kept = forward_call(
         tokens_all, eight_rows(vectors), policy_set, own_bias(hidden_bias), layout, block, inner,
-        True, frozen_shards, 2,
+        None, frozen_shards, 2,
     )
     kept_values = tuple(kept[:4])
     frozen_set = (*kept[4:6], joined_columns(kept[6]))
     (frozen_low,) = forward_call(
         tokens_all, eight_rows(vectors_frozen), frozen_set, own_bias(hidden_frozen), layout, block,
-        inner, False, None, 3,
+        inner, kept_values[2], None, 3,
     )
     vocab_start = lax.axis_index("tensor") * head_weight.shape[1]
-    policy_logits, policy_total, policy_pick, chosen = vocab_stats(
-        final_low, head_weight, targets, vocab_start
-    )
-    _, frozen_total, frozen_pick, _ = vocab_stats(frozen_low, head_weight, targets, vocab_start)
-    none = jnp.zeros_like(policy_total)
-    stats = jnp.stack(
-        [policy_total, policy_pick, frozen_total, frozen_pick, none, none, none, none]
-    )
+    own_targets = (targets - vocab_start)[:, None]
+    logits, stats = head_call(final_low, frozen_low, head_weight, own_targets)
     doc_rows = jnp.zeros((8, block), F32).at[:SEGS].set(f32(member).T)
     labels = jnp.zeros((8, 128), F32).at[:SEGS].set(f32(desirable[0])[:, None])
-    token_grad, policy_total = reward_call(stats, doc_rows, labels, inner, 6)
-    logit_grad = (
-        token_grad[:, None]
-        * (chosen.astype(F32) - jnp.exp(policy_logits - policy_total[:, None]))
-    ).astype(BF16)
-    final_part = contract_cols(logit_grad, head_weight)
-    final_quarter, branch_low = final_grad_call(final_part, inner, 4)
-    joined = kept_values[3]
-    one_part, two_part, mixed_grad, hidden_low = layer_backward(
-        branch_low, kept_values, policy_set, positions, allowed
-    )
-    scaled_part = (one_part * vectors[0] + two_part * vectors[2]).astype(BF16)
+    token_rows = reward_call(stats, doc_rows, labels, inner, 6)
+    final_part = logit_grad_call(logits, head_weight, own_targets, token_rows)
+    input_grad, branch_low, mixed_grad, hidden_low, vector_part, bias_part = backward_call(
+        final_part, tokens_all, eight_rows(vectors), policy_set, kept_values, layout, inner, 4
+    )
     shards = tuple(w.shape for w in masters)
-    grads = (
-        contract_rows(one_low, mixed_grad).astype(BF16),
-        contract_rows(two_low, hidden_low).astype(BF16),
-        contract_rows(joined, branch_low).astype(BF16),
-    )
-    none = jnp.zeros_like(vectors[0])
-    vector_part = jnp.stack(
-        [
-            jnp.sum(one_part * normed, axis=0),
-            jnp.sum(one_part, axis=0),
-            jnp.sum(two_part * normed, axis=0),
-            jnp.sum(two_part, axis=0),
-            jnp.sum(f32(final_quarter.astype(BF16)), axis=0),
-            none,
-            none,
-            none,
-        ]
-    )
-    bias_part = jnp.concatenate(
-        [jnp.sum(mixed_grad, axis=0, dtype=F32), jnp.sum(hidden_low, axis=0, dtype=F32)]
-    )
     bias_rows = (width_qkv + width_up) // 128
     bias_tile = (
         jnp.zeros((-(-bias_rows // 8) * 8, 128), F32)
         .at[:bias_rows]
         .set(bias_part.reshape(bias_rows, 128))
     )
-    input_grad, qkv_grad, up_grad, out_grad, down_grad, vector_sum, bias_sum, square = finish_call(
-        scaled_part, inputs, final_quarter, grads, vector_part, bias_tile, shards, inner, 5
+    qkv_grad, up_grad, out_grad, down_grad, vector_sum, bias_sum, square = finish_call(
+        tokens_all, branch_low, eight_rows(vectors), kept_values[2:], (mixed_grad, hidden_low),
+        vector_part, bias_tile, shards, inner, 5,
     )
     input_grad = f32(input_grad)
     vector_grad = jnp.concatenate([vector_sum[:5], vector_sum[4:5]], axis=0)

time: 904 us -> 787 us (0.87)
  matrix products: 142 us -> 0 us
  Pallas kernels: 662 us -> 725 us
  other arithmetic: 54.6 us -> 34 us
  local copies, waits for them, and re-layouts: 33.5 us -> 17.3 us
    dot_general x14 -> x0, matrix products: 142 us -> none  [the longest x4 57.8 us: contract_cols(): lax.dot_general(left_rows, right_rows, (((1,), (1,)), ((), ())), preferre...]
    pallas_call x2 -> x4, Pallas kernels: 249 us -> 326 us  [the longest x1 163 us: backward_call(): pl.pallas_call(functools.partial(backward_kernel, inner), out_shape=[jax....]
    reduce_sum x6 -> x0, other arithmetic: 17.3 us -> none  [the longest x1 11.5 us: vocab_stats(): picked = jnp.sum(jnp.where(chosen, logits, 0.0), axis=1)]
    pallas_call x2, Pallas kernels: 260 us -> 249 us  [forward_call(): pl.pallas_call(functools.partial(forward_kernel, inner, keep, background)...]
where the time goes in v4:
time: 787 us; the launch traced here: 782 us
  Pallas kernels  725 us (92%)
  other arithmetic  34 us (4%)
  local copies, waits for them, and re-layouts  17.3 us (2%)
    pallas_call x2, Pallas kernels, forward_call(): pl.pallas_call(functools.partial(forward_kernel, inner, keep, background)...  249 us
    pallas_call x1, Pallas kernels, backward_call(): pl.pallas_call(functools.partial(backward_kernel, inner), out_shape=[jax....  163 us
    pallas_call x1, Pallas kernels, spread_weights(): pl.pallas_call(functools.partial(spread_weights_kernel, inner), out_shape...  134 us
    pallas_call x1, Pallas kernels, finish_call(): pl.pallas_call(functools.partial(finish_kernel, inner), out_shape=[*(jax....  101 us
    pallas_call x1, Pallas kernels, head_call(): pl.pallas_call(head_kernel, grid=(width // columns,), out_shape=[jax.Shap...  38.4 us
    pallas_call x1, Pallas kernels, logit_grad_call(): pl.pallas_call(logit_grad_kernel, grid=(width // columns,), out_shape=jax...  23.1 us
    sub x6, other arithmetic, adam_step(): master - rate * (mean_hat / (jnp.sqrt(square_hat) + ADAM_EPS) + decay_rat...  17 us
    pallas_call x1, Pallas kernels, reward_call(): pl.pallas_call(functools.partial(reward_kernel, inner), out_shape=jax.Sha...  16 us

profile of v4, /device:TPU:0, one launch (start us, length us, event | category | flops | bytes accessed | tf_op | source)
XLA Modules:
  0.0 781.9 jit_solution(14258300432051722245)
XLA Ops:
  0.7 2.9 convert_element_type.51.up
  3.5 1.1 convert_element_type.52.down
  5.3 1.0 convert_element_type.49.qkv
  7.6 134.4 %shard_map.436 = (bf16[2048,384]{1,0:T(8,128)(2,1)}, bf16[2048,512]{1,0:T(8,128)(2,1)}, bf16[640,2048]{1,0:T(8,128)(2,1)}, bf16[2048,2048]{1,0:T(8,128)(2,1)}, s32[4,8,128]{2,1,0:T(8,128)}) custom-call(bf16[256,1536]{1,0:T(8,128)(2,1)} %convert_element_type.49.qkv, bf16[512,256]{1,0:T(8,128)(2,1)} %convert_element_type.50.out, ...), custom_call_target="tpu_custom_call" | custom-call | tf_op jit(solution)/shard_map/pallas_call | solution.py:300
  143.1 3.7 fusion.4
  147.0 1.9 maximum_maximum_fusion
  150.2 1.3 copy.98
  152.8 141.6 %shard_map.437 = (bf16[512,2048]{1,0:T(8,128)(2,1)}, f32[2048,512]{1,0:T(8,128)}, bf16[2048,384]{1,0:T(8,128)(2,1)}, f32[2048,8]{1,0:T(8,128)}, bf16[2048,640]{1...) custom-call(bf16[2048,2048]{1,0:T(8,128)(2,1)} %get-tuple-element.137.refs_0_.toke, ...), custom_call_target="tpu_custom_call" | custom-call | tf_op jit(solution)/shard_map/pallas_call | solution.py:629
  295.8 1.3 dynamic_slice.15
  297.8 107.0 %shard_map.438.frozen_ref = bf16[512,2048]{1,0:T(8,128)(2,1)} custom-call(bf16[2048,2048]{1,0:T(8,128)(2,1)} %get-tuple-element.137.refs_0_.tokens_hbm.tokens_ref, f32[8,2048]{1,0:T(8,128)} %scatter.30.refs_1_, bf16[2048,384]{1,0:T(8,128)(2,1)} %get-tuple-element.143.refs_2_, bf16[2048,512]{1,0:T(8,128)(2,1)} %get-tuple-element.144.refs_3_, ...), custom_call_target="tpu_custom_call" | custom-call | tf_op jit(solution)/shard_map/pallas_call | solution.py:629
  404.8 0.9 copy.93.target_ref
  405.6 38.4 %shard_map.439 = (f32[512,6400]{1,0:T(8,128)}, f32[8,512]{1,0:T(8,128)}) custom-call(bf16[512,2048]{1,0:T(8,128)(2,1)} %get-tuple-element.220.policy_ref, bf16[512,2048]{1,0:T(8,128)(2,1)} %shard_map.438.frozen_ref, bf16[2048,6400]{1,0:T(8,128)(2,1)} %head_ref.3, s32[512,1]{1,0:T(8,128)} %copy.93.target_ref), custom_call_target="tpu_custom_call" | custom-call | flops 26843545600 | bytes 39321600 | tf_op jit(solution)/shard_map/pallas_call | solution.py:1379
  450.0 16.0 %shard_map.440.token_ref = f32[512,8]{1,0:T(8,128)} custom-call(f32[8,512]{1,0:T(8,128)} %get-tuple-element.148.stats_ref, f32[8,512]{1,0:T(8,128)} %pad_convert_fusion.member_ref, f32[8,128]{1,0:T(8,128)} %scatter.36.label_ref), custom_call_target="tpu_custom_call" | custom-call | tf_op jit(solution)/shard_map/pallas_call | solution.py:1266
  466.0 23.1 %shard_map.441.final_part = bf16[512,2048]{1,0:T(8,128)(2,1)} custom-call(f32[512,6400]{1,0:T(8,128)} %get-tuple-element.147.logits_ref, bf16[2048,6400]{1,0:T(8,128)(2,1)} %head_ref.3, s32[512,1]{1,0:T(8,128)} %copy.93.target_ref, f32[512,8]{1,0:T(8,128)} %shard_map.440.token_ref), custom_call_target="tpu_custom_call" | custom-call | flops 13421772800 | bytes 39321600 | tf_op jit(solution)/shard_map/pallas_call | solution.py:1441
  489.1 163.4 %shard_map.442 = (bf16[512,2048]{1,0:T(8,128)(2,1)}, bf16[2048,2048]{1,0:T(8,128)(2,1)}, bf16[2048,384]{1,0:T(8,128)(2,1)}, bf16[2048,512]{1,0:T(8,128)(2,1)}, f32[8,2048]{1,0:T(8,128)}, /*index=5*/f32[1,896]{1,0:T(1,128)}) custom-call(bf16[512,2048]{1,0:T(8,128)(2,1)} %shard_map.441.final_part, ...), custom_call_target="tpu_custom_call" | custom-call | tf_op jit(solution)/shard_map/pallas_call | solution.py:880
  653.8 101.2 %shard_map.443 = (bf16[256,1536]{1,0:T(8,128)(2,1)}, bf16[256,2048]{1,0:T(8,128)(2,1)}, bf16[512,256]{1,0:T(8,128)(2,1)}, bf16[2048,256]{1,0:T(8,128)(2,1)}, f32...) custom-call(bf16[2048,2048]{1,0:T(8,128)(2,1)} %get-tuple-element.137.refs_0_.tokens_hbm.tokens_ref, ...), custom_call_target="tpu_custom_call" | custom-call | tf_op jit(solution)/shard_map/pallas_call | solution.py:1171
  755.8 1.2 slice.175
  759.3 1.6 multiply_subtract_fusion.4
  760.8 6.5 multiply_subtract_fusion
  767.4 3.9 multiply_subtract_fusion.1
  771.3 1.4 multiply_subtract_fusion.3
  773.7 3.0 multiply_subtract_fusion.2
  776.8 2.5 convert_element_type.57
  779.3 1.3 copy.104
  (94 shorter events, 15.8 us)
Async XLA Ops:
  0.7 2.9 copy-start
  3.5 2.8 copy-start.6
  147.0 1.9 copy-start.20
  147.0 5.2 copy-start.16
  152.8 144.3 %copy-start.17 = (f32[6,2048]{1,0:T(8,128)S(1)}, f32[6,2048]{1,0:T(8,128)}, u32[]{:S(2)}) copy-start(f32[6,2048]{1,0:T(8,128)} %param.72) | copy-start | bytes 147460
  297.8 107.0 %copy-start.24 = (s32[512]{0:T(512)S(1)}, s32[512]{0:T(512)}, u32[]{:S(2)}) copy-start(s32[512]{0:T(512)} %param.46) | copy-start | bytes 6148
  405.6 43.7 %copy-start.25 = (s32[1,4]{1,0:T(1,128)S(1)}, s32[1,4]{1,0:T(1,128)}, u32[]{:S(2)}) copy-start(s32[1,4]{1,0:T(1,128)} %param.48) | copy-start | bytes 52
  653.8 103.9 %copy-start.22 = (f32[3584]{0:T(1024)S(1)}, f32[3584]{0:T(1024)}, u32[]{:S(2)}) copy-start(f32[3584]{0:T(1024)} %param.67) | copy-start | bytes 43012
  653.8 103.9 %copy-start.23 = (f32[3584]{0:T(1024)S(1)}, f32[3584]{0:T(1024)}, u32[]{:S(2)}) copy-start(f32[3584]{0:T(1024)} %param.61) | copy-start | bytes 43012
  653.8 105.4 %copy-start.18 = (f32[6,2048]{1,0:T(8,128)S(1)}, f32[6,2048]{1,0:T(8,128)}, u32[]{:S(2)}) copy-start(f32[6,2048]{1,0:T(8,128)} %param.66) | copy-start | bytes 147460
  653.8 105.4 %copy-start.19 = (f32[6,2048]{1,0:T(8,128)S(1)}, f32[6,2048]{1,0:T(8,128)}, u32[]{:S(2)}) copy-start(f32[6,2048]{1,0:T(8,128)} %param.60) | copy-start | bytes 147460
  760.8 6.5 copy-start.1
  760.8 6.5 copy-start.7
  760.8 6.5 copy-start.8
  760.8 6.5 copy-start.11
  767.3 4.0 copy-start.13
  767.3 4.0 copy-start.14
  767.3 3.9 copy-start.15
  767.4 5.4 copy-start.10
  767.4 5.3 copy-start.12
  771.3 2.0 copy-start.3
  771.3 2.4 copy-start.9
  773.7 3.0 copy-start.4
  776.8 2.5 copy-start.5
  (2 other events, 3.5 us)

commit v5 on v4

--- a/solution.py
+++ b/solution.py
@@ -326,8 +326,9 @@
         self.near_sems, self.far_sems, self.outer_sems = sems[0:2], sems[2:4], sems[4:6]
         self.quarter_sems = sems[6:8]
         self.rows = far_out.shape[1]
-        self.near, self.far, self.outer = {}, {}, {}
+        self.near, self.far, self.outer, self.coming = {}, {}, {}, {}
         self.slots = None
+        self.before = None
 
     def recycle(self, step):
         for side in range(2):
@@ -351,6 +352,8 @@
     def across(self, step):
         here = self.here
         self.near[step, 0].wait_recv()
+        if self.before:
+            self.before.far.pop(step).wait_send()
         self.far_out[step] = (
             f32(self.part[self.rows_of(step, here.far), :]) + f32(self.near_in[step, 0])
         ).astype(BF16)
@@ -374,8 +377,10 @@
         if step == SPLIT - 1:
             self.total[...] = value
             return
+        if self.before:
+            self.before.outer.pop(step).wait_send()
         self.outer_out[step] = value.astype(BF16)
-        self.outer[step] = remote(
+        self.outer[step] = self.coming[step] = remote(
             self.outer_out.at[step],
             self.outer_in.at[step],
             self.outer_sems[0].at[step],
@@ -386,7 +391,7 @@
     def value(self):
         value = self.total[...]
         for step in range(SPLIT - 1):
-            self.outer[step].wait_recv()
+            self.coming[step].wait_recv()
             value = value + f32(self.outer_in[step])
         return value
 
@@ -396,18 +401,34 @@
                 copy.wait_send()
 
 
+class Quarters:
+    def __init__(self, here, ref, rows, send, recv):
+        self.here, self.ref, self.rows, self.send, self.recv = here, ref, rows, send, recv
+
+    def copy(self, number, quarter, peer):
+        piece = self.ref.at[pl.ds(quarter * self.rows, self.rows), :]
+        return remote(piece, piece, self.send.at[number], self.recv.at[number], peer)
+
+    def start(self):
+        self.far = self.copy(0, self.here.t, self.here.far_peer())
+        self.near = self.copy(1, self.here.t, self.here.near_peer())
+
+    def pass_on(self):
+        self.far.wait_recv()
+        self.passed = self.copy(2, self.here.far, self.here.near_peer())
+
+    def finish(self):
+        self.near.wait_recv()
+        self.passed.wait_recv()
+        for copy in (self.far, self.near, self.passed):
+            copy.wait_send()
+
+
 def gather_quarters(here, ref, rows, send, recv):
-    def piece(quarter):
-        return ref.at[pl.ds(quarter * rows, rows), :]
-
-    far = remote(piece(here.t), piece(here.t), send.at[0], recv.at[0], here.far_peer())
-    near = remote(piece(here.t), piece(here.t), send.at[1], recv.at[1], here.near_peer())
-    far.wait_recv()
-    passed = remote(piece(here.far), piece(here.far), send.at[2], recv.at[2], here.near_peer())
-    near.wait_recv()
-    passed.wait_recv()
-    for copy in (far, near, passed):
-        copy.wait_send()
+    quarters = Quarters(here, ref, rows, send, recv)
+    quarters.start()
+    quarters.pass_on()
+    quarters.finish()
 
 
 def reduce_peers(here):
@@ -451,26 +472,38 @@
         body(pl.ds(pl.multiple_of(start + n * tile, tile), tile), pl.ds(pl.multiple_of(n * tile, tile), tile))
 
 
-def forward_kernel(inner, keep, background, *refs):
+def forward_kernel(inner, keeps, background, *refs):
     here = Place(inner)
-    (tokens_ref, rows_ref, qkv_ref, up_ref, low_ref, qkv_bias, up_bias, cosine, sine,
-     doc_col, doc_row, *refs) = refs
-    if not keep:
-        facts_ref, *refs = refs
+    refs = list(refs)
+
+    def take(count):
+        taken = refs[:count]
+        del refs[:count]
+        return taken
+
+    tokens_ref, cosine, sine, doc_col, doc_row = take(5)
     tables = (cosine, sine)
-    shards = refs[:4] if background else []
-    refs = refs[len(shards):]
-    final_ref, *refs = refs
-    if keep:
-        slope_ref, mixed_ref, facts_ref, joined_ref, *refs = refs
-    wholes = refs[:3] if background else []
-    refs = refs[len(wholes):]
-    if not keep:
-        mixed_ref, joined_ref, *refs = refs
-    one_ref, two_ref, hidden_ref, part_ref, *refs = refs
-    sums = RowSum(here, part_ref, *refs[:14])
-    refs = refs[14:]
+    own_rows = [take(3) for _ in keeps]
+    given = take(3)
+    facts_ref = None if keeps[0] else take(1)[0]
+    shards = take(4 if background else 0)
+    finals = take(len(keeps))
+    slope_ref, kept_mixed, facts_ref, kept_joined = take(4) if keeps[0] else (None, None, facts_ref, None)
+    wholes = take(3 if background else 0)
+    weights, load = take(3), take(1)[0]
+    other_mixed, other_joined = (None, None) if all(keeps) else take(2)
+    one_ref, two_ref, hidden_ref, part_ref = take(4)
     block = one_ref.shape[0]
+    common = take(14)
+    sums = [RowSum(here, part_ref, *common)]
+    if len(keeps) > 1:
+        total, outer_in, *sems = take(10)
+        sums.append(RowSum(here, part_ref, total, *common[1:4], outer_in, common[5], *sems))
+        sums[1].before = sums[0]
+    for number, layer in enumerate(sums):
+        layer.slots = {step: (number * SPLIT + step) % 2 for step in range(SPLIT)}
+    rows = sums[0].rows
+    qkv_ref, up_ref, low_ref = weights
     heads = qkv_ref.shape[1] // (3 * HD)
     cut = heads * HD
     peers = reduce_peers(here)
@@ -480,6 +513,15 @@
         peers = spread.peers() + [here.far_peer(), here.near_peer()]
     greet(peers)
     events = []
+    loads = []
+
+    def fetch(sources):
+        for number, (source, target) in enumerate(zip(sources, weights)):
+            copy = pltpu.make_async_copy(source, target, load.at[number])
+            copy.start()
+            loads.append(copy)
+
+    fetch(given)
     if background:
         for number in range(AHEAD):
             spread.send_on(number)
@@ -490,8 +532,30 @@
         if events:
             spread.step(events.pop(0))
 
-    for step in range(SPLIT):
-        start = ((here.o + 1 + step) % SPLIT) * block
+    def stage(name, position):
+        if 0 <= position < len(keeps) * SPLIT:
+            getattr(sums[position // SPLIT], name)(position % SPLIT)
+
+    gathers = []
+
+    def settle(number):
+        rows_ref = own_rows[number][0]
+        branch = sums[number].value() + rows_ref[4:5, :] + rows_ref[5:6, :]
+        quarter = pl.ds(pl.multiple_of(here.o * block + here.t * rows, rows), rows)
+        mine = pl.ds(pl.multiple_of(here.t * rows, rows), rows)
+        finals[number][mine, :] = (f32(tokens_ref[quarter, :]) + branch).astype(BF16)
+        gathers.append(Quarters(here, finals[number], rows, *sums[number].quarter_sems))
+        gathers[-1].start()
+
+    for position in range(len(keeps) * SPLIT):
+        number, step = position // SPLIT, position % SPLIT
+        keep = keeps[number]
+        rows_ref, qkv_bias, up_bias = own_rows[number]
+        mixed_ref, joined_ref = (
+            (kept_mixed, kept_joined) if keep else (other_mixed, other_joined)
+        )
+        own_block = (here.o + 1 + step) % SPLIT
+        start = own_block * block
         kept = start if keep else 0
 
         def norm(where, own):
@@ -512,10 +576,16 @@
 
         row_tiles(start, block, 16, norm)
         serve()
-        if step:
-            sums.across(step - 1)
+        stage("across", position - 1)
+        if number and step == 0:
+            while events:
+                serve()
+            spread.finish()
+            fetch(wholes)
+        while loads:
+            loads.pop(0).wait()
         whole = pl.ds(pl.multiple_of(start, block), block)
-        mine = pl.ds(pl.multiple_of(kept, block), block)
+        mine = pl.ds(kept if keep else 0, block)
         mixed = dot(one_ref[...], qkv_ref[...]) + qkv_bias[...]
         for head in range(heads):
             at = head * 3 * HD
@@ -537,7 +607,6 @@
                 scores = dot_cols(
                     mixed_ref[queries, at : at + HD], mixed_ref[keys, at + HD : at + 2 * HD]
                 ) * HD ** (-0.5)
-                own_block = (here.o + 1 + step) % SPLIT
                 same = doc_col[tokens_at, :] == doc_row[own_block][:, : first + 128]
                 earlier = first + lax.broadcasted_iota(
                     jnp.int32, scores.shape, 0
@@ -553,8 +622,8 @@
                 joined_ref[queries, head * HD : (head + 1) * HD] = dot(
                     probs, mixed_ref[keys, at + 2 * HD : at + 3 * HD]
                 ).astype(BF16)
-        if step > 1:
-            sums.along(step - 2)
+        stage("along", position - 2)
+        stage("recycle", position - 2)
 
         def activate(where, own):
             hidden = hidden_ref[own, :] + up_bias[...]
@@ -567,35 +636,42 @@
         row_tiles(kept, block, 32, activate)
         serve()
         columns = 512
+        slot = pl.ds((position % 2) * block, block)
 
         @pl.loop(0, part_ref.shape[1] // columns)
         def _(n):
             at = pl.ds(pl.multiple_of(n * columns, columns), columns)
-            part_ref[whole, at] = dot(joined_ref[mine, :], low_ref[:, at]).astype(BF16)
-
-        sums.start(step)
-    sums.across(SPLIT - 1)
+            part_ref[slot, at] = dot(joined_ref[mine, :], low_ref[:, at]).astype(BF16)
+
+        stage("start", position)
+        if number and step == 2:
+            settle(0)
+        if number and step == 3:
+            gathers[0].pass_on()
+    last = len(keeps) - 1
+    sums[last].across(SPLIT - 1)
     while events:
         serve()
-    sums.along(SPLIT - 2)
-    sums.along(SPLIT - 1)
-    branch = sums.value() + rows_ref[4:5, :] + rows_ref[5:6, :]
-    quarter = pl.ds(pl.multiple_of(here.o * block + here.t * sums.rows, sums.rows), sums.rows)
-    final_ref[pl.ds(pl.multiple_of(here.t * sums.rows, sums.rows), sums.rows), :] = (
-        f32(tokens_ref[quarter, :]) + branch
-    ).astype(BF16)
-    gather_quarters(here, final_ref, sums.rows, *sums.quarter_sems)
-    sums.finish()
-    if background:
+    sums[last].along(SPLIT - 2)
+    sums[last].along(SPLIT - 1)
+    settle(last)
+    gathers[last].pass_on()
+    for gather in gathers:
+        gather.finish()
+    for layer in sums:
+        layer.finish()
+    if background and last == 0:
         spread.finish()
 
 
-def forward_call(tokens, rows, weights, biases, layout, block, inner, facts, shards, number):
+def forward_call(tokens, layout, layers, weights, block, inner, facts, shards, number):
     total_rows, d_model = tokens.shape
     qkv_all, up_all, low_all = weights
-    background, keep = shards is not None, facts is None
-    outs = [jax.ShapeDtypeStruct((block, d_model), BF16)]
-    if keep:
+    background = shards is not None
+    keeps = (facts is None,) + (False,) * (len(layers) - 1)
+    dma = pltpu.SemaphoreType.DMA
+    outs = [jax.ShapeDtypeStruct((block, d_model), BF16) for _ in layers]
+    if keeps[0]:
         outs += [
             jax.ShapeDtypeStruct((total_rows, up_all.shape[1]), F32),
             jax.ShapeDtypeStruct((total_rows, qkv_all.shape[1]), BF16),
@@ -603,8 +679,8 @@
             jax.ShapeDtypeStruct((total_rows, low_all.shape[0]), BF16),
         ]
     specs = [VMEM_SPEC] * len(outs)
-    scratch = []
-    if not keep:
+    scratch = [pltpu.VMEM(w.shape, BF16) for w in weights] + [dma((3,))]
+    if not all(keeps):
         scratch += [
             pltpu.VMEM((block, qkv_all.shape[1]), BF16),
             pltpu.VMEM((block, low_all.shape[0]), BF16),
@@ -613,13 +689,21 @@
         pltpu.VMEM((block, d_model), BF16),
         pltpu.VMEM((block, d_model), BF16),
         pltpu.VMEM((block, up_all.shape[1]), F32),
-        pltpu.VMEM((total_rows, d_model), BF16),
+        pltpu.VMEM((2 * block, d_model), BF16),
     ]
-    scratch += reduce_scratch(block // QUARTERS, d_model)
-    operands = [tokens, rows, qkv_all, up_all, low_all, *biases, *layout]
-    if not keep:
+    one_sum = reduce_scratch(block // QUARTERS, d_model)
+    scratch += one_sum
+    if len(layers) > 1:
+        scratch += [one_sum[0], one_sum[4], *one_sum[6:]]
+    operands = [tokens, *layout]
+    for layer in layers:
+        operands += layer
+    in_specs = [VMEM_SPEC] * len(operands)
+    operands += weights
+    in_specs += [ANY_SPEC] * 3
+    if not keeps[0]:
         operands.append(facts)
-    in_specs = [VMEM_SPEC] * len(operands)
+        in_specs.append(VMEM_SPEC)
     if background:
         operands += shards
         in_specs += [ANY_SPEC] * 4
@@ -627,7 +711,7 @@
         specs += [ANY_SPEC] * 3
         scratch += spread_scratch(shards, inner)
     return pl.pallas_call(
-        functools.partial(forward_kernel, inner, keep, background),
+        functools.partial(forward_kernel, inner, keeps, background),
         out_shape=outs,
         in_specs=in_specs,
         out_specs=specs,
@@ -1532,16 +1616,22 @@
         doc_of.reshape(-1, 1),
         doc_of[:, None, :],
     )
-    final_low, *kept = forward_call(
-        tokens_all, eight_rows(vectors), policy_set, own_bias(hidden_bias), layout, block, inner,
-        None, frozen_shards, 2,
-    )
-    kept_values = tuple(kept[:4])
-    frozen_set = (*kept[4:6], joined_columns(kept[6]))
-    (frozen_low,) = forward_call(
-        tokens_all, eight_rows(vectors_frozen), frozen_set, own_bias(hidden_frozen), layout, block,
-        inner, kept_values[2], None, 3,
-    )
+    policy = (eight_rows(vectors), *own_bias(hidden_bias))
+    frozen = (eight_rows(vectors_frozen), *own_bias(hidden_frozen))
+    if aligned(out_master.shape[1]):
+        final_low, frozen_low, *kept = forward_call(
+            tokens_all, layout, (policy, frozen), policy_set, block, inner, None, frozen_shards, 2
+        )
+        kept_values = tuple(kept[:4])
+    else:
+        final_low, *kept = forward_call(
+            tokens_all, layout, (policy,), policy_set, block, inner, None, frozen_shards, 2
+        )
+        kept_values = tuple(kept[:4])
+        frozen_set = (*kept[4:6], joined_columns(kept[6]))
+        (frozen_low,) = forward_call(
+            tokens_all, layout, (frozen,), frozen_set, block, inner, kept_values[2], None, 3
+        )
     vocab_start = lax.axis_index("tensor") * head_weight.shape[1]
     own_targets = (targets - vocab_start)[:, None]
     logits, stats = head_call(final_low, frozen_low, head_weight, own_targets)

time: 787 us -> 739 us (0.939)
  Pallas kernels: 725 us -> 677 us
    pallas_call x2 -> x1, Pallas kernels: 249 us -> 197 us  [forward_call(): pl.pallas_call(functools.partial(forward_kernel, inner, keeps, background...]
where the time goes in v5:
time: 739 us; the launch traced here: 734 us
  Pallas kernels  677 us (92%)
  other arithmetic  34 us (5%)
  local copies, waits for them, and re-layouts  17.3 us (2%)
    pallas_call x1, Pallas kernels, forward_call(): pl.pallas_call(functools.partial(forward_kernel, inner, keeps, background...  197 us
    pallas_call x1, Pallas kernels, backward_call(): pl.pallas_call(functools.partial(backward_kernel, inner), out_shape=[jax....  164 us
    pallas_call x1, Pallas kernels, spread_weights(): pl.pallas_call(functools.partial(spread_weights_kernel, inner), out_shape...  134 us
    pallas_call x1, Pallas kernels, finish_call(): pl.pallas_call(functools.partial(finish_kernel, inner), out_shape=[*(jax....  102 us
    pallas_call x1, Pallas kernels, head_call(): pl.pallas_call(head_kernel, grid=(width // columns,), out_shape=[jax.Shap...  38.4 us
    pallas_call x1, Pallas kernels, logit_grad_call(): pl.pallas_call(logit_grad_kernel, grid=(width // columns,), out_shape=jax...  23.1 us
    pallas_call x1, Pallas kernels, reward_call(): pl.pallas_call(functools.partial(reward_kernel, inner), out_shape=jax.Sha...  19.3 us
    sub x6, other arithmetic, adam_step(): master - rate * (mean_hat / (jnp.sqrt(square_hat) + ADAM_EPS) + decay_rat...  17 us

profile of v5, /device:TPU:0, one launch (start us, length us, event | category | flops | bytes accessed | tf_op | source)
XLA Modules:
  0.0 733.9 jit_solution(15145190823569159037)
XLA Ops:
  0.7 2.9 convert_element_type.51.up
  3.5 1.1 convert_element_type.52.down
  5.3 1.0 convert_element_type.49.qkv
  7.6 134.4 %shard_map.436 = (bf16[2048,384]{1,0:T(8,128)(2,1)}, bf16[2048,512]{1,0:T(8,128)(2,1)}, bf16[640,2048]{1,0:T(8,128)(2,1)}, bf16[2048,2048]{1,0:T(8,128)(2,1)}, s32[4,8,128]{2,1,0:T(8,128)}) custom-call(bf16[256,1536]{1,0:T(8,128)(2,1)} %convert_element_type.49.qkv, bf16[512,256]{1,0:T(8,128)(2,1)} %convert_element_type.50.out, ...), custom_call_target="tpu_custom_call" | custom-call | tf_op jit(solution)/shard_map/pallas_call | solution.py:300
  143.1 3.7 fusion.4
  147.0 1.9 maximum_maximum_fusion
  151.6 1.3 dynamic_slice.15
  152.9 1.3 copy.94
  156.1 196.7 %shard_map.437 = (bf16[512,2048]{1,0:T(8,128)(2,1)}, bf16[512,2048]{1,0:T(8,128)(2,1)}, f32[2048,512]{1,0:T(8,128)}, bf16[2048,384]{1,0:T(8,128)(2,1)}, f32[2048...) custom-call(bf16[2048,2048]{1,0:T(8,128)(2,1)} %get-tuple-element.13, ...), custom_call_target="tpu_custom_call" | custom-call | tf_op jit(solution)/shard_map/pallas_call | solution.py:713
  352.8 0.9 copy.89.target_ref
  353.7 38.4 %shard_map.438 = (f32[512,6400]{1,0:T(8,128)}, f32[8,512]{1,0:T(8,128)}) custom-call(bf16[512,2048]{1,0:T(8,128)(2,1)} %get-tuple-element.216.policy_ref, bf16[512,2048]{1,0:T(8,128)(2,1)} %get-tuple-element.141.frozen_ref, bf16[2048,6400]{1,0:T(8,128)(2,1)} %head_ref.3, s32[512,1]{1,0:T(8,128)} %copy.89.target_ref), custom_call_target="tpu_custom_call" | custom-call | flops 26843545600 | bytes 39321600 | tf_op jit(solution)/shard_map/pallas_call | solution.py:1463
  398.1 19.3 %shard_map.439.token_ref = f32[512,8]{1,0:T(8,128)} custom-call(f32[8,512]{1,0:T(8,128)} %get-tuple-element.143.stats_ref, f32[8,512]{1,0:T(8,128)} %pad_convert_fusion.member_ref, f32[8,128]{1,0:T(8,128)} %scatter.36.label_ref), custom_call_target="tpu_custom_call" | custom-call | tf_op jit(solution)/shard_map/pallas_call | solution.py:1350
  417.3 23.1 %shard_map.440.final_part = bf16[512,2048]{1,0:T(8,128)(2,1)} custom-call(f32[512,6400]{1,0:T(8,128)} %get-tuple-element.142.logits_ref, bf16[2048,6400]{1,0:T(8,128)(2,1)} %head_ref.3, s32[512,1]{1,0:T(8,128)} %copy.89.target_ref, f32[512,8]{1,0:T(8,128)} %shard_map.439.token_ref), custom_call_target="tpu_custom_call" | custom-call | flops 13421772800 | bytes 39321600 | tf_op jit(solution)/shard_map/pallas_call | solution.py:1525
  440.4 163.5 %shard_map.441 = (bf16[512,2048]{1,0:T(8,128)(2,1)}, bf16[2048,2048]{1,0:T(8,128)(2,1)}, bf16[2048,384]{1,0:T(8,128)(2,1)}, bf16[2048,512]{1,0:T(8,128)(2,1)}, f32[8,2048]{1,0:T(8,128)}, /*index=5*/f32[1,896]{1,0:T(1,128)}) custom-call(bf16[512,2048]{1,0:T(8,128)(2,1)} %shard_map.440.final_part, ...), custom_call_target="tpu_custom_call" | custom-call | tf_op jit(solution)/shard_map/pallas_call | solution.py:964
  605.3 101.7 %shard_map.442 = (bf16[256,1536]{1,0:T(8,128)(2,1)}, bf16[256,2048]{1,0:T(8,128)(2,1)}, bf16[512,256]{1,0:T(8,128)(2,1)}, bf16[2048,256]{1,0:T(8,128)(2,1)}, f32...) custom-call(bf16[2048,2048]{1,0:T(8,128)(2,1)} %get-tuple-element.135.refs_0_.tokens_hbm.tokens_ref, ...), custom_call_target="tpu_custom_call" | custom-call | tf_op jit(solution)/shard_map/pallas_call | solution.py:1255
  707.8 1.2 slice.175
  710.3 0.8 slice.177
  711.2 1.6 multiply_subtract_fusion.4
  712.8 6.5 multiply_subtract_fusion
  719.3 3.9 multiply_subtract_fusion.1
  723.2 1.4 multiply_subtract_fusion.3
  725.7 3.0 multiply_subtract_fusion.2
  728.7 2.5 convert_element_type.57
  731.2 1.3 copy.100
  (93 shorter events, 14.9 us)
Async XLA Ops:
  0.7 2.9 copy-start
  3.5 2.8 copy-start.6
  147.0 1.9 copy-start.20
  147.0 7.9 %copy-start.16 = (f32[6,2048]{1,0:T(8,128)S(1)}, f32[6,2048]{1,0:T(8,128)}, u32[]{:S(2)}) copy-start(f32[6,2048]{1,0:T(8,128)} %param.54) | copy-start | bytes 147460
  147.0 8.5 %copy-start.17 = (f32[6,2048]{1,0:T(8,128)S(1)}, f32[6,2048]{1,0:T(8,128)}, u32[]{:S(2)}) copy-start(f32[6,2048]{1,0:T(8,128)} %param.72) | copy-start | bytes 147460
  156.1 196.7 %copy-start.24 = (s32[512]{0:T(512)S(1)}, s32[512]{0:T(512)}, u32[]{:S(2)}) copy-start(s32[512]{0:T(512)} %param.46) | copy-start | bytes 6148
  353.7 43.7 %copy-start.25 = (s32[1,4]{1,0:T(1,128)S(1)}, s32[1,4]{1,0:T(1,128)}, u32[]{:S(2)}) copy-start(s32[1,4]{1,0:T(1,128)} %param.48) | copy-start | bytes 52
  605.3 104.4 %copy-start.22 = (f32[3584]{0:T(1024)S(1)}, f32[3584]{0:T(1024)}, u32[]{:S(2)}) copy-start(f32[3584]{0:T(1024)} %param.67) | copy-start | bytes 43012
  605.3 104.4 %copy-start.23 = (f32[3584]{0:T(1024)S(1)}, f32[3584]{0:T(1024)}, u32[]{:S(2)}) copy-start(f32[3584]{0:T(1024)} %param.61) | copy-start | bytes 43012
  605.3 105.9 %copy-start.18 = (f32[6,2048]{1,0:T(8,128)S(1)}, f32[6,2048]{1,0:T(8,128)}, u32[]{:S(2)}) copy-start(f32[6,2048]{1,0:T(8,128)} %param.66) | copy-start | bytes 147460
  605.3 105.9 %copy-start.19 = (f32[6,2048]{1,0:T(8,128)S(1)}, f32[6,2048]{1,0:T(8,128)}, u32[]{:S(2)}) copy-start(f32[6,2048]{1,0:T(8,128)} %param.60) | copy-start | bytes 147460
  712.8 6.5 copy-start.1
  712.8 6.5 copy-start.7
  712.8 6.5 copy-start.8
  712.8 6.5 copy-start.11
  719.3 4.0 copy-start.13
  719.3 3.9 copy-start.14
  719.3 3.9 copy-start.15
  719.3 5.4 copy-start.10
  719.3 5.3 copy-start.12
  723.2 2.0 copy-start.3
  723.2 2.4 copy-start.9
  725.7 3.0 copy-start.4
  728.7 2.5 copy-start.5
  (2 other events, 3.5 us)

commit v6 on v5

--- a/solution.py
+++ b/solution.py
@@ -2,6 +2,7 @@
 
 import jax
 import jax.numpy as jnp
+import numpy as np
 from jax import lax
 from jax.experimental import pallas as pl
 from jax.experimental.pallas import tpu as pltpu
@@ -466,6 +467,15 @@
     return values * cosine + direction * (jnp.where(first, ahead, behind) * sine)
 
 
+def documents(lengths, index):
+    end = jnp.zeros((1, 1), jnp.int32)
+    found = jnp.zeros(index.shape, jnp.int32)
+    for segment in range(SEGS - 1):
+        end = end + lengths[0:1, segment : segment + 1]
+        found = found + (index >= end).astype(jnp.int32)
+    return found
+
+
 def row_tiles(start, count, tile, body):
     @pl.loop(0, count // tile)
     def _(n):
@@ -481,9 +491,9 @@
         del refs[:count]
         return taken
 
-    tokens_ref, cosine, sine, doc_col, doc_row = take(5)
+    tokens_ref, lengths_ref, cosine, sine = take(4)
     tables = (cosine, sine)
-    own_rows = [take(3) for _ in keeps]
+    own_rows = [take(2) for _ in keeps]
     given = take(3)
     facts_ref = None if keeps[0] else take(1)[0]
     shards = take(4 if background else 0)
@@ -550,7 +560,7 @@
     for position in range(len(keeps) * SPLIT):
         number, step = position // SPLIT, position % SPLIT
         keep = keeps[number]
-        rows_ref, qkv_bias, up_bias = own_rows[number]
+        rows_ref, bias_ref = own_rows[number]
         mixed_ref, joined_ref = (
             (kept_mixed, kept_joined) if keep else (other_mixed, other_joined)
         )
@@ -586,18 +596,23 @@
             loads.pop(0).wait()
         whole = pl.ds(pl.multiple_of(start, block), block)
         mine = pl.ds(kept if keep else 0, block)
-        mixed = dot(one_ref[...], qkv_ref[...]) + qkv_bias[...]
+        width = qkv_ref.shape[1]
+        first_bias = bias_ref[:, pl.ds(pl.multiple_of(here.o * width, 128), width)]
+        mixed = dot(one_ref[...], qkv_ref[...]) + first_bias
         for head in range(heads):
             at = head * 3 * HD
             for offset in (0, HD):
                 mixed_ref[mine, at + offset : at + offset + HD] = turn(
-                    mixed[:, at + offset : at + offset + HD], tables, whole, 1.0
+                    mixed[:, at + offset : at + offset + HD], tables, pl.ds(0, block), 1.0
                 ).astype(BF16)
             mixed_ref[mine, at + 2 * HD : at + 3 * HD] = mixed[:, at + 2 * HD : at + 3 * HD].astype(
                 BF16
             )
         hidden_ref[...] = dot(two_ref[...], up_ref[...])
         serve()
+        lengths = lengths_ref[own_block]
+        doc_col = documents(lengths, lax.broadcasted_iota(jnp.int32, (block, 1), 0))
+        doc_row = documents(lengths, lax.broadcasted_iota(jnp.int32, (1, block), 1))
         for head in range(heads):
             at = head * 3 * HD
             for first in range(0, block, 128):
@@ -607,7 +622,7 @@
                 scores = dot_cols(
                     mixed_ref[queries, at : at + HD], mixed_ref[keys, at + HD : at + 2 * HD]
                 ) * HD ** (-0.5)
-                same = doc_col[tokens_at, :] == doc_row[own_block][:, : first + 128]
+                same = doc_col[first : first + 128] == doc_row[:, : first + 128]
                 earlier = first + lax.broadcasted_iota(
                     jnp.int32, scores.shape, 0
                 ) >= lax.broadcasted_iota(jnp.int32, scores.shape, 1)
@@ -626,7 +641,9 @@
         stage("recycle", position - 2)
 
         def activate(where, own):
-            hidden = hidden_ref[own, :] + up_bias[...]
+            width = up_ref.shape[1]
+            begin = SPLIT * qkv_ref.shape[1] + here.o * width
+            hidden = hidden_ref[own, :] + bias_ref[:, pl.ds(pl.multiple_of(begin, 128), width)]
             share = 0.5 * (1.0 + error_function(hidden * 0.7071067811865476))
             joined_ref[where, cut:] = (hidden * share).astype(BF16)
             if keep:
@@ -757,7 +774,7 @@
 
 def backward_kernel(
     inner, final_part, tokens_hbm, rows_ref, qkv_ref, up_ref, low_ref, slope_ref, mixed_ref,
-    facts_ref, cosine, sine, doc_col, doc_row,
+    facts_ref, lengths_ref, cosine, sine,
     grad_ref, branch_all, mixed_grad, hidden_grad, rows_out, bias_out,
     near_in, far_in, far_out, low, quarter, tokens_ref, own_tokens, joined_ref, key_ref, value_ref,
     part_ref,
@@ -879,6 +896,9 @@
         serve()
         if position:
             sums.across(steps[position - 1])
+        lengths = lengths_ref[part]
+        doc_col = documents(lengths, lax.broadcasted_iota(jnp.int32, (block, 1), 0))
+        doc_row = documents(lengths, lax.broadcasted_iota(jnp.int32, (1, block), 1))
         for head in range(heads):
             at = head * 3 * HD
             key_ref[...] = jnp.zeros_like(key_ref)
@@ -890,7 +910,7 @@
                 query = mixed_ref[queries, at : at + HD]
                 key = mixed_ref[keys, at + HD : at + 2 * HD]
                 scores = dot_cols(query, key) * HD ** (-0.5)
-                same = doc_col[queries, :] == doc_row[part][:, :width]
+                same = doc_col[first : first + 128] == doc_row[:, :width]
                 earlier = first + lax.broadcasted_iota(
                     jnp.int32, scores.shape, 0
                 ) >= lax.broadcasted_iota(jnp.int32, scores.shape, 1)
@@ -903,20 +923,21 @@
                 mean = jnp.sum(probs * prob_grad, axis=1, keepdims=True)
                 score_grad = (probs * (prob_grad - mean)).astype(BF16)
                 mixed_grad[queries, at : at + HD] = turn(
-                    dot(score_grad, key) * HD ** (-0.5), tables, queries, -1.0
+                    dot(score_grad, key) * HD ** (-0.5), tables, pl.ds(first, 128), -1.0
                 ).astype(BF16)
                 key_ref[:width, :] += dot_rows(score_grad, query)
                 value_ref[:width, :] += dot_rows(probs.astype(BF16), attended_grad)
             mixed_grad[whole, at + HD : at + 2 * HD] = turn(
-                key_ref[...] * HD ** (-0.5), tables, whole, -1.0
+                key_ref[...] * HD ** (-0.5), tables, pl.ds(0, block), -1.0
             ).astype(BF16)
             mixed_grad[whole, at + 2 * HD : at + 3 * HD] = value_ref[...].astype(BF16)
-        bias_out[0:1, : mixed_grad.shape[1]] += jnp.sum(
-            f32(mixed_grad[whole, :]), axis=0, keepdims=True
-        )
-        bias_out[0:1, mixed_grad.shape[1] :] += jnp.sum(
-            f32(hidden_grad[whole, :]), axis=0, keepdims=True
-        )
+        row = 0
+        for ref in (mixed_grad, hidden_grad):
+            for n in range(0, ref.shape[1], 128):
+                bias_out[row : row + 1, :] += jnp.sum(
+                    f32(ref[whole, n : n + 128]), axis=0, keepdims=True
+                )
+                row += 1
         serve()
         if position > 1:
             sums.along(steps[position - 2])
@@ -960,6 +981,7 @@
     block, width = part.shape
     quarter = block // QUARTERS
     slope, mixed, facts, joined = kept
+    bias_rows = -(-(mixed.shape[1] + slope.shape[1]) // 1024) * 8
     dma = pltpu.SemaphoreType.DMA
     return pl.pallas_call(
         functools.partial(backward_kernel, inner),
@@ -968,10 +990,10 @@
             jax.ShapeDtypeStruct((SPLIT * block, width), BF16),
             jax.ShapeDtypeStruct(mixed.shape, BF16),
             jax.ShapeDtypeStruct(slope.shape, BF16),
-            jax.ShapeDtypeStruct(rows.shape, F32),
-            jax.ShapeDtypeStruct((1, mixed.shape[1] + slope.shape[1]), F32),
+            jax.ShapeDtypeStruct((8, rows.shape[1]), F32),
+            jax.ShapeDtypeStruct((bias_rows, 128), F32),
         ],
-        in_specs=[VMEM_SPEC, ANY_SPEC] + [VMEM_SPEC] * 11,
+        in_specs=[VMEM_SPEC, ANY_SPEC] + [VMEM_SPEC] * (7 + len(layout)),
         out_specs=[VMEM_SPEC] * 6,
         scratch_shapes=[
             pltpu.VMEM((2, quarter, width), BF16),
@@ -1288,7 +1310,7 @@
 
 
 def reward_kernel(
-    inner, stats_ref, member_ref, label_ref, out_ref, stats, outer_in, inner_in,
+    inner, stats_ref, facts_ref, out_ref, stats, outer_in, inner_in,
     send, recv, send_o, recv_o, send_i, recv_i,
 ):
     here = Place(inner)
@@ -1313,7 +1335,15 @@
     totals = highest + jnp.log(summed)
     picks = functools.reduce(lambda a, b: a + b, quarters)
     log_probs = picks - totals_to_picks(totals)
-    member = member_ref[...]
+    doc = lax.broadcasted_iota(jnp.int32, (8, 1), 0)
+    start = end = labels = jnp.zeros((8, 1), jnp.int32)
+    for segment in range(SEGS):
+        length = facts_ref[0:1, segment : segment + 1]
+        start = start + jnp.where(doc > segment, length, 0)
+        end = end + jnp.where(doc >= segment, length, 0)
+        labels = labels + jnp.where(doc == segment, facts_ref[1:2, segment : segment + 1], 0)
+    token = lax.broadcasted_iota(jnp.int32, (8, stats_ref.shape[1]), 1)
+    member = jnp.where((token >= start) & (token < end), 1.0, 0.0)
     policy_docs = jnp.sum(member * log_probs[1:2, :], axis=1, keepdims=True)
     frozen_docs = jnp.sum(member * log_probs[3:4, :], axis=1, keepdims=True)
     reward = policy_docs - frozen_docs
@@ -1329,7 +1359,7 @@
     seq_count = inner * SPLIT * SEGS
     shift = total[:, 0:1] / seq_count
     sigmoid_value = 1.0 / (1.0 + jnp.exp(-BETA_KTO * (reward - shift)))
-    labels = label_ref[:, 0:1]
+    labels = f32(labels)
     doc_grad = BETA_KTO * sigmoid_value * (1.0 - sigmoid_value) * (1.0 - 2.0 * labels) / seq_count
     token_grad = jnp.sum(member * doc_grad, axis=0, keepdims=True)
     out_ref[...] = jnp.transpose(
@@ -1343,14 +1373,14 @@
     return jnp.concatenate([totals[0:1], totals[0:1], totals[2:3], totals[2:3], totals[4:]], axis=0)
 
 
-def reward_call(stats, member, labels, inner, number):
+def reward_call(stats, facts, inner, number):
     dma = pltpu.SemaphoreType.DMA
     tile = (8, 128)
     peers = max(inner - 1, 1)
     return pl.pallas_call(
         functools.partial(reward_kernel, inner),
         out_shape=jax.ShapeDtypeStruct((stats.shape[1], 8), F32),
-        in_specs=[VMEM_SPEC] * 3,
+        in_specs=[VMEM_SPEC] * 2,
         out_specs=VMEM_SPEC,
         scratch_shapes=[
             pltpu.VMEM((QUARTERS, *stats.shape), F32),
@@ -1364,34 +1394,19 @@
             dma((peers,)),
         ],
         compiler_params=pltpu.CompilerParams(collective_id=number, has_side_effects=True),
-    )(stats, member, labels)
-
-
-def turn_tables(positions):
+    )(stats, facts)
+
+
+def turn_tables(count):
     half = ROT // 2
-    frequency = 10000.0 ** (-2.0 * jnp.arange(half, dtype=F32) / ROT)
-    angles = positions.reshape(-1).astype(F32)[:, None] * frequency
-    cosine, sine = jnp.cos(angles), jnp.sin(angles)
-    none = jnp.zeros((angles.shape[0], HD - ROT), F32)
+    frequency = np.float32(10000.0) ** (np.float32(-2.0) * np.arange(half, dtype=np.float32) / ROT)
+    angles = np.arange(count, dtype=np.float32)[:, None] * frequency.astype(np.float32)
+    cosine, sine = np.cos(angles), np.sin(angles)
+    none = np.zeros((count, HD - ROT), np.float32)
     return (
-        jnp.concatenate([cosine, cosine, none + 1.0], axis=1),
-        jnp.concatenate([-sine, sine, none], axis=1),
+        jnp.asarray(np.concatenate([cosine, cosine, none + 1.0], axis=1), F32),
+        jnp.asarray(np.concatenate([-sine, sine, none], axis=1), F32),
     )
-
-
-def doc_layout(lengths_row, row_count):
-    ends, run = [], 0
-    for segment in range(lengths_row.shape[0]):
-        run = run + lengths_row[segment]
-        ends.append(run)
-    doc_ends = jnp.stack(ends)
-    starts = doc_ends - lengths_row
-    index_rows = jnp.arange(row_count, dtype=jnp.int32)
-    member = (index_rows[:, None] >= starts[None, :]) & (index_rows[:, None] < doc_ends[None, :])
-    doc_ids = jnp.arange(lengths_row.shape[0], dtype=jnp.int32)
-    doc_of = jnp.sum(jnp.where(member, doc_ids[None, :], 0), axis=1)
-    positions = index_rows - jnp.sum(jnp.where(member, starts[None, :], 0), axis=1)
-    return (member, positions, doc_of)
 
 
 def chunk_of(width):
@@ -1553,10 +1568,6 @@
         mean_hat / (jnp.sqrt(square_hat) + ADAM_EPS) + decay_rate * master
     )
     return (mean_new, square_new, master_new)
-
-
-def eight_rows(rows):
-    return jnp.zeros((8, rows.shape[1]), F32).at[: rows.shape[0]].set(rows)
 
 
 def on_device(
@@ -1595,29 +1606,17 @@
     inner = dp_size // SPLIT
     outer_index = lax.axis_index("dp") // inner
     block = inputs.shape[0]
-    lengths_tile = jnp.zeros((8, 128), jnp.int32).at[0, :SEGS].set(doc_lengths[0])
+    small = jnp.concatenate([doc_lengths, desirable], axis=0).astype(jnp.int32)
+    lengths_tile = jnp.pad(small, ((0, 8 - small.shape[0]), (0, 128 - SEGS)))
     masters = tuple(w.astype(BF16) for w in (qkv_master, out_master, up_master, down_master))
     *policy_set, tokens_all, lengths_all = spread_weights(masters, inner, inputs, lengths_tile, 0)
     frozen_shards = (qkv_frozen, out_frozen, up_frozen, down_frozen)
-    member, _, _ = doc_layout(doc_lengths[0], block)
-    _, positions, doc_of = jax.vmap(lambda row: doc_layout(row, block))(lengths_all[:, 0, :SEGS])
-
     cut = qkv_master.shape[1]
     width_qkv, width_up = cut // SPLIT, up_master.shape[1] // SPLIT
 
-    def own_bias(bias):
-        return (
-            lax.dynamic_slice(bias, (outer_index * width_qkv,), (width_qkv,))[None],
-            lax.dynamic_slice(bias, (cut + outer_index * width_up,), (width_up,))[None],
-        )
-
-    layout = (
-        *turn_tables(positions),
-        doc_of.reshape(-1, 1),
-        doc_of[:, None, :],
-    )
-    policy = (eight_rows(vectors), *own_bias(hidden_bias))
-    frozen = (eight_rows(vectors_frozen), *own_bias(hidden_frozen))
+    layout = (lengths_all, *turn_tables(block))
+    policy = (vectors, hidden_bias[None])
+    frozen = (vectors_frozen, hidden_frozen[None])
     if aligned(out_master.shape[1]):
         final_low, frozen_low, *kept = forward_call(
             tokens_all, layout, (policy, frozen), policy_set, block, inner, None, frozen_shards, 2
@@ -1635,25 +1634,18 @@
     vocab_start = lax.axis_index("tensor") * head_weight.shape[1]
     own_targets = (targets - vocab_start)[:, None]
     logits, stats = head_call(final_low, frozen_low, head_weight, own_targets)
-    doc_rows = jnp.zeros((8, block), F32).at[:SEGS].set(f32(member).T)
-    labels = jnp.zeros((8, 128), F32).at[:SEGS].set(f32(desirable[0])[:, None])
-    token_rows = reward_call(stats, doc_rows, labels, inner, 6)
+    token_rows = reward_call(stats, lengths_tile, inner, 6)
     final_part = logit_grad_call(logits, head_weight, own_targets, token_rows)
-    input_grad, branch_low, mixed_grad, hidden_low, vector_part, bias_part = backward_call(
-        final_part, tokens_all, eight_rows(vectors), policy_set, kept_values, layout, inner, 4
+    input_grad, branch_low, mixed_grad, hidden_low, vector_part, bias_tile = backward_call(
+        final_part, tokens_all, vectors, policy_set, kept_values, layout, inner, 4
     )
     shards = tuple(w.shape for w in masters)
     bias_rows = (width_qkv + width_up) // 128
-    bias_tile = (
-        jnp.zeros((-(-bias_rows // 8) * 8, 128), F32)
-        .at[:bias_rows]
-        .set(bias_part.reshape(bias_rows, 128))
-    )
+    input_grad = f32(input_grad)
     qkv_grad, up_grad, out_grad, down_grad, vector_sum, bias_sum, square = finish_call(
-        tokens_all, branch_low, eight_rows(vectors), kept_values[2:], (mixed_grad, hidden_low),
+        tokens_all, branch_low, vectors, kept_values[2:], (mixed_grad, hidden_low),
         vector_part, bias_tile, shards, inner, 5,
     )
-    input_grad = f32(input_grad)
     vector_grad = jnp.concatenate([vector_sum[:5], vector_sum[4:5]], axis=0)
     bias_sum = bias_sum[:, :bias_rows].reshape(SPLIT, bias_rows * 128)
     hidden_grad = jnp.concatenate(

time: 739 us -> 723 us (0.978)
  local copies, waits for them, and re-layouts: 17.3 us -> 8.6 us
  other arithmetic: 34 us -> 25.8 us
where the time goes in v6:
time: 723 us; the launch traced here: 714 us
  Pallas kernels  676 us (93%)
  other arithmetic  25.8 us (4%)
  local copies, waits for them, and re-layouts  8.6 us (1%)
    pallas_call x1, Pallas kernels, forward_call(): pl.pallas_call(functools.partial(forward_kernel, inner, keeps, background...  196 us
    pallas_call x1, Pallas kernels, backward_call(): pl.pallas_call(functools.partial(backward_kernel, inner), out_shape=[jax....  163 us
    pallas_call x1, Pallas kernels, spread_weights(): pl.pallas_call(functools.partial(spread_weights_kernel, inner), out_shape...  134 us
    pallas_call x1, Pallas kernels, finish_call(): pl.pallas_call(functools.partial(finish_kernel, inner), out_shape=[*(jax....  102 us
    pallas_call x1, Pallas kernels, head_call(): pl.pallas_call(head_kernel, grid=(width // columns,), out_shape=[jax.Shap...  38.3 us
    pallas_call x1, Pallas kernels, logit_grad_call(): pl.pallas_call(logit_grad_kernel, grid=(width // columns,), out_shape=jax...  22.8 us
    pallas_call x1, Pallas kernels, reward_call(): pl.pallas_call(functools.partial(reward_kernel, inner), out_shape=jax.Sha...  19.9 us
    sub x6, other arithmetic, adam_step(): master - rate * (mean_hat / (jnp.sqrt(square_hat) + ADAM_EPS) + decay_rat...  17 us

profile of v6, /device:TPU:0, one launch (start us, length us, event | category | flops | bytes accessed | tf_op | source)
XLA Modules:
  0.0 713.7 jit_solution(13634991281214408657)
XLA Ops:
  0.7 0.8 pad_add_fusion
  2.1 2.7 convert_element_type.29.up
  4.8 1.1 convert_element_type.30.down
  5.9 0.7 copy-done.2
  6.6 1.0 convert_element_type.27.qkv
  7.6 0.7 convert_element_type.28.out
  8.3 134.5 %shard_map.454 = (bf16[2048,384]{1,0:T(8,128)(2,1)}, bf16[2048,512]{1,0:T(8,128)(2,1)}, bf16[640,2048]{1,0:T(8,128)(2,1)}, bf16[2048,2048]{1,0:T(8,128)(2,1)}, s32[4,8,128]{2,1,0:T(8,128)}) custom-call(bf16[256,1536]{1,0:T(8,128)(2,1)} %convert_element_type.27.qkv, bf16[512,256]{1,0:T(8,128)(2,1)} %convert_element_type.28.out, ...), custom_call_target="tpu_custom_call" | custom-call | tf_op jit(solution)/shard_map/pallas_call | solution.py:301
  144.0 196.1 %shard_map.455 = (bf16[512,2048]{1,0:T(8,128)(2,1)}, bf16[512,2048]{1,0:T(8,128)(2,1)}, f32[2048,512]{1,0:T(8,128)}, bf16[2048,384]{1,0:T(8,128)(2,1)}, f32[2048...) custom-call(bf16[2048,2048]{1,0:T(8,128)(2,1)} %get-tuple-element.47, ...), custom_call_target="tpu_custom_call" | custom-call | tf_op jit(solution)/shard_map/pallas_call | solution.py:730
  340.1 0.9 copy.52.target_ref
  340.9 38.3 %shard_map.456 = (f32[512,6400]{1,0:T(8,128)}, f32[8,512]{1,0:T(8,128)}) custom-call(bf16[512,2048]{1,0:T(8,128)(2,1)} %get-tuple-element.112.policy_ref, bf16[512,2048]{1,0:T(8,128)(2,1)} %get-tuple-element.53.frozen_ref, bf16[2048,6400]{1,0:T(8,128)(2,1)} %head_ref.3, s32[512,1]{1,0:T(8,128)} %copy.52.target_ref), custom_call_target="tpu_custom_call" | custom-call | flops 26843545600 | bytes 39321600 | tf_op jit(solution)/shard_map/pallas_call | solution.py:1478
  379.3 19.9 %shard_map.457.token_ref = f32[512,8]{1,0:T(8,128)} custom-call(f32[8,512]{1,0:T(8,128)} %get-tuple-element.55.stats_ref, s32[8,128]{1,0:T(8,128)} %pad.4.lengths.facts_ref), custom_call_target="tpu_custom_call" | custom-call | tf_op jit(solution)/shard_map/pallas_call | solution.py:1380
  399.2 22.8 %shard_map.458.final_part = bf16[512,2048]{1,0:T(8,128)(2,1)} custom-call(f32[512,6400]{1,0:T(8,128)} %get-tuple-element.54.logits_ref, bf16[2048,6400]{1,0:T(8,128)(2,1)} %head_ref.3, s32[512,1]{1,0:T(8,128)} %copy.52.target_ref, f32[512,8]{1,0:T(8,128)} %shard_map.457.token_ref), custom_call_target="tpu_custom_call" | custom-call | flops 13421772800 | bytes 39321600 | tf_op jit(solution)/shard_map/pallas_call | solution.py:1540
  422.0 162.8 %shard_map.459 = (bf16[512,2048]{1,0:T(8,128)(2,1)}, bf16[2048,2048]{1,0:T(8,128)(2,1)}, bf16[2048,384]{1,0:T(8,128)(2,1)}, bf16[2048,512]{1,0:T(8,128)(2,1)}, f32[8,2048]{1,0:T(8,128)}, /*index=5*/f32[8,128]{1,0:T(8,128)}) custom-call(bf16[512,2048]{1,0:T(8,128)(2,1)} %shard_map.458.final_part, ...), custom_call_target="tpu_custom_call" | custom-call | tf_op jit(solution)/shard_map/pallas_call | solution.py:986
  584.8 101.8 %shard_map.460 = (bf16[256,1536]{1,0:T(8,128)(2,1)}, bf16[256,2048]{1,0:T(8,128)(2,1)}, bf16[512,256]{1,0:T(8,128)(2,1)}, bf16[2048,256]{1,0:T(8,128)(2,1)}, f32...) custom-call(bf16[2048,2048]{1,0:T(8,128)(2,1)} %get-tuple-element.47.refs_0_.tokens_hbm.tokens_ref, ...), custom_call_target="tpu_custom_call" | custom-call | tf_op jit(solution)/shard_map/pallas_call | solution.py:1277
  686.6 0.7 slice_bitcast_fusion
  687.4 1.2 slice.18
  690.0 0.8 slice.20
  690.8 1.6 multiply_subtract_fusion.4
  692.4 6.5 multiply_subtract_fusion
  698.9 3.9 multiply_subtract_fusion.1
  702.9 1.4 multiply_subtract_fusion.3
  705.3 3.0 multiply_subtract_fusion.2
  708.3 2.5 convert_element_type.31
  710.9 1.3 copy.59
  (57 shorter events, 3.6 us)
Async XLA Ops:
  0.7 4.2 copy-start
  4.8 1.8 copy-start.2
  4.8 2.7 copy-start.6
  8.3 134.5 %copy-start.22 = (f32[3584]{0:T(1024)S(1)}, f32[3584]{0:T(1024)}, u32[]{:S(2)}) copy-start(f32[3584]{0:T(1024)} %param.59) | copy-start | bytes 43012
  8.3 135.1 %copy-start.17 = (f32[3584]{0:T(1024)S(1)}, f32[3584]{0:T(1024)}, u32[]{:S(2)}) copy-start(f32[3584]{0:T(1024)} %param.41) | copy-start | bytes 43012
  144.0 196.1 %copy-start.23 = (s32[512]{0:T(512)S(1)}, s32[512]{0:T(512)}, u32[]{:S(2)}) copy-start(s32[512]{0:T(512)} %param.32) | copy-start | bytes 6148
  584.8 104.5 %copy-start.20 = (f32[3584]{0:T(1024)S(1)}, f32[3584]{0:T(1024)}, u32[]{:S(2)}) copy-start(f32[3584]{0:T(1024)} %param.53) | copy-start | bytes 43012
  584.8 104.5 %copy-start.21 = (f32[3584]{0:T(1024)S(1)}, f32[3584]{0:T(1024)}, u32[]{:S(2)}) copy-start(f32[3584]{0:T(1024)} %param.47) | copy-start | bytes 43012
  584.8 106.0 %copy-start.11 = (f32[6,2048]{1,0:T(8,128)S(1)}, f32[6,2048]{1,0:T(8,128)}, u32[]{:S(2)}) copy-start(f32[6,2048]{1,0:T(8,128)} %gains_ref.1) | copy-start | bytes 147460
  584.8 106.0 %copy-start.18 = (f32[6,2048]{1,0:T(8,128)S(1)}, f32[6,2048]{1,0:T(8,128)}, u32[]{:S(2)}) copy-start(f32[6,2048]{1,0:T(8,128)} %param.52) | copy-start | bytes 147460
  584.8 106.0 %copy-start.19 = (f32[6,2048]{1,0:T(8,128)S(1)}, f32[6,2048]{1,0:T(8,128)}, u32[]{:S(2)}) copy-start(f32[6,2048]{1,0:T(8,128)} %param.46) | copy-start | bytes 147460
  692.4 6.5 copy-start.1
  692.4 6.5 copy-start.7
  692.4 6.5 copy-start.8
  692.4 6.5 copy-start.12
  698.9 4.0 copy-start.14
  698.9 3.9 copy-start.15
  698.9 3.9 copy-start.16
  698.9 5.4 copy-start.10
  698.9 5.3 copy-start.13
  702.8 2.0 copy-start.3
  702.8 2.4 copy-start.9
  705.3 3.0 copy-start.4
  708.3 2.5 copy-start.5

commit v7 on v6

--- a/solution.py
+++ b/solution.py
@@ -51,6 +51,13 @@
 
     def inner_peer(self, shift):
         return (self.o * self.inner + (self.i + shift) % self.inner, self.t)
+
+    def tensor_peers(self):
+        return [(self.dp, (self.t + s) % QUARTERS) for s in range(1, QUARTERS)]
+
+    def dp_peers(self):
+        count = SPLIT * self.inner
+        return [((self.dp + s) % count, self.t) for s in range(1, count)]
 
     def near_peer(self):
         return (self.dp, self.near)
@@ -1085,6 +1092,48 @@
         return value
 
 
+class ShortSum:
+    def __init__(self, here, quarters, parts, send, recv, send_dp, recv_dp):
+        self.here, self.quarters, self.parts = here, quarters, parts
+        self.sems, self.dp_sems = (send, recv), (send_dp, recv_dp)
+        self.copies = []
+
+    def share(self, buffer, index, sems, peers):
+        waiting = [
+            remote(buffer.at[index], buffer.at[index], sems[0].at[n], sems[1].at[n], peer)
+            for n, peer in enumerate(peers)
+        ]
+        self.copies += waiting
+        for copy in waiting:
+            copy.wait_recv()
+        return functools.reduce(lambda a, b: a + b, [buffer[n] for n in range(buffer.shape[0])])
+
+    def along_tensor(self, value):
+        self.quarters[self.here.t] = value
+        return self.share(self.quarters, self.here.t, self.sems, self.here.tensor_peers())
+
+    def along_dp(self, value):
+        self.parts[self.here.dp] = value
+        return self.share(self.parts, self.here.dp, self.dp_sems, self.here.dp_peers())
+
+    def finish(self):
+        for copy in self.copies:
+            copy.wait_send()
+
+
+def short_sum_scratch(inner):
+    dma = pltpu.SemaphoreType.DMA
+    count = SPLIT * inner
+    return [
+        pltpu.VMEM((QUARTERS, 8, 128), F32),
+        pltpu.VMEM((count, 8, 128), F32),
+        dma((QUARTERS - 1,)),
+        dma((QUARTERS - 1,)),
+        dma((count - 1,)),
+        dma((count - 1,)),
+    ]
+
+
 def all_sum_scratch(shape, inner):
     dma = pltpu.SemaphoreType.DMA
     return [
@@ -1110,8 +1159,8 @@
     sends, inputs, totals = scratch[:3], scratch[3:6], scratch[6:9]
     turned, send_i, recv_i, send_o, recv_o, local, held = scratch[9:16]
     small = AllSum(here, *scratch[16:23])
-    squares = AllSum(here, *scratch[23:30])
-    bias_in, bias_send, bias_recv = scratch[30:33]
+    squares = ShortSum(here, *scratch[23:29])
+    bias_in, bias_send, bias_recv = scratch[29:32]
     outs = (qkv_out, up_out, out_out, down_out)
     shard = qkv_out.shape[0]
     width_out = out_out.shape[0] // SPLIT
@@ -1144,7 +1193,7 @@
         width = outs[m].shape[0] // SPLIT
         return outs[m].at[pl.ds(here.o * width, width), :]
 
-    greet(reduce_peers(here) + [here.inner_peer(r) for r in range(1, inner)])
+    greet(here.tensor_peers() + here.dp_peers())
     first, last, own = {}, [], []
     order = [(kind, s) for kind in (2, 1, 0) for s in (2, 1, 3, 0)]
     turned[...] = jnp.transpose(joined_ref[...])
@@ -1238,11 +1287,8 @@
     rows_out[...] = small.value()
     for number in range(9, len(order)):
         square = square + settle(number)
-    squares.near(jnp.broadcast_to(square, norm_ref.shape))
-    squares.far()
-    squares.along_outer()
-    squares.along_inner()
-    norm = squares.value()
+    norm = squares.along_dp(squares.along_tensor(jnp.broadcast_to(square, norm_ref.shape)))
+    squares.finish()
     rows = rows_out[...]
     doubled = lax.broadcasted_iota(jnp.int32, rows.shape, 0) == 4
     norm_ref[...] = norm + whole_sum(rows * rows * jnp.where(doubled, 2.0, 1.0))
@@ -1297,7 +1343,7 @@
             pltpu.VMEM((16, 128) if aligned(shard) else (tokens.shape[0], shard), BF16),
         ]
         + all_sum_scratch(sums.shape, inner)
-        + all_sum_scratch(tile, inner)
+        + short_sum_scratch(inner)
         + [
             pltpu.VMEM((inner, *bias.shape), F32),
             dma((SPLIT + inner,)),
@@ -1310,14 +1356,11 @@
 
 
 def reward_kernel(
-    inner, stats_ref, facts_ref, out_ref, stats, outer_in, inner_in,
-    send, recv, send_o, recv_o, send_i, recv_i,
+    inner, stats_ref, facts_ref, out_ref, stats, send, recv, *scratch,
 ):
     here = Place(inner)
-    tensor_peers = [(here.dp, (here.t + s) % QUARTERS) for s in range(1, QUARTERS)]
-    outer_peers = [here.outer_peer(s) for s in range(1, SPLIT)]
-    inner_peers = [here.inner_peer(r) for r in range(1, inner)]
-    greet(tensor_peers + outer_peers + inner_peers)
+    sums = ShortSum(here, *scratch)
+    greet(here.tensor_peers() + here.dp_peers())
 
     def share(buffer, index, sends, recvs, peers):
         return [
@@ -1326,7 +1369,7 @@
         ]
 
     stats[here.t] = stats_ref[...]
-    copies = share(stats, here.t, send, recv, tensor_peers)
+    copies = share(stats, here.t, send, recv, here.tensor_peers())
     for copy in copies:
         copy.wait_recv()
     quarters = [stats[q] for q in range(QUARTERS)]
@@ -1347,15 +1390,7 @@
     policy_docs = jnp.sum(member * log_probs[1:2, :], axis=1, keepdims=True)
     frozen_docs = jnp.sum(member * log_probs[3:4, :], axis=1, keepdims=True)
     reward = policy_docs - frozen_docs
-    outer_in[here.o] = jnp.broadcast_to(whole_sum(reward), outer_in.shape[1:])
-    more = share(outer_in, here.o, send_o, recv_o, outer_peers)
-    for copy in more:
-        copy.wait_recv()
-    inner_in[here.i] = functools.reduce(lambda a, b: a + b, [outer_in[n] for n in range(SPLIT)])
-    rest = share(inner_in, here.i, send_i, recv_i, inner_peers)
-    for copy in rest:
-        copy.wait_recv()
-    total = functools.reduce(lambda a, b: a + b, [inner_in[n] for n in range(inner)])
+    total = sums.along_dp(jnp.broadcast_to(whole_sum(reward), (8, 128)))
     seq_count = inner * SPLIT * SEGS
     shift = total[:, 0:1] / seq_count
     sigmoid_value = 1.0 / (1.0 + jnp.exp(-BETA_KTO * (reward - shift)))
@@ -1365,8 +1400,9 @@
     out_ref[...] = jnp.transpose(
         jnp.concatenate([token_grad, totals[0:1, :], jnp.zeros((6, totals.shape[1]), F32)], axis=0)
     )
-    for copy in copies + more + rest:
+    for copy in copies:
         copy.wait_send()
+    sums.finish()
 
 
 def totals_to_picks(totals):
@@ -1375,8 +1411,6 @@
 
 def reward_call(stats, facts, inner, number):
     dma = pltpu.SemaphoreType.DMA
-    tile = (8, 128)
-    peers = max(inner - 1, 1)
     return pl.pallas_call(
         functools.partial(reward_kernel, inner),
         out_shape=jax.ShapeDtypeStruct((stats.shape[1], 8), F32),
@@ -1384,14 +1418,9 @@
         out_specs=VMEM_SPEC,
         scratch_shapes=[
             pltpu.VMEM((QUARTERS, *stats.shape), F32),
-            pltpu.VMEM((SPLIT, *tile), F32),
-            pltpu.VMEM((inner, *tile), F32),
             dma((QUARTERS - 1,)),
             dma((QUARTERS - 1,)),
-            dma((SPLIT - 1,)),
-            dma((SPLIT - 1,)),
-            dma((peers,)),
-            dma((peers,)),
+            *short_sum_scratch(inner),
         ],
         compiler_params=pltpu.CompilerParams(collective_id=number, has_side_effects=True),
     )(stats, facts)

time: 723 us -> 721 us (level)
  no operation moved by 1% of the time
where the time goes in v7:
time: 721 us; the launch traced here: 711 us
  Pallas kernels  674 us (93%)
  other arithmetic  25.8 us (4%)
  local copies, waits for them, and re-layouts  8.6 us (1%)
    pallas_call x1, Pallas kernels, forward_call(): pl.pallas_call(functools.partial(forward_kernel, inner, keeps, background...  196 us
    pallas_call x1, Pallas kernels, backward_call(): pl.pallas_call(functools.partial(backward_kernel, inner), out_shape=[jax....  165 us
    pallas_call x1, Pallas kernels, spread_weights(): pl.pallas_call(functools.partial(spread_weights_kernel, inner), out_shape...  134 us
    pallas_call x1, Pallas kernels, finish_call(): pl.pallas_call(functools.partial(finish_kernel, inner), out_shape=[*(jax....  99.5 us
    pallas_call x1, Pallas kernels, head_call(): pl.pallas_call(head_kernel, grid=(width // columns,), out_shape=[jax.Shap...  38.3 us
    pallas_call x1, Pallas kernels, logit_grad_call(): pl.pallas_call(logit_grad_kernel, grid=(width // columns,), out_shape=jax...  22.8 us
    pallas_call x1, Pallas kernels, reward_call(): pl.pallas_call(functools.partial(reward_kernel, inner), out_shape=jax.Sha...  18 us
    sub x6, other arithmetic, adam_step(): master - rate * (mean_hat / (jnp.sqrt(square_hat) + ADAM_EPS) + decay_rat...  17 us

profile of v7, /device:TPU:0, one launch (start us, length us, event | category | flops | bytes accessed | tf_op | source)
XLA Modules:
  0.0 711.3 jit_solution(7070197354721266091)
XLA Ops:
  0.7 0.8 pad_add_fusion
  2.1 2.7 convert_element_type.29.up
  4.8 1.1 convert_element_type.30.down
  5.9 0.7 copy-done.2
  6.6 1.0 convert_element_type.27.qkv
  7.6 0.7 convert_element_type.28.out
  8.3 134.5 %shard_map.454 = (bf16[2048,384]{1,0:T(8,128)(2,1)}, bf16[2048,512]{1,0:T(8,128)(2,1)}, bf16[640,2048]{1,0:T(8,128)(2,1)}, bf16[2048,2048]{1,0:T(8,128)(2,1)}, s32[4,8,128]{2,1,0:T(8,128)}) custom-call(bf16[256,1536]{1,0:T(8,128)(2,1)} %convert_element_type.27.qkv, bf16[512,256]{1,0:T(8,128)(2,1)} %convert_element_type.28.out, ...), custom_call_target="tpu_custom_call" | custom-call | tf_op jit(solution)/shard_map/pallas_call | solution.py:308
  144.0 196.1 %shard_map.455 = (bf16[512,2048]{1,0:T(8,128)(2,1)}, bf16[512,2048]{1,0:T(8,128)(2,1)}, f32[2048,512]{1,0:T(8,128)}, bf16[2048,384]{1,0:T(8,128)(2,1)}, f32[2048...) custom-call(bf16[2048,2048]{1,0:T(8,128)(2,1)} %get-tuple-element.47, ...), custom_call_target="tpu_custom_call" | custom-call | tf_op jit(solution)/shard_map/pallas_call | solution.py:737
  340.1 0.9 copy.52.target_ref
  340.9 38.3 %shard_map.456 = (f32[512,6400]{1,0:T(8,128)}, f32[8,512]{1,0:T(8,128)}) custom-call(bf16[512,2048]{1,0:T(8,128)(2,1)} %get-tuple-element.112.policy_ref, bf16[512,2048]{1,0:T(8,128)(2,1)} %get-tuple-element.53.frozen_ref, bf16[2048,6400]{1,0:T(8,128)(2,1)} %head_ref.3, s32[512,1]{1,0:T(8,128)} %copy.52.target_ref), custom_call_target="tpu_custom_call" | custom-call | flops 26843545600 | bytes 39321600 | tf_op jit(solution)/shard_map/pallas_call | solution.py:1507
  379.3 18.0 %shard_map.457.token_ref = f32[512,8]{1,0:T(8,128)} custom-call(f32[8,512]{1,0:T(8,128)} %get-tuple-element.55.stats_ref, s32[8,128]{1,0:T(8,128)} %pad.4.lengths.facts_ref), custom_call_target="tpu_custom_call" | custom-call | tf_op jit(solution)/shard_map/pallas_call | solution.py:1414
  397.2 22.8 %shard_map.458.final_part = bf16[512,2048]{1,0:T(8,128)(2,1)} custom-call(f32[512,6400]{1,0:T(8,128)} %get-tuple-element.54.logits_ref, bf16[2048,6400]{1,0:T(8,128)(2,1)} %head_ref.3, s32[512,1]{1,0:T(8,128)} %copy.52.target_ref, f32[512,8]{1,0:T(8,128)} %shard_map.457.token_ref), custom_call_target="tpu_custom_call" | custom-call | flops 13421772800 | bytes 39321600 | tf_op jit(solution)/shard_map/pallas_call | solution.py:1569
  420.1 164.6 %shard_map.459 = (bf16[512,2048]{1,0:T(8,128)(2,1)}, bf16[2048,2048]{1,0:T(8,128)(2,1)}, bf16[2048,384]{1,0:T(8,128)(2,1)}, bf16[2048,512]{1,0:T(8,128)(2,1)}, f32[8,2048]{1,0:T(8,128)}, /*index=5*/f32[8,128]{1,0:T(8,128)}) custom-call(bf16[512,2048]{1,0:T(8,128)(2,1)} %shard_map.458.final_part, ...), custom_call_target="tpu_custom_call" | custom-call | tf_op jit(solution)/shard_map/pallas_call | solution.py:993
  584.7 99.5 %shard_map.460 = (bf16[256,1536]{1,0:T(8,128)(2,1)}, bf16[256,2048]{1,0:T(8,128)(2,1)}, bf16[512,256]{1,0:T(8,128)(2,1)}, bf16[2048,256]{1,0:T(8,128)(2,1)}, f32...) custom-call(bf16[2048,2048]{1,0:T(8,128)(2,1)} %get-tuple-element.47.refs_0_.tokens_hbm.tokens_ref, ...), custom_call_target="tpu_custom_call" | custom-call | tf_op jit(solution)/shard_map/pallas_call | solution.py:1323
  684.2 0.7 slice_bitcast_fusion
  685.0 1.2 slice.18
  687.6 0.8 slice.20
  688.4 1.6 multiply_subtract_fusion.4
  690.0 6.5 multiply_subtract_fusion
  696.5 3.9 multiply_subtract_fusion.1
  700.4 1.4 multiply_subtract_fusion.3
  702.9 3.0 multiply_subtract_fusion.2
  705.9 2.5 convert_element_type.31
  708.5 1.3 copy.59
  (57 shorter events, 3.6 us)
Async XLA Ops:
  0.7 4.2 copy-start
  4.8 1.8 copy-start.2
  4.8 2.7 copy-start.6
  8.3 134.5 %copy-start.22 = (f32[3584]{0:T(1024)S(1)}, f32[3584]{0:T(1024)}, u32[]{:S(2)}) copy-start(f32[3584]{0:T(1024)} %param.59) | copy-start | bytes 43012
  8.3 135.1 %copy-start.17 = (f32[3584]{0:T(1024)S(1)}, f32[3584]{0:T(1024)}, u32[]{:S(2)}) copy-start(f32[3584]{0:T(1024)} %param.41) | copy-start | bytes 43012
  144.0 196.1 %copy-start.23 = (s32[512]{0:T(512)S(1)}, s32[512]{0:T(512)}, u32[]{:S(2)}) copy-start(s32[512]{0:T(512)} %param.32) | copy-start | bytes 6148
  584.7 102.2 %copy-start.20 = (f32[3584]{0:T(1024)S(1)}, f32[3584]{0:T(1024)}, u32[]{:S(2)}) copy-start(f32[3584]{0:T(1024)} %param.53) | copy-start | bytes 43012
  584.7 102.2 %copy-start.21 = (f32[3584]{0:T(1024)S(1)}, f32[3584]{0:T(1024)}, u32[]{:S(2)}) copy-start(f32[3584]{0:T(1024)} %param.47) | copy-start | bytes 43012
  584.7 103.7 %copy-start.11 = (f32[6,2048]{1,0:T(8,128)S(1)}, f32[6,2048]{1,0:T(8,128)}, u32[]{:S(2)}) copy-start(f32[6,2048]{1,0:T(8,128)} %gains_ref.1) | copy-start | bytes 147460
  584.7 103.7 %copy-start.18 = (f32[6,2048]{1,0:T(8,128)S(1)}, f32[6,2048]{1,0:T(8,128)}, u32[]{:S(2)}) copy-start(f32[6,2048]{1,0:T(8,128)} %param.52) | copy-start | bytes 147460
  584.7 103.7 %copy-start.19 = (f32[6,2048]{1,0:T(8,128)S(1)}, f32[6,2048]{1,0:T(8,128)}, u32[]{:S(2)}) copy-start(f32[6,2048]{1,0:T(8,128)} %param.46) | copy-start | bytes 147460
  690.0 6.5 copy-start.1
  690.0 6.5 copy-start.7
  690.0 6.5 copy-start.8
  690.0 6.5 copy-start.12
  696.5 4.0 copy-start.14
  696.5 3.9 copy-start.15
  696.5 3.9 copy-start.16
  696.5 5.4 copy-start.10
  696.5 5.3 copy-start.13
  700.4 2.0 copy-start.3
  700.4 2.4 copy-start.9
  702.9 3.0 copy-start.4
  705.9 2.5 copy-start.5
